TPU v7x, 256 devices: a whole 4x4x8 slice. The times are simulated.
256 devices in a mesh: gx: 16 (over z, core), gy: 16 (over y, x).
Axes of the slice: x: 4, y: 4, z: 8, core: 2. Of those that a mesh axis runs over, the one named last changes fastest.
Arguments:
- latent_noise: float32 [1024, 65536], P('gx', 'gy'), may hold values from -6 to 6
- kappa_sq: float32 [1024, 1024], P('gx', 'gy'), may hold values from 0.25 to 4
- obs_cell: int32 [65536], P(('gx', 'gy')), may hold values from 0 to 4095
- obs_value: float32 [65536], P(('gx', 'gy')), may hold values from -6 to 6
- obs_var: float32 [65536], P(('gx', 'gy')), may hold values from 0.1 to 1
Outputs:
- latent_new: float32 [1024, 65536], P('gx', 'gy')
- prior_field: float32 [1024, 65536], P('gx', 'gy')
Inputs may be any that keep to these rules, and one draw needn't show every extreme that they name: obs_cell[j] is a cell of the block held by device j // 256 in the order of gx+gy (gx slowest), written as row * 64 + column within that block.
All inputs are finite; a program needn't handle non-finite values.
Results may differ from a plain program's by a relative error of at most 0.0001.
Values sent between devices are 32-bit elements; how exact they have to be, the bound alone decides.
No kernel may reach another device: no remote copies, remote signals or barrier semaphores. Data moves between devices by JAX's collectives and lax.ppermute only.
A program may use at most 64 MiB of HBM per device.

v0:
```python
import jax
import jax.numpy as jnp
import numpy as np
from jax import lax
from jax.sharding import PartitionSpec as P

MEMBERS = 64
SWEEPS = 4


LOWER_EDGE = 0.25
UPPER_EDGE = 12.0


def padded(block, sides, width):
    for axis, dim in sides:
        count = lax.axis_size(axis)
        forward = [(i, i + 1) for i in range(count - 1)]
        backward = [(target, source) for source, target in forward]
        low = lax.ppermute(
            lax.slice_in_dim(block, block.shape[dim] - width, None, axis=dim), axis, forward
        )
        high = lax.ppermute(lax.slice_in_dim(block, 0, width, axis=dim), axis, backward)
        block = jnp.concatenate([low, block, high], axis=dim)
    return block


def cheb_coeffs(terms):
    angles = np.pi * (np.arange(64) + 0.5) / 64.0
    nodes = 0.5 * (UPPER_EDGE + LOWER_EDGE) + 0.5 * (UPPER_EDGE - LOWER_EDGE) * np.cos(angles)
    values = []
    for order in range(terms):
        coeff = 2.0 / 64.0 * np.sum(np.cos(order * angles) / nodes)
        if order == 0:
            coeff = 0.5 * coeff
        values.append(float(coeff))
    return values


def chol_solve(factor, rhs):
    lower_sol = lax.linalg.triangular_solve(factor, rhs, left_side=True, lower=True)
    return lax.linalg.triangular_solve(
        factor, lower_sol, left_side=True, lower=True, transpose_a=True
    )


def stencil(field, along_x, along_y, diagonal):
    beside = along_x[2:] + along_x[:-2] + along_y[:, 2 * MEMBERS :] + along_y[:, : -2 * MEMBERS]
    applied = diagonal * field - beside
    return (2.0 * applied - (UPPER_EDGE + LOWER_EDGE) * field) / (UPPER_EDGE - LOWER_EDGE)


def chebyshev(start, scaled, coeffs):
    earlier = start
    current = scaled(start)
    total = coeffs[0] * start + coeffs[1] * current
    for order in range(2, len(coeffs)):
        following = 2.0 * scaled(current) - earlier
        total = total + coeffs[order] * following
        earlier, current = (current, following)
    return total


def per_device(latent_noise, kappa_sq, obs_cell, obs_value, obs_var):
    rows_x, width = latent_noise.shape
    cells_y = width // MEMBERS
    coeffs = cheb_coeffs(SWEEPS + 1)
    diagonal = jnp.repeat(kappa_sq + 4.0, MEMBERS, axis=1)

    def scaled(field):
        along_x = padded(field, (("gx", 0),), 1)
        along_y = padded(field, (("gy", 1),), MEMBERS)
        return stencil(field, along_x, along_y, diagonal)

    prior_field = chebyshev(latent_noise, scaled, coeffs)
    field_cells = prior_field.reshape(rows_x * cells_y, MEMBERS)
    predicted = jnp.take(field_cells, obs_cell, axis=0)
    weight = 1.0 / obs_var
    misfits = obs_value[:, None] - predicted
    own_misfit = jnp.sum(misfits * misfits * weight[:, None])
    spread = predicted - jnp.mean(predicted, axis=1, keepdims=True)
    scale_down = float(MEMBERS * (MEMBERS - 1))
    misfit_total = lax.psum(own_misfit, ("gx", "gy"))
    inflation = 1.0 + misfit_total / scale_down
    scaled_spread = spread * (weight / inflation)[:, None]
    own_gram = jnp.dot(
        scaled_spread.T, spread, precision=lax.Precision.HIGHEST, preferred_element_type=jnp.float32
    )
    own_cross = jnp.dot(
        scaled_spread.T,
        misfits,
        precision=lax.Precision.HIGHEST,
        preferred_element_type=jnp.float32,
    )
    gram, cross = lax.psum((own_gram, own_cross), ("gx", "gy"))
    system = (MEMBERS - 1) * jnp.eye(MEMBERS, dtype=jnp.float32) + gram
    factor = jnp.linalg.cholesky(system)
    gain = chol_solve(factor, cross)
    latent_cells = latent_noise.reshape(rows_x * cells_y, MEMBERS)
    deviation = latent_cells - jnp.mean(latent_cells, axis=1, keepdims=True)
    update = jnp.dot(
        deviation, gain, precision=lax.Precision.HIGHEST, preferred_element_type=jnp.float32
    )
    latent_new = (latent_cells + update).reshape(rows_x, width)
    return (latent_new, prior_field)


def solution(mesh):
    placed = (P("gx", "gy"), P("gx", "gy"), P(("gx", "gy")), P(("gx", "gy")), P(("gx", "gy")))
    return jax.shard_map(
        per_device,
        mesh=mesh,
        in_specs=placed,
        out_specs=(P("gx", "gy"), P("gx", "gy")),
        check_vma=False,
    )
```

profile of v0, /device:TPU:2, one launch (start us, length us, event | category | flops | bytes accessed | tf_op | source)
XLA Modules:
  0.0 264.7 jit_solution(12779640378611144372)
XLA Ops:
  1.5 4.2 %collective-permute-start.2 = (f32[64,64]{1,0:T(8,128)S(1)}, f32[64,64]{1,0:T(8,128)S(1)}, u32[]{:S(2)}, u32[]{:S(2)}) collective-permute-start(f32[64,64]{1,0:T(8,128)S(1)} %get-tuple-element.20), channel_id=1, source_target_pairs={{1,0},{2,1},{3,2},{4,3},{5,4},{6,5},{7,6},{8,7},{9,8},{10,9},{11,1... | collective-permute-start | bytes 49160 | tf_op jit(solution)/shard_map/ppermute | solution.py:23
  5.7 1.9 collective-permute-start.3
  8.6 1.3 collective-permute-start
  9.9 3.0 %collective-permute-start.1 = (f32[1,4096]{1,0:T(1,128)S(1)}, f32[1,4096]{1,0:T(1,128)S(1)}, u32[]{:S(2)}, u32[]{:S(2)}) collective-permute-start(f32[1,4096]{1,0:T(1,128)S(1)} %get-tuple-element.19), channel_id=1, source_target_pairs={{0,16},{16,32},{32,48},{48,64},{64,80},{80,96},{96,112},{112,128},... | collective-permute-start | bytes 49160 | tf_op jit(solution)/shard_map/ppermute | solution.py:20
  13.0 2.0 reshape.43
  15.6 1.9 broadcast_in_dim.23
  17.6 3.0 %reshape.44 = f32[64,4096]{1,0:T(8,128)} reshape(f32[64,64,64]{2,1,0:T(8,128)} %broadcast_in_dim.23) | data formatting | bytes 2097152 | tf_op jit(solution)/shard_map/reshape | solution.py:68
  20.6 1.9 broadcast_multiply_fusion
  22.6 3.9 %collective-permute-start.6 = (f32[64,64]{1,0:T(8,128)S(1)}, f32[64,64]{1,0:T(8,128)S(1)}, u32[]{:S(2)}, u32[]{:S(2)}) collective-permute-start(f32[64,64]{1,0:T(8,128)S(1)} %get-tuple-element.16), channel_id=1, source_target_pairs={{1,0},{2,1},{3,2},{4,3},{5,4},{6,5},{7,6},{8,7},{9,8},{10,9},{11,1... | collective-permute-start | bytes 49160 | tf_op jit(solution)/shard_map/ppermute | solution.py:23
  26.6 1.9 collective-permute-start.7
  28.5 1.3 collective-permute-start.4
  29.8 3.3 %collective-permute-start.5 = (f32[1,4096]{1,0:T(1,128)S(1)}, f32[1,4096]{1,0:T(1,128)S(1)}, u32[]{:S(2)}, u32[]{:S(2)}) collective-permute-start(f32[1,4096]{1,0:T(1,128)S(1)} %get-tuple-element.15), channel_id=1, source_target_pairs={{0,16},{16,32},{32,48},{48,64},{64,80},{80,96},{96,112},{112,128},... | collective-permute-start | bytes 49160 | tf_op jit(solution)/shard_map/ppermute | solution.py:20
  33.9 2.0 fusion.24
  36.0 3.7 %collective-permute-start.10 = (f32[64,64]{1,0:T(8,128)S(1)}, f32[64,64]{1,0:T(8,128)S(1)}, u32[]{:S(2)}, u32[]{:S(2)}) collective-permute-start(f32[64,64]{1,0:T(8,128)S(1)} %get-tuple-element.12), channel_id=1, source_target_pairs={{1,0},{2,1},{3,2},{4,3},{5,4},{6,5},{7,6},{8,7},{9,8},{10,9},{11,1... | collective-permute-start | bytes 49160 | tf_op jit(solution)/shard_map/ppermute | solution.py:23
  39.7 3.2 %collective-permute-start.11 = (f32[64,64]{1,0:T(8,128)S(1)}, f32[64,64]{1,0:T(8,128)S(1)}, u32[]{:S(2)}, u32[]{:S(2)}) collective-permute-start(f32[64,64]{1,0:T(8,128)S(1)} %get-tuple-element.13), channel_id=1, source_target_pairs={{0,1},{1,2},{2,3},{3,4},{4,5},{5,6},{6,7},{7,8},{8,9},{9,10},{10,1... | collective-permute-start | bytes 49160 | tf_op jit(solution)/shard_map/ppermute | solution.py:20
  42.9 1.3 collective-permute-start.8
  44.2 4.0 %collective-permute-start.9 = (f32[1,4096]{1,0:T(1,128)S(1)}, f32[1,4096]{1,0:T(1,128)S(1)}, u32[]{:S(2)}, u32[]{:S(2)}) collective-permute-start(f32[1,4096]{1,0:T(1,128)S(1)} %get-tuple-element.11), channel_id=1, source_target_pairs={{0,16},{16,32},{32,48},{48,64},{64,80},{80,96},{96,112},{112,128},... | collective-permute-start | bytes 49160 | tf_op jit(solution)/shard_map/ppermute | solution.py:20
  49.0 2.0 fusion.16
  52.1 1.9 collective-permute-start.14
  54.0 5.8 %collective-permute-start.15 = (f32[64,64]{1,0:T(8,128)S(1)}, f32[64,64]{1,0:T(8,128)S(1)}, u32[]{:S(2)}, u32[]{:S(2)}) collective-permute-start(f32[64,64]{1,0:T(8,128)S(1)} %get-tuple-element.9), channel_id=1, source_target_pairs={{0,1},{1,2},{2,3},{3,4},{4,5},{5,6},{6,7},{7,8},{8,9},{9,10},{10,1... | collective-permute-start | bytes 49160 | tf_op jit(solution)/shard_map/ppermute | solution.py:20
  61.1 4.9 %collective-permute-start.13 = (f32[1,4096]{1,0:T(1,128)S(1)}, f32[1,4096]{1,0:T(1,128)S(1)}, u32[]{:S(2)}, u32[]{:S(2)}) collective-permute-start(f32[1,4096]{1,0:T(1,128)S(1)} %get-tuple-element.7), channel_id=1, source_target_pairs={{0,16},{16,32},{32,48},{48,64},{64,80},{80,96},{96,112},{112,128},... | collective-permute-start | bytes 49160 | tf_op jit(solution)/shard_map/ppermute | solution.py:20
  65.9 1.6 copy.9
  67.5 5.6 %fusion.8 = f32[64,4096]{1,0:T(8,128)} fusion(f32[64,4096]{1,0:T(8,128)} %copy-done.2, f32[64,4096]{1,0:T(8,128)} %copy-done.3, f32[64,64]{1,0:T(8,128)S(1)} %collective-permute-done.15, f32[64,64]{1,0:T(8,128)S(1)} %collective-permute-done.14, f32[1,4096]{1,0:T(1,128)S(1)} %collective-permute-done.13, f32[1,4096]{1,0:T(1,128)S(1)} %collective-permute-done.12, ...), kind=kLoop, calls=%fused_computation.11 | loop fusion | flops 9175040 | bytes 5373952 | tf_op jit(solution)/shard_map/add | solution.py:59
  73.2 3.2 %reshape.45 = f32[4096,64]{1,0:T(8,128)} reshape(f32[64,4096]{1,0:T(8,128)} %fusion.8) | data formatting | bytes 2097152 | tf_op jit(solution)/shard_map/reshape | solution.py:76
  76.4 2.3 gather_fusion
  79.5 89.6 %psum.21 = f32[]{:T(128)} all-reduce(f32[]{:T(128)} %get-tuple-element.3), channel_id=1, replica_groups=mesh['gx'=16,'gy'=16] {'gx','gy'}, use_global_device_ids=true, to_apply=%region_3.4 | all-reduce | flops 1 | bytes 8 | tf_op jit(solution)/shard_map/psum | solution.py:83
  170.9 74.0 %all-reduce = (f32[64,64]{1,0:T(8,128)S(1)}, f32[64,64]{1,0:T(8,128)S(1)}) all-reduce(f32[64,64]{1,0:T(8,128)S(1)} %fusion.34, f32[64,64]{1,0:T(8,128)S(1)} %fusion.36), channel_id=1, replica_groups=mesh['gx'=16,'gy'=16] {'gx','gy'}, use_global_device_ids=true, to_apply=%region_7.8 | all-reduce | flops 8192 | bytes 65536 | tf_op jit(solution)/shard_map/psum | solution.py:95
  245.0 5.8 %cholesky.16 = f32[64,64]{1,0:T(8,128)S(1)} custom-call(f32[64,64]{1,0:T(8,128)S(1)} %fusion.57), custom_call_target="Cholesky" | custom-call | tf_op jit(solution)/shard_map/jit(cholesky)/cholesky | solution.py:97
  252.2 4.9 %custom-call.8 = f32[1,64,64]{1,2,0:T(8,128)S(1)} custom-call(f32[1,64,64]{2,1,0:T(8,128)S(1)} %fusion.52), custom_call_target="InvertDiagBlocksLowerTriangular" | custom-call | tf_op jit(solution)/shard_map/triangular_solve | solution.py:42
  257.6 3.7 %convolution_add_fusion = f32[4096,64]{0,1:T(8,128)} fusion(f32[4096,64]{0,1:T(8,128)S(1)} %copy-done.4, f32[64,64]{1,0:T(8,128)S(1)} %fusion.53, f32[4096,64]{1,0:T(8,128)S(1)} %reshape.43, f32[4096]{0:T(1024)S(1)} %broadcast_multiply_fusion.1), kind=kOutput, calls=%fused_computation.1 | convolution fusion | flops 201850880 | bytes 3178496 | tf_op jit(solution)/shard_map/dot_general | solution.py:101
  261.3 1.8 copy.10
  263.1 1.6 reshape.46
  (63 shorter events, 10.5 us)
Async XLA Ops:
  0.6 14.3 %copy-start.5 = (f32[64,64]{1,0:T(8,128)S(1)}, f32[64,64]{1,0:T(8,128)}, u32[]{:S(2)}) copy-start(f32[64,64]{1,0:T(8,128)} %param.6) | copy-start | bytes 49156
  1.5 19.1 %collective-permute-start.2 = (f32[64,64]{1,0:T(8,128)S(1)}, f32[64,64]{1,0:T(8,128)S(1)}, u32[]{:S(2)}, u32[]{:S(2)}) collective-permute-start(f32[64,64]{1,0:T(8,128)S(1)} %get-tuple-element.20), channel_id=1, source_target_pairs={{1,0},{2,1},{3,2},{4,3},{5,4},{6,5},{7,6},{8,7},{9,8},{10,9},{11,1... | collective-permute-start | bytes 49160 | tf_op jit(solution)/shard_map/ppermute | solution.py:23
  5.7 14.9 %collective-permute-start.3 = (f32[64,64]{1,0:T(8,128)S(1)}, f32[64,64]{1,0:T(8,128)S(1)}, u32[]{:S(2)}, u32[]{:S(2)}) collective-permute-start(f32[64,64]{1,0:T(8,128)S(1)} %get-tuple-element.21), channel_id=1, source_target_pairs={{0,1},{1,2},{2,3},{3,4},{4,5},{5,6},{6,7},{7,8},{8,9},{9,10},{10,1... | collective-permute-start | bytes 49160 | tf_op jit(solution)/shard_map/ppermute | solution.py:20
  8.6 12.0 %collective-permute-start = (f32[1,4096]{1,0:T(1,128)S(1)}, f32[1,4096]{1,0:T(1,128)S(1)}, u32[]{:S(2)}, u32[]{:S(2)}) collective-permute-start(f32[1,4096]{1,0:T(1,128)S(1)} %get-tuple-element.18), channel_id=1, source_target_pairs={{16,0},{32,16},{48,32},{64,48},{80,64},{96,80},{112,96},{128,112},... | collective-permute-start | bytes 49160 | tf_op jit(solution)/shard_map/ppermute | solution.py:23
  9.9 5.7 %copy-start.8 = (s32[256]{0:T(256)S(1)}, s32[256]{0:T(256)}, u32[]{:S(2)}) copy-start(s32[256]{0:T(256)} %param.7) | copy-start | bytes 3076
  9.9 10.7 %collective-permute-start.1 = (f32[1,4096]{1,0:T(1,128)S(1)}, f32[1,4096]{1,0:T(1,128)S(1)}, u32[]{:S(2)}, u32[]{:S(2)}) collective-permute-start(f32[1,4096]{1,0:T(1,128)S(1)} %get-tuple-element.19), channel_id=1, source_target_pairs={{0,16},{16,32},{32,48},{48,64},{64,80},{80,96},{96,112},{112,128},... | collective-permute-start | bytes 49160 | tf_op jit(solution)/shard_map/ppermute | solution.py:20
  17.6 3.0 %copy-start = (f32[64,4096]{1,0:T(8,128)S(1)}, f32[64,4096]{1,0:T(8,128)}, u32[]{:S(2)}) copy-start(f32[64,4096]{1,0:T(8,128)} %param.5) | copy-start | bytes 3145732
  20.5 12.5 %copy-start.6 = (f32[256]{0:T(256)S(1)}, f32[256]{0:T(256)}, u32[]{:S(2)}) copy-start(f32[256]{0:T(256)} %param.9) | copy-start | bytes 3076
  20.6 13.3 %copy-start.1 = (f32[64,4096]{1,0:T(8,128)S(1)}, f32[64,4096]{1,0:T(8,128)}, u32[]{:S(2)}) copy-start(f32[64,4096]{1,0:T(8,128)} %reshape.44) | copy-start | bytes 3145732
  22.6 10.4 %collective-permute-start.6 = (f32[64,64]{1,0:T(8,128)S(1)}, f32[64,64]{1,0:T(8,128)S(1)}, u32[]{:S(2)}, u32[]{:S(2)}) collective-permute-start(f32[64,64]{1,0:T(8,128)S(1)} %get-tuple-element.16), channel_id=1, source_target_pairs={{1,0},{2,1},{3,2},{4,3},{5,4},{6,5},{7,6},{8,7},{9,8},{10,9},{11,1... | collective-permute-start | bytes 49160 | tf_op jit(solution)/shard_map/ppermute | solution.py:23
  26.6 6.5 %collective-permute-start.7 = (f32[64,64]{1,0:T(8,128)S(1)}, f32[64,64]{1,0:T(8,128)S(1)}, u32[]{:S(2)}, u32[]{:S(2)}) collective-permute-start(f32[64,64]{1,0:T(8,128)S(1)} %get-tuple-element.17), channel_id=1, source_target_pairs={{0,1},{1,2},{2,3},{3,4},{4,5},{5,6},{6,7},{7,8},{8,9},{9,10},{10,1... | collective-permute-start | bytes 49160 | tf_op jit(solution)/shard_map/ppermute | solution.py:20
  28.5 4.6 %collective-permute-start.4 = (f32[1,4096]{1,0:T(1,128)S(1)}, f32[1,4096]{1,0:T(1,128)S(1)}, u32[]{:S(2)}, u32[]{:S(2)}) collective-permute-start(f32[1,4096]{1,0:T(1,128)S(1)} %get-tuple-element.14), channel_id=1, source_target_pairs={{16,0},{32,16},{48,32},{64,48},{80,64},{96,80},{112,96},{128,112},... | collective-permute-start | bytes 49160 | tf_op jit(solution)/shard_map/ppermute | solution.py:23
  29.8 4.1 %collective-permute-start.5 = (f32[1,4096]{1,0:T(1,128)S(1)}, f32[1,4096]{1,0:T(1,128)S(1)}, u32[]{:S(2)}, u32[]{:S(2)}) collective-permute-start(f32[1,4096]{1,0:T(1,128)S(1)} %get-tuple-element.15), channel_id=1, source_target_pairs={{0,16},{16,32},{32,48},{48,64},{64,80},{80,96},{96,112},{112,128},... | collective-permute-start | bytes 49160 | tf_op jit(solution)/shard_map/ppermute | solution.py:20
  35.9 15.2 %copy-start.2 = (f32[64,4096]{1,0:T(8,128)}, f32[64,4096]{1,0:T(8,128)S(1)}, u32[]{:S(2)}) copy-start(f32[64,4096]{1,0:T(8,128)S(1)} %fusion.24) | copy-start | bytes 3145732
  36.0 12.3 %collective-permute-start.10 = (f32[64,64]{1,0:T(8,128)S(1)}, f32[64,64]{1,0:T(8,128)S(1)}, u32[]{:S(2)}, u32[]{:S(2)}) collective-permute-start(f32[64,64]{1,0:T(8,128)S(1)} %get-tuple-element.12), channel_id=1, source_target_pairs={{1,0},{2,1},{3,2},{4,3},{5,4},{6,5},{7,6},{8,7},{9,8},{10,9},{11,1... | collective-permute-start | bytes 49160 | tf_op jit(solution)/shard_map/ppermute | solution.py:23
  39.7 8.6 %collective-permute-start.11 = (f32[64,64]{1,0:T(8,128)S(1)}, f32[64,64]{1,0:T(8,128)S(1)}, u32[]{:S(2)}, u32[]{:S(2)}) collective-permute-start(f32[64,64]{1,0:T(8,128)S(1)} %get-tuple-element.13), channel_id=1, source_target_pairs={{0,1},{1,2},{2,3},{3,4},{4,5},{5,6},{6,7},{7,8},{8,9},{9,10},{10,1... | collective-permute-start | bytes 49160 | tf_op jit(solution)/shard_map/ppermute | solution.py:20
  42.9 5.4 %collective-permute-start.8 = (f32[1,4096]{1,0:T(1,128)S(1)}, f32[1,4096]{1,0:T(1,128)S(1)}, u32[]{:S(2)}, u32[]{:S(2)}) collective-permute-start(f32[1,4096]{1,0:T(1,128)S(1)} %get-tuple-element.10), channel_id=1, source_target_pairs={{16,0},{32,16},{48,32},{64,48},{80,64},{96,80},{112,96},{128,112},... | collective-permute-start | bytes 49160 | tf_op jit(solution)/shard_map/ppermute | solution.py:23
  44.2 4.8 %collective-permute-start.9 = (f32[1,4096]{1,0:T(1,128)S(1)}, f32[1,4096]{1,0:T(1,128)S(1)}, u32[]{:S(2)}, u32[]{:S(2)}) collective-permute-start(f32[1,4096]{1,0:T(1,128)S(1)} %get-tuple-element.11), channel_id=1, source_target_pairs={{0,16},{16,32},{32,48},{48,64},{64,80},{80,96},{96,112},{112,128},... | collective-permute-start | bytes 49160 | tf_op jit(solution)/shard_map/ppermute | solution.py:20
  51.0 1.0 copy-start.3
  52.1 15.4 %collective-permute-start.14 = (f32[64,64]{1,0:T(8,128)S(1)}, f32[64,64]{1,0:T(8,128)S(1)}, u32[]{:S(2)}, u32[]{:S(2)}) collective-permute-start(f32[64,64]{1,0:T(8,128)S(1)} %get-tuple-element.8), channel_id=1, source_target_pairs={{1,0},{2,1},{3,2},{4,3},{5,4},{6,5},{7,6},{8,7},{9,8},{10,9},{11,1... | collective-permute-start | bytes 49160 | tf_op jit(solution)/shard_map/ppermute | solution.py:23
  54.0 13.5 %collective-permute-start.15 = (f32[64,64]{1,0:T(8,128)S(1)}, f32[64,64]{1,0:T(8,128)S(1)}, u32[]{:S(2)}, u32[]{:S(2)}) collective-permute-start(f32[64,64]{1,0:T(8,128)S(1)} %get-tuple-element.9), channel_id=1, source_target_pairs={{0,1},{1,2},{2,3},{3,4},{4,5},{5,6},{6,7},{7,8},{8,9},{9,10},{10,1... | collective-permute-start | bytes 49160 | tf_op jit(solution)/shard_map/ppermute | solution.py:20
  59.8 7.7 %collective-permute-start.12 = (f32[1,4096]{1,0:T(1,128)S(1)}, f32[1,4096]{1,0:T(1,128)S(1)}, u32[]{:S(2)}, u32[]{:S(2)}) collective-permute-start(f32[1,4096]{1,0:T(1,128)S(1)} %get-tuple-element.6), channel_id=1, source_target_pairs={{16,0},{32,16},{48,32},{64,48},{80,64},{96,80},{112,96},{128,112},... | collective-permute-start | bytes 49160 | tf_op jit(solution)/shard_map/ppermute | solution.py:23
  61.1 6.5 %collective-permute-start.13 = (f32[1,4096]{1,0:T(1,128)S(1)}, f32[1,4096]{1,0:T(1,128)S(1)}, u32[]{:S(2)}, u32[]{:S(2)}) collective-permute-start(f32[1,4096]{1,0:T(1,128)S(1)} %get-tuple-element.7), channel_id=1, source_target_pairs={{0,16},{16,32},{32,48},{48,64},{64,80},{80,96},{96,112},{112,128},... | collective-permute-start | bytes 49160 | tf_op jit(solution)/shard_map/ppermute | solution.py:20
  73.2 5.5 %copy-start.7 = (f32[256]{0:T(256)S(1)}, f32[256]{0:T(256)}, u32[]{:S(2)}) copy-start(f32[256]{0:T(256)} %param.8) | copy-start | bytes 3076
  73.2 184.4 %copy-start.4 = (f32[4096,64]{0,1:T(8,128)S(1)}, f32[4096,64]{0,1:T(8,128)}, u32[]{:S(2)}) copy-start(f32[4096,64]{0,1:T(8,128)} %copy.9) | copy-start | bytes 3145732
where the time goes:
time: 267 us; the launch traced here: 265 us
  blocking collectives  164 us (61%)
  starting transfers between devices  46.8 us (18%)
  other arithmetic  25.1 us (9%)
  local copies, waits for them, and re-layouts  20.6 us (8%)
  matrix products  5.31 us (2%)
    psum x1, blocking collectives, per_device(): misfit_total = lax.psum(own_misfit, ('gx', 'gy'))  89.6 us
    psum x1, blocking collectives, per_device(): gram, cross = lax.psum((own_gram, own_cross), ('gx', 'gy'))  74 us
    ppermute x8, starting transfers between devices, padded(): lax.ppermute(lax.slice_in_dim(block, block.shape[dim] - width, None, axis...  28 us
    ppermute x8, starting transfers between devices, padded(): lax.ppermute(lax.slice_in_dim(block, 0, width, axis=dim), axis, backward)  18.9 us
    another operation x3, other arithmetic, per_device(): factor = jnp.linalg.cholesky(system)  6.55 us
    add x1, other arithmetic, chebyshev(): total = total + coeffs[order] * following  5.64 us
    another operation x2, other arithmetic, chol_solve(): lax.linalg.triangular_solve(factor, lower_sol, left_side=True, lower=True...  5.53 us
  transfers between devices with their start and end apart: 16, of which 2 were waited for; matrix products, arithmetic and copies ran while one was open for 4% of the time, Pallas kernels for 0%

commit v1 on v0

v1 whole, which is shorter than its diff:
```python
import jax
import jax.numpy as jnp
import numpy as np
from jax import lax
from jax.experimental import pallas as pl
from jax.experimental.pallas import tpu as pltpu
from jax.sharding import PartitionSpec as P

MEMBERS = 64
SWEEPS = 4
LOWER_EDGE = 0.25
UPPER_EDGE = 12.0
HALO = SWEEPS
CX = 64
CY = 64
OBS = 256
EXT_ROWS = CX + 16
EXT_LANES = (CY + 2 * HALO) * MEMBERS
BLOCKS = EXT_LANES // 128
LEFT = HALO * MEMBERS
WIDTH = CY * MEMBERS
STAT_ROWS = 40
VMEM = pltpu.MemorySpace.VMEM
SMEM = pltpu.MemorySpace.SMEM


def power_coeffs():
    angles = np.pi * (np.arange(64) + 0.5) / 64.0
    centre, half = 0.5 * (UPPER_EDGE + LOWER_EDGE), 0.5 * (UPPER_EDGE - LOWER_EDGE)
    nodes = centre + half * np.cos(angles)
    cheb = [2.0 / 64.0 * np.sum(np.cos(k * angles) / nodes) for k in range(SWEEPS + 1)]
    cheb[0] *= 0.5
    mono = np.polynomial.chebyshev.cheb2poly(cheb)
    return [float(v / half**k) for k, v in enumerate(mono)]


def split3(a):
    hi = a.astype(jnp.bfloat16)
    lo = (a - hi.astype(jnp.float32)).astype(jnp.bfloat16)
    return hi, lo


def field_kernel(flags, cell, lat, kap, xlo, xhi, ylo, yhi, val, var, prior, stat, ext, alp, ua, ub, tall, kext, pbuf):
    fx0, fx1, fy0, fy1 = flags[0], flags[1], flags[2], flags[3]
    right = LEFT + WIDTH
    zero4 = jnp.zeros((4, EXT_LANES), jnp.float32)
    ext[0:4, :] = zero4
    ext[EXT_ROWS - 4 : EXT_ROWS, :] = zero4
    ext[8 : 8 + CX, LEFT:right] = lat[...]
    ext[4:8, LEFT:right] = xlo[:, 0:WIDTH] * fx0
    ext[8 + CX : 12 + CX, LEFT:right] = xhi[:, 0:WIDTH] * fx1
    for ref, flag, at in ((ylo, fy0, 0), (yhi, fy1, right)):
        ext[8 : 8 + CX, at : at + LEFT] = ref[0:CX, 0:LEFT] * flag
        ext[4:8, at : at + LEFT] = ref[CX : CX + 4, 0:LEFT] * (flag * fx0)
        ext[8 + CX : 12 + CX, at : at + LEFT] = ref[CX + 4 : CX + 8, 0:LEFT] * (flag * fx1)
    kext[...] = jnp.zeros((EXT_ROWS, 128), jnp.float32)
    kext[8 : 8 + CX, HALO : HALO + CY] = kap[...]
    kext[4:8, HALO : HALO + CY] = xlo[:, WIDTH : WIDTH + CY]
    kext[8 + CX : 12 + CX, HALO : HALO + CY] = xhi[:, WIDTH : WIDTH + CY]
    for ref, at in ((ylo, 0), (yhi, HALO + CY)):
        kext[8 : 8 + CX, at : at + HALO] = ref[0:CX, LEFT : LEFT + HALO]
        kext[4:8, at : at + HALO] = ref[CX : CX + 4, LEFT : LEFT + HALO]
        kext[8 + CX : 12 + CX, at : at + HALO] = ref[CX + 4 : CX + 8, LEFT : LEFT + HALO]
    shifted = kext[...] - (0.5 * (UPPER_EDGE + LOWER_EDGE) - 4.0)
    lane = lax.broadcasted_iota(jnp.int32, (EXT_ROWS, 128), 1)
    upper = lane // MEMBERS
    low_half = upper == 0
    for c in range(BLOCKS):
        alp[:, c * 128 : (c + 1) * 128] = jnp.take_along_axis(shifted, upper + 2 * c, axis=1)

    coeffs = power_coeffs()

    def block(ref, c):
        c = min(max(c, 0), BLOCKS - 1)
        return ref[:, c * 128 : (c + 1) * 128]

    def sweep(src, first, last, coeff, scale, store):
        turned = [None] * (BLOCKS + 2)

        def turn(c):
            return pltpu.roll(block(src, c), 64, 1)

        before, here = turn(first - 1), turn(first)
        for c in range(first, last + 1):
            after = turn(c + 1)
            v = block(src, c)
            beside = here + jnp.where(low_half, before, after)
            beside = beside + pltpu.roll(v, 1, 0) + pltpu.roll(v, EXT_ROWS - 1, 0)
            applied = block(alp, c) * v - beside
            if scale != 1.0:
                applied = applied * scale
            store(c, coeff * block(ext, c) + applied)
            before, here = here, after

    def keep(dst):
        def store(c, new):
            flag = fy0 if c < LEFT // 128 else fy1 if c >= right // 128 else None
            if flag is not None:
                new = new * flag
            at = slice(c * 128, (c + 1) * 128)
            dst[0:8, at] = new[0:8] * fx0
            dst[8 : 8 + CX, at] = new[8 : 8 + CX]
            dst[8 + CX : EXT_ROWS, at] = new[8 + CX : EXT_ROWS] * fx1

        return store

    def finish(c, new):
        prior[:, c * 128 - LEFT : (c + 1) * 128 - LEFT] = new[8 : 8 + CX]
        at = (c - LEFT // 128) * CX
        tall[at : at + CX, :] = new[8 : 8 + CX]

    sweep(ext, 0, BLOCKS - 1, coeffs[3], coeffs[4], keep(ua))
    sweep(ua, 1, BLOCKS - 2, coeffs[2], 1.0, keep(ub))
    sweep(ub, 1, BLOCKS - 2, coeffs[1], 1.0, keep(ua))
    sweep(ua, 2, BLOCKS - 3, coeffs[0], 1.0, finish)

    for j in range(OBS):
        at = cell[j]
        pair = lax.bitwise_and(at, CY - 2) * (CX // 2)
        pbuf[j : j + 1, :] = tall[pl.ds(pair + lax.shift_right_logical(at, 6), 1), :]

    def column(row):
        pieces = [jnp.transpose(jnp.broadcast_to(row[i : i + 1, :], (128, 128))) for i in range(OBS // 128)]
        return jnp.concatenate(pieces, axis=0)

    value = column(val[0:2, :])
    weight = 1.0 / column(var[0:2, :])
    odd = column(val[2:4, :]) > 0.5
    both = pbuf[...]
    plane = lax.broadcasted_iota(jnp.int32, (OBS, 128), 1)
    member = plane < MEMBERS
    predicted = jnp.where(odd, pltpu.roll(both, 64, 1), both)
    predicted = jnp.where(member, predicted, 0.0)
    mean = jnp.sum(predicted, axis=1, keepdims=True) * (1.0 / MEMBERS)
    spread = jnp.where(member, predicted - mean, jnp.where(plane == MEMBERS, value - mean, 0.0))
    full = lax.dot_general(
        spread * weight,
        spread,
        (((0,), (0,)), ((), ())),
        precision=lax.Precision.HIGHEST,
        preferred_element_type=jnp.float32,
    )
    half = MEMBERS // 2
    tile = lax.broadcasted_iota(jnp.int32, (half, 128), 1)
    stat[0:half, :] = jnp.where(tile < MEMBERS, full[0:half], pltpu.roll(full[half:MEMBERS], 64, 1))
    stat[half:STAT_ROWS, :] = full[MEMBERS : MEMBERS + 8]


def update_kernel(parts, lat, out):
    total = parts[0]
    for i in range(1, parts.shape[0]):
        total = total + parts[i]
    half = MEMBERS // 2
    packed = total[0:half]
    gram = jnp.concatenate([packed, pltpu.roll(packed, 64, 1)], axis=0)
    last = total[half : half + 1]
    shape = (MEMBERS, 128)
    row = lax.broadcasted_iota(jnp.int32, shape, 0)
    lane = lax.broadcasted_iota(jnp.int32, shape, 1)
    eye = row == lane
    low = lane < MEMBERS
    square = jnp.sum(jnp.where(lane[0:1] == MEMBERS, last, 0.0), axis=1, keepdims=True)
    trace = jnp.sum(jnp.sum(jnp.where(eye, gram, 0.0), axis=0, keepdims=True), axis=1, keepdims=True)
    inflation = 1.0 + (MEMBERS * square + trace) / float(MEMBERS * (MEMBERS - 1))
    shift = (MEMBERS - 1) * inflation
    towards = jnp.transpose(jnp.broadcast_to(last, (128, 128)))[0:MEMBERS]
    aug = jnp.where(low, gram + jnp.where(eye, shift, 0.0), towards - pltpu.roll(gram, 64, 1))
    for k in range(MEMBERS):
        pivot_row = aug[k : k + 1, :]
        scaled = pivot_row / pivot_row[:, k : k + 1]
        aug = jnp.where(row == k, scaled, aug - aug[:, k : k + 1] * scaled)
    gain = aug - jnp.sum(aug, axis=0, keepdims=True) * (1.0 / MEMBERS)
    weights = jnp.concatenate(
        [jnp.where(low, pltpu.roll(gain, 64, 1), 0.0), jnp.where(low, 0.0, gain)], axis=0
    )
    w_hi, w_lo = split3(weights)
    for c in range(WIDTH // 128):
        x = lat[:, c * 128 : (c + 1) * 128]
        x_hi, x_lo = split3(x)
        dot = lambda a, b: jnp.dot(a, b, preferred_element_type=jnp.float32)
        out[:, c * 128 : (c + 1) * 128] = x + ((dot(x_lo, w_hi) + dot(x_hi, w_lo)) + dot(x_hi, w_hi))


def ring(axis, step):
    count = lax.axis_size(axis)
    return [(i, (i + step) % count) for i in range(count)]


def per_device(latent, kappa, obs_cell, obs_value, obs_var):
    gx, gy = lax.axis_index("gx"), lax.axis_index("gy")
    last_x, last_y = lax.axis_size("gx") - 1, lax.axis_size("gy") - 1
    flags = jnp.stack([gx > 0, gx < last_x, gy > 0, gy < last_y]).astype(jnp.float32)

    rows = jnp.concatenate([latent, jnp.pad(kappa, ((0, 0), (0, 128 - CY)))], axis=1)
    xlo = lax.ppermute(rows[CX - HALO :], "gx", ring("gx", 1))
    xhi = lax.ppermute(rows[:HALO], "gx", ring("gx", -1))

    def cols(at):
        tall = jnp.concatenate(
            [a[:, at * MEMBERS : (at + HALO) * MEMBERS] for a in (latent, xlo, xhi)], axis=0
        )
        thin = jnp.concatenate(
            [kappa[:, at : at + HALO], xlo[:, WIDTH + at : WIDTH + at + HALO], xhi[:, WIDTH + at : WIDTH + at + HALO]], axis=0
        )
        return jnp.concatenate([tall, jnp.pad(thin, ((0, 0), (0, 128 - HALO)))], axis=1)

    ylo = lax.ppermute(cols(CY - HALO), "gy", ring("gy", 1))
    yhi = lax.ppermute(cols(0), "gy", ring("gy", -1))

    odd = (obs_cell % 2).astype(jnp.float32)
    val = jnp.concatenate([obs_value.reshape(2, 128), odd.reshape(2, 128)], axis=0)
    var = obs_var.reshape(2, 128)
    vmem, smem = pl.BlockSpec(memory_space=VMEM), pl.BlockSpec(memory_space=SMEM)
    wide = pltpu.VMEM((EXT_ROWS, EXT_LANES), jnp.float32)
    prior, stat = pl.pallas_call(
        field_kernel,
        out_shape=(
            jax.ShapeDtypeStruct((CX, WIDTH), jnp.float32),
            jax.ShapeDtypeStruct((STAT_ROWS, 128), jnp.float32),
        ),
        in_specs=[smem, smem] + [vmem] * 8,
        out_specs=(vmem, vmem),
        scratch_shapes=[wide] * 4
        + [pltpu.VMEM((r, 128), jnp.float32) for r in (CX * CY // 2, EXT_ROWS, OBS)],
        name="field",
    )(flags, obs_cell, latent, kappa, xlo, xhi, ylo, yhi, val, var)

    for axis in ("gy", "gx"):
        count = lax.axis_size(axis)
        parts = lax.all_to_all(jnp.broadcast_to(stat[None], (count,) + stat.shape), axis, 0, 0)
        if axis == "gy":
            stat = jnp.sum(parts, axis=0)

    latent_new = pl.pallas_call(
        update_kernel,
        out_shape=jax.ShapeDtypeStruct((CX, WIDTH), jnp.float32),
        in_specs=[vmem] * 2,
        out_specs=vmem,
        name="update",
    )(parts, latent)
    return (latent_new, prior)


def solution(mesh):
    placed = (P("gx", "gy"), P("gx", "gy"), P(("gx", "gy")), P(("gx", "gy")), P(("gx", "gy")))
    return jax.shard_map(
        per_device,
        mesh=mesh,
        in_specs=placed,
        out_specs=(P("gx", "gy"), P("gx", "gy")),
        check_vma=False,
    )
```

time: 267 us -> 71 us (0.27)
  the two profiles are of different devices: /device:TPU:2 before, /device:TPU:1 now
where the time goes in v1:
time: 71 us; the launch traced here: 70.7 us
  blocking collectives  37.2 us (52%)
  Pallas kernels  15.1 us (21%)
  starting transfers between devices  8.36 us (12%)
  waiting for transfers between devices  3.98 us (6%)
  other arithmetic  2.68 us (4%)
  local copies, waits for them, and re-layouts  2.6 us (4%)
  between operations  0.76 us (1%)
    all_to_all x2, blocking collectives, per_device(): lax.all_to_all(jnp.broadcast_to(stat[None], (count,) + stat.shape), axis,...  37.2 us
    pallas_call x1, Pallas kernels, per_device(): pl.pallas_call(update_kernel, out_shape=jax.ShapeDtypeStruct((CX, WIDTH),...  8.95 us
    pallas_call x1, Pallas kernels, per_device(): pl.pallas_call(field_kernel, out_shape=(jax.ShapeDtypeStruct((CX, WIDTH),...  6.12 us
    ppermute x1, starting transfers between devices, per_device(): yhi = lax.ppermute(cols(0), 'gy', ring('gy', -1))  3.81 us
    ppermute x1, starting transfers between devices, per_device(): xhi = lax.ppermute(rows[:HALO], 'gx', ring('gx', -1))  3.25 us
    ppermute x1, waiting for transfers between devices, per_device(): xlo = lax.ppermute(rows[CX - HALO:], 'gx', ring('gx', 1))  2.48 us
  transfers between devices with their start and end apart: 4, of which 3 were waited for; matrix products, arithmetic and copies ran while one was open for 3% of the time, Pallas kernels for 0%

profile of v1, /device:TPU:1, one launch (start us, length us, event | category | flops | bytes accessed | tf_op | source)
XLA Modules:
  0.0 70.7 jit_solution(12150017907716913489)
XLA Ops:
  0.6 0.0 copy-start
  0.6 0.0 copy-start.5
  0.7 0.0 copy-start.6
  0.7 1.3 %select_maximum_fusion = f32[64,4224]{1,0:T(8,128)S(1)} fusion(f32[64,64]{1,0:T(8,128)} %kap.1, f32[64,4096]{1,0:T(8,128)} %lat.3), kind=kLoop, calls=%fused_computation | loop fusion | flops 811008 | bytes 2146304 | tf_op jit(solution)/shard_map/concatenate | solution.py:194
  2.0 3.3 %collective-permute-start.1 = (f32[4,4224]{1,0:T(4,128)S(1)}, f32[4,4224]{1,0:T(4,128)S(1)}, u32[]{:S(2)}, u32[]{:S(2)}) collective-permute-start(f32[4,4224]{1,0:T(4,128)S(1)} %get-tuple-element.6), channel_id=1, source_target_pairs={{0,240},{16,0},{32,16},{48,32},{64,48},{80,64},{96,80},{112,96},{1... | collective-permute-start | bytes 202760 | tf_op jit(solution)/shard_map/ppermute | solution.py:196
  5.3 0.0 collective-permute-start
  5.3 0.0 copy-done
  5.3 0.1 fusion.9
  5.4 0.9 %fusion.4 = (f32[64,256]{1,0:T(8,128)S(1)}, f32[64,256]{1,0:T(8,128)S(1)}) fusion(f32[64,4096]{1,0:T(8,128)} %lat.3), kind=kLoop, calls=%fused_computation.18 | loop fusion | bytes 262144 | tf_op jit(solution)/shard_map/slice | solution.py:200
  6.3 0.0 copy-done.5
  6.3 0.0 copy-done.6
  6.3 0.6 pad_maximum_fusion.2.val
  6.9 0.2 collective-permute-done.1.xhi
  7.0 0.0 copy-start.3
  7.0 0.1 fusion.8
  7.1 2.5 %collective-permute-done.xlo = f32[4,4224]{1,0:T(4,128)S(1)} collective-permute-done((f32[4,4224]{1,0:T(4,128)S(1)}, f32[4,4224]{1,0:T(4,128)S(1)}, u32[]{:S(2)}, u32[]{:S(2)}) %collective-permute-start) | collective-permute-done | bytes 67616 | tf_op jit(solution)/shard_map/ppermute | solution.py:195
  9.6 0.0 copy-start.4
  9.6 0.1 fusion.7
  9.7 1.3 %collective-permute-start.2 = (f32[72,384]{1,0:T(8,128)S(1)}, f32[72,384]{1,0:T(8,128)S(1)}, u32[]{:S(2)}, u32[]{:S(2)}) collective-permute-start(f32[72,384]{1,0:T(8,128)S(1)} %pad_maximum_fusion), channel_id=1, source_target_pairs={{0,1},{1,2},{2,3},{3,4},{4,5},{5,6},{6,7},{7,8},{8,9},{9,10},{10,1... | collective-permute-start | bytes 331784 | tf_op jit(solution)/shard_map/ppermute | solution.py:207
  11.1 3.8 %collective-permute-start.3 = (f32[72,384]{1,0:T(8,128)S(1)}, f32[72,384]{1,0:T(8,128)S(1)}, u32[]{:S(2)}, u32[]{:S(2)}) collective-permute-start(f32[72,384]{1,0:T(8,128)S(1)} %pad_maximum_fusion.1), channel_id=1, source_target_pairs={{0,15},{1,0},{2,1},{3,2},{4,3},{5,4},{6,5},{7,6},{8,7},{9,8},{10,9... | collective-permute-start | bytes 331784 | tf_op jit(solution)/shard_map/ppermute | solution.py:208
  14.9 0.7 add_convert_fusion.flags
  15.5 1.4 %collective-permute-done.2.ylo = f32[72,384]{1,0:T(8,128)S(1)} collective-permute-done((f32[72,384]{1,0:T(8,128)S(1)}, f32[72,384]{1,0:T(8,128)S(1)}, u32[]{:S(2)}, u32[]{:S(2)}) %collective-permute-start.2) | collective-permute-done | bytes 110624 | tf_op jit(solution)/shard_map/ppermute | solution.py:207
  16.9 0.0 collective-permute-done.3.yhi
  16.9 0.0 copy-done.3
  16.9 0.0 copy-done.4
  16.9 0.6 copy-done.1
  17.5 0.0 copy-done.2
  17.6 6.1 %field.1 = (f32[64,4096]{1,0:T(8,128)}, f32[40,128]{1,0:T(8,128)}) custom-call(f32[4]{0:T(128)} %add_convert_fusion.flags, s32[256]{0:T(256)} %cell.1, f32[64,4096]{1,0:T(8,128)} %lat.3, f32[64,64]{1,0:T(8,128)} %kap.1, f32[4,4224]{1,0:T(4,128)} %copy-done.4, f32[4,4224]{1,0:T(4,128)} %copy-done.3, f32[72,384]{1,0:T(8,128)} %copy-done.1, ...), custom_call_target="tpu_custom_call" | custom-call | tf_op jit(solution)/shard_map/field/pallas_call | solution.py:215
  23.7 0.7 %broadcast_in_dim.4 = f32[16,40,128]{2,1,0:T(8,128)S(1)} broadcast(f32[40,128]{1,0:T(8,128)} %get-tuple-element.4), dimensions={1,2} | broadcast | bytes 348160 | tf_op jit(solution)/shard_map/broadcast_in_dim | solution.py:230
  24.4 13.9 %all_to_all.10 = f32[16,40,128]{2,1,0:T(8,128)S(1)} all-to-all(f32[16,40,128]{2,1,0:T(8,128)S(1)} %broadcast_in_dim.4), channel_id=1, replica_groups=mesh['gx'=16,'gy'=16] {'gy'}, dimensions={0} | all-to-all | bytes 655360 | tf_op jit(solution)/shard_map/all_to_all | solution.py:230
  38.4 23.3 %all_to_all.11.parts = f32[16,40,128]{2,1,0:T(8,128)} all-to-all(f32[16,40,128]{2,1,0:T(8,128)S(1)} %broadcast_in_dim.5), channel_id=1, replica_groups=mesh['gx'=16,'gy'=16] {'gx'}, dimensions={0} | all-to-all | bytes 655360 | tf_op jit(solution)/shard_map/all_to_all | solution.py:230
  61.7 8.9 %update.1 = f32[64,4096]{1,0:T(8,128)} custom-call(f32[16,40,128]{2,1,0:T(8,128)} %all_to_all.11.parts, f32[64,4096]{1,0:T(8,128)} %lat.3), custom_call_target="tpu_custom_call" | custom-call | tf_op jit(solution)/shard_map/update/pallas_call | solution.py:234
  (12 shorter events, 0.1 us)
Async XLA Ops:
  0.6 4.7 %copy-start = (f32[64,64]{1,0:T(8,128)S(1)}, f32[64,64]{1,0:T(8,128)}, u32[]{:S(2)}) copy-start(f32[64,64]{1,0:T(8,128)} %kap.1) | copy-start | bytes 49156
  0.6 5.6 %copy-start.5 = (s32[256]{0:T(256)S(1)}, s32[256]{0:T(256)}, u32[]{:S(2)}) copy-start(s32[256]{0:T(256)} %cell.1) | copy-start | bytes 3076
  0.7 5.6 %copy-start.6 = (f32[256]{0:T(256)S(1)}, f32[256]{0:T(256)}, u32[]{:S(2)}) copy-start(f32[256]{0:T(256)} %param.8) | copy-start | bytes 3076
  2.0 5.0 %collective-permute-start.1 = (f32[4,4224]{1,0:T(4,128)S(1)}, f32[4,4224]{1,0:T(4,128)S(1)}, u32[]{:S(2)}, u32[]{:S(2)}) collective-permute-start(f32[4,4224]{1,0:T(4,128)S(1)} %get-tuple-element.6), channel_id=1, source_target_pairs={{0,240},{16,0},{32,16},{48,32},{64,48},{80,64},{96,80},{112,96},{1... | collective-permute-start | bytes 202760 | tf_op jit(solution)/shard_map/ppermute | solution.py:196
  5.3 4.3 %collective-permute-start = (f32[4,4224]{1,0:T(4,128)S(1)}, f32[4,4224]{1,0:T(4,128)S(1)}, u32[]{:S(2)}, u32[]{:S(2)}) collective-permute-start(f32[4,4224]{1,0:T(4,128)S(1)} %get-tuple-element.7), channel_id=1, source_target_pairs={{0,16},{16,32},{32,48},{48,64},{64,80},{80,96},{96,112},{112,128},... | collective-permute-start | bytes 202760 | tf_op jit(solution)/shard_map/ppermute | solution.py:195
  7.0 9.8 %copy-start.3 = (f32[4,4224]{1,0:T(4,128)}, f32[4,4224]{1,0:T(4,128)S(1)}, u32[]{:S(2)}) copy-start(f32[4,4224]{1,0:T(4,128)S(1)} %collective-permute-done.1.xhi) | copy-start | bytes 202756
  9.6 7.3 %copy-start.4 = (f32[4,4224]{1,0:T(4,128)}, f32[4,4224]{1,0:T(4,128)S(1)}, u32[]{:S(2)}) copy-start(f32[4,4224]{1,0:T(4,128)S(1)} %collective-permute-done.xlo) | copy-start | bytes 202756
  9.7 7.1 %collective-permute-start.2 = (f32[72,384]{1,0:T(8,128)S(1)}, f32[72,384]{1,0:T(8,128)S(1)}, u32[]{:S(2)}, u32[]{:S(2)}) collective-permute-start(f32[72,384]{1,0:T(8,128)S(1)} %pad_maximum_fusion), channel_id=1, source_target_pairs={{0,1},{1,2},{2,3},{3,4},{4,5},{5,6},{6,7},{7,8},{8,9},{9,10},{10,1... | collective-permute-start | bytes 331784 | tf_op jit(solution)/shard_map/ppermute | solution.py:207
  11.1 5.8 %collective-permute-start.3 = (f32[72,384]{1,0:T(8,128)S(1)}, f32[72,384]{1,0:T(8,128)S(1)}, u32[]{:S(2)}, u32[]{:S(2)}) collective-permute-start(f32[72,384]{1,0:T(8,128)S(1)} %pad_maximum_fusion.1), channel_id=1, source_target_pairs={{0,15},{1,0},{2,1},{3,2},{4,3},{5,4},{6,5},{7,6},{8,7},{9,8},{10,9... | collective-permute-start | bytes 331784 | tf_op jit(solution)/shard_map/ppermute | solution.py:208
  16.9 0.6 copy-start.1
  16.9 0.7 copy-start.2

commit v2 on v0

v2 whole, which is shorter than its diff:
```python
import jax
import jax.numpy as jnp
import numpy as np
from jax import lax
from jax.experimental import pallas as pl
from jax.experimental.pallas import tpu as pltpu
from jax.sharding import PartitionSpec as P

MEMBERS = 64
SWEEPS = 4
LOWER_EDGE = 0.25
UPPER_EDGE = 12.0
HALO = SWEEPS
CX = 64
CY = 64
OBS = 256
TALL = CX + 16
WIDTH = CY * MEMBERS
BLOCKS = WIDTH // 128
EDGE = HALO * MEMBERS
RIM = 6
STAT = 17
HALF = MEMBERS // 2
VMEM = pltpu.MemorySpace.VMEM
SMEM = pltpu.MemorySpace.SMEM
F32 = jnp.float32


def power_coeffs():
    angles = np.pi * (np.arange(64) + 0.5) / 64.0
    centre, half = 0.5 * (UPPER_EDGE + LOWER_EDGE), 0.5 * (UPPER_EDGE - LOWER_EDGE)
    nodes = centre + half * np.cos(angles)
    cheb = [2.0 / 64.0 * np.sum(np.cos(k * angles) / nodes) for k in range(SWEEPS + 1)]
    cheb[0] *= 0.5
    mono = np.polynomial.chebyshev.cheb2poly(cheb)
    return [float(v / half**k) for k, v in enumerate(mono)]


COEFFS = power_coeffs()
CENTRE = 0.5 * (UPPER_EDGE + LOWER_EDGE) - 4.0


def lanes(c):
    return slice(c * 128, (c + 1) * 128)


def sweep(src, xi, alpha, first, last, coeff, scale, store):
    top = src.shape[1] // 128 - 1
    low_half = lax.broadcasted_iota(jnp.int32, (TALL, 128), 1) < MEMBERS

    def turn(c):
        return pltpu.roll(src[:, lanes(min(max(c, 0), top))], 64, 1)

    before, here = turn(first - 1), turn(first)
    for c in range(first, last + 1):
        after = turn(c + 1)
        v = src[:, lanes(c)]
        beside = here + jnp.where(low_half, before, after)
        beside = beside + pltpu.roll(v, 1, 0) + pltpu.roll(v, TALL - 1, 0)
        applied = alpha[:, lanes(c)] * v - beside
        if scale != 1.0:
            applied = applied * scale
        store(c, coeff * xi[:, lanes(c)] + applied)
        before, here = here, after


def spread_kappa(alpha, shifted, count, start):
    upper = (lax.broadcasted_iota(jnp.int32, (TALL, 128), 1) >= MEMBERS).astype(jnp.int32)
    for c in range(count):
        alpha[:, lanes(c)] = jnp.take_along_axis(shifted, upper + (2 * c + start), axis=1)


def rows_kernel(lat_hbm, kap_hbm, to_lo, to_hi, first, last, kap, sems):
    copies = [
        pltpu.make_async_copy(lat_hbm.at[0:8, :], first, sems.at[0]),
        pltpu.make_async_copy(lat_hbm.at[CX - 8 : CX, :], last, sems.at[1]),
        pltpu.make_async_copy(kap_hbm, kap, sems.at[2]),
    ]
    for copy in copies:
        copy.start()
    for copy in copies:
        copy.wait()
    to_lo[:, 0:WIDTH] = first[0:HALO, :]
    to_hi[:, 0:WIDTH] = last[8 - HALO : 8, :]
    blank = jnp.zeros((HALO, 128 - CY), F32)
    to_lo[:, WIDTH:] = jnp.concatenate([kap[0:HALO, :], blank], axis=1)
    to_hi[:, WIDTH:] = jnp.concatenate([kap[CX - HALO : CX, :], blank], axis=1)


def kappa_rows(dst, kap, xlo, xhi):
    dst[...] = jnp.zeros(dst.shape, F32)
    dst[8 : 8 + CX, 0:CY] = kap[...]
    dst[4:8, :] = xlo[:, WIDTH:]
    dst[8 + CX : 12 + CX, :] = xhi[:, WIDTH:]


def cols_kernel(first, last, kap, xlo, xhi, to_lo, to_hi, kext):
    kappa_rows(kext, kap, xlo, xhi)
    turned = jnp.transpose(kext[...])
    for dst, src, at in ((to_lo, first, 0), (to_hi, last, CY - HALO)):
        dst[0:CX, :] = src[...]
        dst[CX : CX + 4, :] = xlo[:, at * MEMBERS : at * MEMBERS + EDGE]
        dst[CX + 4 : CX + 8, :] = xhi[:, at * MEMBERS : at * MEMBERS + EDGE]
        dst[CX + 8 : CX + 16, 128:256] = jnp.zeros((8, 128), F32)
        dst[CX + 12 : CX + 16, 0:128] = jnp.zeros((4, 128), F32)
        dst[CX + 8 : CX + 12, 0:128] = turned[at : at + HALO, :]


def keep_rows(dst, flags):
    def store(c, new):
        dst[0:8, lanes(c)] = new[0:8] * flags[0:1, :]
        dst[8 : 8 + CX, lanes(c)] = new[8 : 8 + CX]
        dst[8 + CX : TALL, lanes(c)] = new[8 + CX : TALL] * flags[1:2, :]

    return store


def into_tiles(tiles, c, new):
    for t in range(CX // 8):
        at = (t * BLOCKS + c) * 8
        tiles[at : at + 8, :] = new[8 + 8 * t : 16 + 8 * t]


def fill_rows(ext, flags, at, body, xlo, xhi, extra=None):
    to = slice(at, at + body.shape[1])
    zero4 = jnp.zeros((4, body.shape[1]), F32)
    reps = body.shape[1] // 128
    low, high = (jnp.concatenate([flags[i : i + 1, :]] * reps, axis=1) for i in (0, 1))
    if extra is not None:
        side = jnp.concatenate([extra] * reps, axis=1)
        body, low, high = body * side, low * side, high * side
    ext[0:4, to] = zero4
    ext[TALL - 4 : TALL, to] = zero4
    ext[8 : 8 + CX, to] = body
    ext[4:8, to] = xlo * low
    ext[8 + CX : 12 + CX, to] = xhi * high


def inner_kernel(flags, lat, kap, xlo, xhi, val, var, tiles, value, weight, odd, ext, alpha, ua, ub, kext):
    for c in range(BLOCKS):
        fill_rows(ext, flags, c * 128, lat[:, lanes(c)], xlo[:, lanes(c)], xhi[:, lanes(c)])
    kappa_rows(kext, kap, xlo, xhi)
    spread_kappa(alpha, kext[0:TALL, :] - CENTRE, BLOCKS, 0)
    top = BLOCKS - 1
    sweep(ext, ext, alpha, 0, top, COEFFS[3], COEFFS[4], keep_rows(ua, flags))
    sweep(ua, ext, alpha, 1, top - 1, COEFFS[2], 1.0, keep_rows(ub, flags))
    sweep(ub, ext, alpha, 1, top - 1, COEFFS[1], 1.0, keep_rows(ua, flags))
    sweep(ua, ext, alpha, 2, top - 2, COEFFS[0], 1.0, lambda c, new: into_tiles(tiles, c, new))

    def column(row):
        pieces = [jnp.transpose(jnp.broadcast_to(row[i : i + 1, :], (128, 128))) for i in range(OBS // 128)]
        return jnp.concatenate(pieces, axis=0)

    value[...] = column(val[0:2, :])
    odd[...] = column(val[2:4, :])
    weight[...] = 1.0 / column(var[0:2, :])


def rim_kernel(
    flags, cell_hbm, lat0, lat1, kap, xlo, xhi, ylo, yhi, value, weight, odd, held,
    tiles, stat, cell, sems, ext, alpha, ua, ub, kext, pbuf,
):
    copies = [pltpu.make_async_copy(cell_hbm, cell, sems.at[CX // 8])]
    for t in range(CX // 8):
        at = pl.ds((t * BLOCKS + 2) * 8, (BLOCKS - 4) * 8)
        copies.append(pltpu.make_async_copy(held.at[at, :], tiles.at[at, :], sems.at[t]))
    for copy in copies:
        copy.start()
    kappa_rows(kext, kap, xlo, xhi)
    own = jnp.transpose(kext[...])
    near = RIM * 128 - EDGE
    for side, (lat, msg) in enumerate(((lat0, ylo), (lat1, yhi))):
        flag = flags[2 + side : 3 + side, :]
        at = 0 if side == 0 else WIDTH - near
        here, there = (EDGE, 0) if side == 0 else (0, near)
        fill_rows(ext, flags, here, lat[...], xlo[:, at : at + near], xhi[:, at : at + near])
        fill_rows(ext, flags, there, msg[0:CX, :], msg[CX : CX + 4, :], msg[CX + 4 : CX + 8, :], flag)
        if side == 0:
            kext[0:4, :] = msg[CX + 8 : CX + 12, 0:128]
            kext[4:16, :] = own[0:12, :]
        else:
            kext[0:8, :] = own[CY - 8 : CY, :]
            kext[8:12, :] = msg[CX + 8 : CX + 12, 0:128]
        shifted = jnp.transpose(kext[...])[0:TALL, :] - CENTRE
        spread_kappa(alpha, shifted, RIM, 0)

        def keep(dst):
            plain = keep_rows(dst, flags)
            outside = (0, 1) if side == 0 else (RIM - 2, RIM - 1)
            return lambda c, new: plain(c, new * flag if c in outside else new)

        def finish(c, new):
            into_tiles(tiles, c - 2 if side == 0 else c + BLOCKS - RIM + 2, new)

        sweep(ext, ext, alpha, 0, RIM - 1, COEFFS[3], COEFFS[4], keep(ua))
        sweep(ua, ext, alpha, 1, RIM - 2, COEFFS[2], 1.0, keep(ub))
        sweep(ub, ext, alpha, 1, RIM - 2, COEFFS[1], 1.0, keep(ua))
        sweep(ua, ext, alpha, 2, RIM - 3, COEFFS[0], 1.0, finish)

    for copy in copies:
        copy.wait()
    for j in range(OBS):
        at = cell[j]
        x, y = lax.shift_right_logical(at, 6), lax.bitwise_and(at, CY - 1)
        row = lax.bitwise_and(x, 56) * BLOCKS + lax.bitwise_and(y, CY - 2) * 4 + lax.bitwise_and(x, 7)
        pbuf[j : j + 1, :] = tiles[pl.ds(row, 1), :]
    both = pbuf[...]
    lane = lax.broadcasted_iota(jnp.int32, (OBS, 128), 1)
    member = lane < MEMBERS
    predicted = jnp.where(odd[...] > 0.5, pltpu.roll(both, 64, 1), both)
    predicted = jnp.where(member, predicted, 0.0)
    mean = jnp.sum(predicted, axis=1, keepdims=True) * (1.0 / MEMBERS)
    spread = jnp.where(member, predicted - mean, jnp.where(lane == MEMBERS, value[...] - mean, 0.0))
    full = lax.dot_general(
        spread * weight[...],
        spread,
        (((0,), (0,)), ((), ())),
        precision=lax.Precision.HIGHEST,
        preferred_element_type=F32,
    )
    lane = lax.broadcasted_iota(jnp.int32, (HALF, 128), 1)
    row = lax.broadcasted_iota(jnp.int32, (HALF, 128), 0)
    first, second = full[0:HALF], full[HALF:MEMBERS]
    packed = jnp.where(lane >= row, first, pltpu.roll(second, 96, 1))
    folded = jnp.where(lane[0:16] < MEMBERS, packed[0:16], pltpu.roll(packed[16:32], 64, 1))
    diagonal = jnp.sum(jnp.where(lane == row + 96, pltpu.roll(second, 64, 1), 0.0), axis=0, keepdims=True)
    last = jnp.where(lane[0:1] < 96, full[MEMBERS : MEMBERS + 1], diagonal)
    stat[0 : STAT - 1, :] = folded
    stat[STAT - 1 : STAT, :] = last


def eliminate(aug):
    size = MEMBERS
    row = lax.broadcasted_iota(jnp.int32, (size, 128), 0)
    for start in range(0, size, 4):
        columns = [jnp.broadcast_to(aug[:, k : k + 1], (size, 128)) for k in range(start, start + 4)]
        for i in range(4):
            k = start + i
            here = row == k
            inverse = 1.0 / columns[i][k : k + 1, :]
            for j in range(i + 1, 4):
                scaled = columns[j][k : k + 1, :] * inverse
                columns[j] = jnp.where(here, scaled, columns[j] - columns[i] * scaled)
            scaled = aug[k : k + 1, :] * inverse
            aug = jnp.where(here, scaled, aug - columns[i] * scaled)
    return aug


def update_kernel(parts, lat, tiles, out_hbm, prior_hbm, total, out, sems):
    copies = [pltpu.make_async_copy(tiles, prior_hbm, sems.at[CX // 8])]
    copies[0].start()
    for i in range(STAT):
        row = parts[0, i]
        for d in range(1, parts.shape[0]):
            row = row + parts[d, i]
        total[i : i + 1, :] = row
    folded, last = total[0:16, :], total[16:17, :]
    packed = jnp.concatenate([folded, pltpu.roll(folded, 64, 1)], axis=0)
    tall = jnp.concatenate([packed, jnp.zeros((32, 128), F32), jnp.broadcast_to(last, (64, 128))], axis=0)
    turned = jnp.transpose(tall)
    lane = lax.broadcasted_iota(jnp.int32, (HALF, 128), 1)
    row = lax.broadcasted_iota(jnp.int32, (HALF, 128), 0)
    first = jnp.where(lane >= row, packed, turned[0:HALF])
    corner = jnp.where(lane < row + HALF, pltpu.roll(packed, 32, 1), pltpu.roll(turned[0:HALF], 32, 1))
    corner = jnp.where(lane == row + HALF, pltpu.roll(last, 64, 1), corner)
    second = jnp.where(lane < HALF, turned[HALF:MEMBERS], corner)
    gram = jnp.concatenate([first, second], axis=0)

    shape = (MEMBERS, 128)
    row = lax.broadcasted_iota(jnp.int32, shape, 0)
    lane = lax.broadcasted_iota(jnp.int32, shape, 1)
    eye = row == lane
    low = lane < MEMBERS
    square = jnp.where(lane[0:1] == MEMBERS, last, 0.0) * float(MEMBERS)
    trace = jnp.sum(jnp.where(eye, gram, 0.0), axis=0, keepdims=True)
    misfit = jnp.sum(square + trace, axis=1, keepdims=True)
    inflation = 1.0 + misfit / float(MEMBERS * (MEMBERS - 1))
    shift = (MEMBERS - 1) * inflation
    right = turned[0:MEMBERS] - pltpu.roll(gram, 64, 1)
    aug = eliminate(jnp.where(low, gram + jnp.where(eye, shift, 0.0), right))
    gain = aug - jnp.sum(aug, axis=0, keepdims=True) * (1.0 / MEMBERS)
    weights = jnp.concatenate(
        [jnp.where(low, pltpu.roll(gain, 64, 1), 0.0), jnp.where(low, 0.0, gain)], axis=0
    )

    def split(a):
        hi = a.astype(jnp.bfloat16)
        return hi, (a - hi.astype(F32)).astype(jnp.bfloat16)

    def dot(a, b):
        return jnp.dot(a, b, preferred_element_type=F32)

    w_hi, w_lo = split(weights)
    for t in range(CX // 8):
        at = slice(t * 256, (t + 1) * 256)
        x = lat[at, :]
        x_hi, x_lo = split(x)
        out[at, :] = x + ((dot(x_lo, w_hi) + dot(x_hi, w_lo)) + dot(x_hi, w_hi))
        copies.append(pltpu.make_async_copy(out.at[at, :], out_hbm.at[at, :], sems.at[t]))
        copies[-1].start()
    for copy in copies:
        copy.wait()


def ring(axis, step):
    count = lax.axis_size(axis)
    return [(i, (i + step) % count) for i in range(count)]


def arr(*shape):
    return jax.ShapeDtypeStruct(shape, F32)


def buf(*shape):
    return pltpu.VMEM(shape, F32)


def params(mib):
    return pltpu.CompilerParams(vmem_limit_bytes=mib << 20)


def cost(flops, moved):
    return pl.CostEstimate(flops=flops, bytes_accessed=moved, transcendentals=0)


def to_tiles(a):
    return a.reshape(CX // 8, 8, BLOCKS, 128).transpose(0, 2, 1, 3).reshape(CX * BLOCKS, 128)


def from_tiles(a):
    return a.reshape(CX // 8, BLOCKS, 8, 128).transpose(0, 2, 1, 3).reshape(CX, WIDTH)


def per_device(latent, kappa, obs_cell, obs_value, obs_var):
    gx, gy = lax.axis_index("gx"), lax.axis_index("gy")
    last_x, last_y = lax.axis_size("gx") - 1, lax.axis_size("gy") - 1
    inside = jnp.stack([gx > 0, gx < last_x, gy > 0, gy < last_y] * 2).astype(F32)
    flags = jnp.broadcast_to(inside[:, None], (8, 128))
    odd = (obs_cell % 2).astype(F32)
    val = jnp.concatenate([obs_value.reshape(2, 128), odd.reshape(2, 128)], axis=0)
    var = obs_var.reshape(2, 128)
    vmem, anywhere = pl.BlockSpec(memory_space=VMEM), pl.BlockSpec(memory_space=pl.ANY)
    hbm = pl.BlockSpec(memory_space=pltpu.MemorySpace.HBM)

    def part(shape, *at):
        return pl.BlockSpec(shape, lambda i: at)

    to_lo, to_hi = pl.pallas_call(
        rows_kernel,
        out_shape=(arr(HALO, WIDTH + 128),) * 2,
        in_specs=[hbm, hbm],
        out_specs=(vmem, vmem),
        scratch_shapes=[buf(8, WIDTH), buf(8, WIDTH), buf(CX, CY), pltpu.SemaphoreType.DMA((3,))],
        compiler_params=params(4),
        name="rows",
    )(latent, kappa)
    xlo = lax.ppermute(to_hi, "gx", ring("gx", 1))
    xhi = lax.ppermute(to_lo, "gx", ring("gx", -1))

    whole = part((HALO, WIDTH + 128), 0, 0)
    to_lo, to_hi = pl.pallas_call(
        cols_kernel,
        grid=(1,),
        out_shape=(arr(CX + 16, EDGE),) * 2,
        in_specs=[part((CX, EDGE), 0, 0), part((CX, EDGE), 0, WIDTH // EDGE - 1), part((CX, CY), 0, 0), whole, whole],
        out_specs=(part((CX + 16, EDGE), 0, 0),) * 2,
        scratch_shapes=[buf(128, 128)],
        compiler_params=params(4),
        name="cols",
    )(latent, latent, kappa, xlo, xhi)
    ylo = lax.ppermute(to_hi, "gy", ring("gy", 1))
    yhi = lax.ppermute(to_lo, "gy", ring("gy", -1))

    tiles, value, weight, odd = pl.pallas_call(
        inner_kernel,
        out_shape=(arr(CX * BLOCKS, 128), arr(OBS, 128), arr(OBS, 128), arr(OBS, 128)),
        in_specs=[vmem] * 7,
        out_specs=(vmem,) * 4,
        scratch_shapes=[buf(TALL, WIDTH)] * 4 + [buf(128, 128)],
        compiler_params=params(12),
        cost_estimate=cost(20_000_000, 12_000_000),
        name="inner",
    )(flags, latent, kappa, xlo, xhi, val, var)

    near = RIM * 128 - EDGE
    whole_of = lambda a: part(a.shape, *([0] * a.ndim))
    operands = (kappa, xlo, xhi, ylo, yhi, value, weight, odd, tiles)
    tiles, stat = pl.pallas_call(
        rim_kernel,
        grid=(1,),
        out_shape=(arr(CX * BLOCKS, 128), arr(STAT, 128)),
        in_specs=[
            whole_of(flags),
            anywhere,
            part((CX, near), 0, 0),
            part((CX, near), 0, WIDTH // near - 1),
            *(whole_of(a) for a in operands[:-1]),
            vmem,
        ],
        out_specs=(vmem, part((STAT, 128), 0, 0)),
        scratch_shapes=[pltpu.SMEM((OBS,), jnp.int32), pltpu.SemaphoreType.DMA((CX // 8 + 1,))]
        + [buf(TALL, RIM * 128)] * 4
        + [buf(128, 128), buf(OBS, 128)],
        compiler_params=params(12),
        name="rim",
    )(flags, obs_cell, latent, latent, *operands)

    stat = stat[:, None, :]
    for axis in ("gy", "gx"):
        count = lax.axis_size(axis)
        parts = lax.all_to_all(jnp.broadcast_to(stat[None], (count,) + stat.shape), axis, 0, 0)
        if axis == "gy":
            stat = jnp.sum(parts, axis=0)

    latent_new, prior = pl.pallas_call(
        update_kernel,
        out_shape=(arr(CX * BLOCKS, 128),) * 2,
        in_specs=[vmem] * 3,
        out_specs=(anywhere,) * 2,
        scratch_shapes=[buf(24, 128), buf(CX * BLOCKS, 128), pltpu.SemaphoreType.DMA((CX // 8 + 1,))],
        compiler_params=params(12),
        name="update",
    )(parts, to_tiles(latent), tiles)
    return (from_tiles(latent_new), from_tiles(prior))


def solution(mesh):
    placed = (P("gx", "gy"), P("gx", "gy"), P(("gx", "gy")), P(("gx", "gy")), P(("gx", "gy")))
    return jax.shard_map(
        per_device,
        mesh=mesh,
        in_specs=placed,
        out_specs=(P("gx", "gy"), P("gx", "gy")),
        check_vma=False,
    )
```

time: 267 us -> 58.1 us (0.22)
  the two profiles are of different devices: /device:TPU:2 before, /device:TPU:1 now
where the time goes in v2:
time: 58.1 us; the launch traced here: 57.8 us
  blocking collectives  31.1 us (54%)
  Pallas kernels  11.3 us (19%)
  starting transfers between devices  8.36 us (14%)
  waiting for transfers between devices  3.34 us (6%)
  local copies, waits for them, and re-layouts  2.92 us (5%)
  between operations  0.74 us (1%)
    all_to_all x2, blocking collectives, per_device(): lax.all_to_all(jnp.broadcast_to(stat[None], (count,) + stat.shape), axis,...  31.1 us
    pallas_call x1, Pallas kernels, per_device(): pl.pallas_call(update_kernel, out_shape=(arr(CX * BLOCKS, 128),) * 2, in_...  4.16 us
    pallas_call x1, Pallas kernels, per_device(): pl.pallas_call(rim_kernel, grid=(1,), out_shape=(arr(CX * BLOCKS, 128), a...  3.83 us
    ppermute x1, starting transfers between devices, per_device(): yhi = lax.ppermute(to_lo, 'gy', ring('gy', -1))  3.82 us
    ppermute x1, starting transfers between devices, per_device(): xlo = lax.ppermute(to_hi, 'gx', ring('gx', 1))  3.04 us
    pallas_call x1, Pallas kernels, per_device(): pl.pallas_call(inner_kernel, out_shape=(arr(CX * BLOCKS, 128), arr(OBS, 1...  2.83 us
    unnamed x14, local copies, waits for them, and re-layouts  2.6 us
    ppermute x1, waiting for transfers between devices, per_device(): xhi = lax.ppermute(to_lo, 'gx', ring('gx', -1))  2.36 us
  transfers between devices with their start and end apart: 4, of which 2 were waited for; matrix products, arithmetic and copies ran while one was open for 0% of the time, Pallas kernels for 5%

profile of v2, /device:TPU:1, one launch (start us, length us, event | category | flops | bytes accessed | tf_op | source)
XLA Modules:
  0.0 57.8 jit_solution(6744867904677816268)
XLA Ops:
  0.6 0.0 copy-start
  0.6 1.2 %copy-done = f32[64,4096]{1,0:T(8,128)S(1)} copy-done((f32[64,4096]{1,0:T(8,128)S(1)}, f32[64,4096]{1,0:T(8,128)}, u32[]{:S(2)}) %copy-start) | copy-done | bytes 1048600
  1.9 0.0 copy-start.2
  1.9 0.8 %copy-done.2 = f32[64,64]{1,0:T(8,128)S(1)} copy-done((f32[64,64]{1,0:T(8,128)S(1)}, f32[64,64]{1,0:T(8,128)}, u32[]{:S(2)}) %copy-start.2) | copy-done | bytes 16408
  2.6 0.0 copy-start.4
  2.6 0.4 rows.1
  3.0 0.0 copy-start.3
  3.0 3.0 %collective-permute-start = (f32[4,4224]{1,0:T(4,128)S(1)}, f32[4,4224]{1,0:T(4,128)S(1)}, u32[]{:S(2)}, u32[]{:S(2)}) collective-permute-start(f32[4,4224]{1,0:T(4,128)S(1)} %get-tuple-element.14), channel_id=1, source_target_pairs={{0,16},{16,32},{32,48},{48,64},{64,80},{80,96},{96,112},{112,128},... | collective-permute-start | bytes 202760 | tf_op jit(solution)/shard_map/ppermute | solution.py:357
  6.1 0.2 collective-permute-start.1
  6.3 0.0 copy-done.4
  6.3 0.1 stack.23
  6.5 1.0 %collective-permute-done.xlo = f32[4,4224]{1,0:T(4,128)S(1)} collective-permute-done((f32[4,4224]{1,0:T(4,128)S(1)}, f32[4,4224]{1,0:T(4,128)S(1)}, u32[]{:S(2)}, u32[]{:S(2)}) %collective-permute-start) | collective-permute-done | bytes 67616 | tf_op jit(solution)/shard_map/ppermute | solution.py:357
  7.4 2.4 %collective-permute-done.1.xhi = f32[4,4224]{1,0:T(4,128)S(1)} collective-permute-done((f32[4,4224]{1,0:T(4,128)S(1)}, f32[4,4224]{1,0:T(4,128)S(1)}, u32[]{:S(2)}, u32[]{:S(2)}) %collective-permute-start.1) | collective-permute-done | bytes 67616 | tf_op jit(solution)/shard_map/ppermute | solution.py:358
  9.8 0.0 copy-done.1
  9.8 0.0 copy-done.3
  9.8 0.1 cols.1
  9.9 1.3 %collective-permute-start.2 = (f32[80,256]{1,0:T(8,128)S(1)}, f32[80,256]{1,0:T(8,128)S(1)}, u32[]{:S(2)}, u32[]{:S(2)}) collective-permute-start(f32[80,256]{1,0:T(8,128)S(1)} %get-tuple-element.16), channel_id=1, source_target_pairs={{0,1},{1,2},{2,3},{3,4},{4,5},{5,6},{6,7},{7,8},{8,9},{9,10},{10,1... | collective-permute-start | bytes 245768 | tf_op jit(solution)/shard_map/ppermute | solution.py:371
  11.1 3.8 %collective-permute-start.3 = (f32[80,256]{1,0:T(8,128)S(1)}, f32[80,256]{1,0:T(8,128)S(1)}, u32[]{:S(2)}, u32[]{:S(2)}) collective-permute-start(f32[80,256]{1,0:T(8,128)S(1)} %get-tuple-element.17), channel_id=1, source_target_pairs={{0,15},{1,0},{2,1},{3,2},{4,3},{5,4},{6,5},{7,6},{8,7},{9,8},{10,9... | collective-permute-start | bytes 245768 | tf_op jit(solution)/shard_map/ppermute | solution.py:372
  15.0 0.0 copy-done.6
  15.0 0.0 copy-start.5
  15.0 0.1 broadcast_in_dim.6.flags
  15.1 0.6 %copy-done.5 = f32[256]{0:T(256)S(1)} copy-done((f32[256]{0:T(256)S(1)}, f32[256]{0:T(256)}, u32[]{:S(2)}) %copy-start.5) | copy-done | bytes 1048
  15.7 2.8 %inner.1 = (f32[2048,128]{1,0:T(8,128)S(1)}, f32[256,128]{1,0:T(8,128)S(1)}, f32[256,128]{1,0:T(8,128)S(1)}, f32[256,128]{1,0:T(8,128)S(1)}) custom-call(f32[8,128]{1,0:T(8,128)S(1)} %broadcast_in_dim.6.flags, f32[64,4096]{1,0:T(8,128)S(1)} %copy-done.1, f32[64,64]{1,0:T(8,128)S(1)} %copy-done.3, f32[4,4224]{1,0:T(4,128)S(1)} %collective-permute-done.xlo, ...), custom_call_target="tpu_custom_call" | custom-call | flops 20000000 | bytes 12000000 | tf_op jit(solution)/shard_map/inner/pallas_call | solution.py:374
  18.5 0.0 collective-permute-done.2.ylo
  18.5 0.0 collective-permute-done.3.yhi
  18.5 3.8 %rim.1 = (f32[2048,128]{1,0:T(8,128)S(1)}, f32[17,128]{1,0:T(8,128)S(1)}) custom-call(f32[8,128]{1,0:T(8,128)S(1)} %broadcast_in_dim.6.flags, s32[256]{0:T(256)S(1)} %copy-done.4, f32[64,4096]{1,0:T(8,128)S(1)} %copy-done.1, f32[64,4096]{1,0:T(8,128)S(1)} %copy-done.1, f32[64,64]{1,0:T(8,128)S(1)} %copy-done.3, f32[4,4224]{1,0:T(4,128)S(1)} %collective-permute-done.xlo, ...), custom_call_target="tpu_custom_call" | custom-call | tf_op jit(solution)/shard_map/rim/pallas_call | solution.py:388
  22.3 0.1 broadcast_in_dim.7
  22.4 11.1 %all_to_all.10 = f32[16,17,1,128]{3,2,1,0:T(1,128)S(1)} all-to-all(f32[16,17,1,128]{3,2,1,0:T(1,128)S(1)} %broadcast_in_dim.7), channel_id=1, replica_groups=mesh['gx'=16,'gy'=16] {'gy'}, dimensions={0} | all-to-all | bytes 278528 | tf_op jit(solution)/shard_map/all_to_all | solution.py:411
  33.5 0.1 reduce_sum.9
  33.6 0.1 broadcast_in_dim.8
  33.7 19.9 %all_to_all.11.parts = f32[16,17,1,128]{3,2,1,0:T(1,128)S(1)} all-to-all(f32[16,17,1,128]{3,2,1,0:T(1,128)S(1)} %broadcast_in_dim.8), channel_id=1, replica_groups=mesh['gx'=16,'gy'=16] {'gx'}, dimensions={0} | all-to-all | bytes 278528 | tf_op jit(solution)/shard_map/all_to_all | solution.py:411
  53.7 4.2 %update.1 = (f32[2048,128]{1,0:T(8,128)}, f32[2048,128]{1,0:T(8,128)}) custom-call(f32[16,17,1,128]{3,2,1,0:T(1,128)S(1)} %all_to_all.11.parts, f32[2048,128]{1,0:T(8,128)S(1)} %bitcast.23, f32[2048,128]{1,0:T(8,128)S(1)} %get-tuple-element.23.tiles), custom_call_target="tpu_custom_call" | custom-call | tf_op jit(solution)/shard_map/update/pallas_call | solution.py:415
  (5 shorter events, 0.0 us)
Async XLA Ops:
  0.6 1.2 %copy-start = (f32[64,4096]{1,0:T(8,128)S(1)}, f32[64,4096]{1,0:T(8,128)}, u32[]{:S(2)}) copy-start(f32[64,4096]{1,0:T(8,128)} %lat1.1) | copy-start | bytes 3145732
  1.9 0.8 %copy-start.2 = (f32[64,64]{1,0:T(8,128)S(1)}, f32[64,64]{1,0:T(8,128)}, u32[]{:S(2)}) copy-start(f32[64,64]{1,0:T(8,128)} %kap.5) | copy-start | bytes 49156
  2.6 3.7 %copy-start.4 = (s32[256]{0:T(256)S(1)}, s32[256]{0:T(256)}, u32[]{:S(2)}) copy-start(s32[256]{0:T(256)} %cell_hbm.1) | copy-start | bytes 3076
  2.6 7.2 %copy-start.1 = (f32[64,4096]{1,0:T(8,128)S(1)}, f32[64,4096]{1,0:T(8,128)}, u32[]{:S(2)}) copy-start(f32[64,4096]{1,0:T(8,128)} %lat1.1) | copy-start | bytes 3145732
  3.0 6.8 %copy-start.3 = (f32[64,64]{1,0:T(8,128)S(1)}, f32[64,64]{1,0:T(8,128)}, u32[]{:S(2)}) copy-start(f32[64,64]{1,0:T(8,128)} %kap.5) | copy-start | bytes 49156
  3.0 4.4 %collective-permute-start = (f32[4,4224]{1,0:T(4,128)S(1)}, f32[4,4224]{1,0:T(4,128)S(1)}, u32[]{:S(2)}, u32[]{:S(2)}) collective-permute-start(f32[4,4224]{1,0:T(4,128)S(1)} %get-tuple-element.14), channel_id=1, source_target_pairs={{0,16},{16,32},{32,48},{48,64},{64,80},{80,96},{96,112},{112,128},... | collective-permute-start | bytes 202760 | tf_op jit(solution)/shard_map/ppermute | solution.py:357
  6.1 3.7 %collective-permute-start.1 = (f32[4,4224]{1,0:T(4,128)S(1)}, f32[4,4224]{1,0:T(4,128)S(1)}, u32[]{:S(2)}, u32[]{:S(2)}) collective-permute-start(f32[4,4224]{1,0:T(4,128)S(1)} %get-tuple-element.15), channel_id=1, source_target_pairs={{0,240},{16,0},{32,16},{48,32},{64,48},{80,64},{96,80},{112,96},{1... | collective-permute-start | bytes 202760 | tf_op jit(solution)/shard_map/ppermute | solution.py:358
  9.9 8.6 %collective-permute-start.2 = (f32[80,256]{1,0:T(8,128)S(1)}, f32[80,256]{1,0:T(8,128)S(1)}, u32[]{:S(2)}, u32[]{:S(2)}) collective-permute-start(f32[80,256]{1,0:T(8,128)S(1)} %get-tuple-element.16), channel_id=1, source_target_pairs={{0,1},{1,2},{2,3},{3,4},{4,5},{5,6},{6,7},{7,8},{8,9},{9,10},{10,1... | collective-permute-start | bytes 245768 | tf_op jit(solution)/shard_map/ppermute | solution.py:371
  11.1 3.8 %copy-start.6 = (f32[256]{0:T(256)S(1)}, f32[256]{0:T(256)}, u32[]{:S(2)}) copy-start(f32[256]{0:T(256)} %param.8) | copy-start | bytes 3076
  11.1 7.4 %collective-permute-start.3 = (f32[80,256]{1,0:T(8,128)S(1)}, f32[80,256]{1,0:T(8,128)S(1)}, u32[]{:S(2)}, u32[]{:S(2)}) collective-permute-start(f32[80,256]{1,0:T(8,128)S(1)} %get-tuple-element.17), channel_id=1, source_target_pairs={{0,15},{1,0},{2,1},{3,2},{4,3},{5,4},{6,5},{7,6},{8,7},{9,8},{10,9... | collective-permute-start | bytes 245768 | tf_op jit(solution)/shard_map/ppermute | solution.py:372
  15.0 0.7 %copy-start.5 = (f32[256]{0:T(256)S(1)}, f32[256]{0:T(256)}, u32[]{:S(2)}) copy-start(f32[256]{0:T(256)} %param.9) | copy-start | bytes 3076

commit v3 on v2

--- a/solution.py
+++ b/solution.py
@@ -40,51 +40,64 @@
 CENTRE = 0.5 * (UPPER_EDGE + LOWER_EDGE) - 4.0
 
 
+PAD = 8
+
+
 def lanes(c):
     return slice(c * 128, (c + 1) * 128)
 
 
-def sweep(src, xi, alpha, first, last, coeff, scale, store):
-    top = src.shape[1] // 128 - 1
-    low_half = lax.broadcasted_iota(jnp.int32, (TALL, 128), 1) < MEMBERS
+def stencil_buf(blocks):
+    return pltpu.VMEM((blocks * TALL + 2 * PAD, 128), F32)
+
+
+def rows_of(c, first=0, count=TALL):
+    at = PAD + c * TALL + first
+    return slice(at, at + count)
+
+
+def sweep(src, xi, alpha, blocks, first, last, coeff, scale, store, tiles=(0, TALL)):
+    at, count = tiles[0], tiles[1] - tiles[0]
+    low_half = lax.broadcasted_iota(jnp.int32, (count, 128), 1) < MEMBERS
 
     def turn(c):
-        return pltpu.roll(src[:, lanes(min(max(c, 0), top))], 64, 1)
+        return pltpu.roll(src[rows_of(min(max(c, 0), blocks - 1), at, count), :], 64, 1)
 
     before, here = turn(first - 1), turn(first)
     for c in range(first, last + 1):
         after = turn(c + 1)
-        v = src[:, lanes(c)]
+        here_rows = rows_of(c, at, count)
         beside = here + jnp.where(low_half, before, after)
-        beside = beside + pltpu.roll(v, 1, 0) + pltpu.roll(v, TALL - 1, 0)
-        applied = alpha[:, lanes(c)] * v - beside
+        beside = beside + (src[rows_of(c, at - 1, count), :] + src[rows_of(c, at + 1, count), :])
+        applied = alpha[here_rows, :] * src[here_rows, :] - beside
         if scale != 1.0:
             applied = applied * scale
-        store(c, coeff * xi[:, lanes(c)] + applied)
+        store(c, coeff * xi[here_rows, :] + applied)
         before, here = here, after
 
 
 def spread_kappa(alpha, shifted, count, start):
     upper = (lax.broadcasted_iota(jnp.int32, (TALL, 128), 1) >= MEMBERS).astype(jnp.int32)
     for c in range(count):
-        alpha[:, lanes(c)] = jnp.take_along_axis(shifted, upper + (2 * c + start), axis=1)
-
-
-def rows_kernel(lat_hbm, kap_hbm, to_lo, to_hi, first, last, kap, sems):
+        alpha[rows_of(c), :] = jnp.take_along_axis(shifted, upper + (2 * c + start), axis=1)
+
+
+def rows_kernel(lat_hbm, kap_hbm, to_lo, to_hi, kap, sems):
     copies = [
-        pltpu.make_async_copy(lat_hbm.at[0:8, :], first, sems.at[0]),
-        pltpu.make_async_copy(lat_hbm.at[CX - 8 : CX, :], last, sems.at[1]),
-        pltpu.make_async_copy(kap_hbm, kap, sems.at[2]),
+        pltpu.make_async_copy(kap_hbm.at[0:8, :], kap.at[0:8, :], sems.at[0]),
+        pltpu.make_async_copy(kap_hbm.at[CX - 8 : CX, :], kap.at[8:16, :], sems.at[1]),
+        pltpu.make_async_copy(lat_hbm.at[0:HALO, :], to_lo.at[:, 0:WIDTH], sems.at[2]),
+        pltpu.make_async_copy(lat_hbm.at[CX - HALO : CX, :], to_hi.at[:, 0:WIDTH], sems.at[3]),
     ]
     for copy in copies:
         copy.start()
-    for copy in copies:
-        copy.wait()
-    to_lo[:, 0:WIDTH] = first[0:HALO, :]
-    to_hi[:, 0:WIDTH] = last[8 - HALO : 8, :]
+    copies[0].wait()
+    copies[1].wait()
     blank = jnp.zeros((HALO, 128 - CY), F32)
     to_lo[:, WIDTH:] = jnp.concatenate([kap[0:HALO, :], blank], axis=1)
-    to_hi[:, WIDTH:] = jnp.concatenate([kap[CX - HALO : CX, :], blank], axis=1)
+    to_hi[:, WIDTH:] = jnp.concatenate([kap[16 - HALO : 16, :], blank], axis=1)
+    copies[2].wait()
+    copies[3].wait()
 
 
 def kappa_rows(dst, kap, xlo, xhi):
@@ -108,9 +121,9 @@
 
 def keep_rows(dst, flags):
     def store(c, new):
-        dst[0:8, lanes(c)] = new[0:8] * flags[0:1, :]
-        dst[8 : 8 + CX, lanes(c)] = new[8 : 8 + CX]
-        dst[8 + CX : TALL, lanes(c)] = new[8 + CX : TALL] * flags[1:2, :]
+        dst[rows_of(c, 0, 8), :] = new[0:8] * flags[0:1, :]
+        dst[rows_of(c, 8, CX), :] = new[8 : 8 + CX]
+        dst[rows_of(c, 8 + CX, 8), :] = new[8 + CX : TALL] * flags[1:2, :]
 
     return store
 
@@ -118,34 +131,28 @@
 def into_tiles(tiles, c, new):
     for t in range(CX // 8):
         at = (t * BLOCKS + c) * 8
-        tiles[at : at + 8, :] = new[8 + 8 * t : 16 + 8 * t]
-
-
-def fill_rows(ext, flags, at, body, xlo, xhi, extra=None):
-    to = slice(at, at + body.shape[1])
-    zero4 = jnp.zeros((4, body.shape[1]), F32)
-    reps = body.shape[1] // 128
-    low, high = (jnp.concatenate([flags[i : i + 1, :]] * reps, axis=1) for i in (0, 1))
-    if extra is not None:
-        side = jnp.concatenate([extra] * reps, axis=1)
-        body, low, high = body * side, low * side, high * side
-    ext[0:4, to] = zero4
-    ext[TALL - 4 : TALL, to] = zero4
-    ext[8 : 8 + CX, to] = body
-    ext[4:8, to] = xlo * low
-    ext[8 + CX : 12 + CX, to] = xhi * high
+        tiles[at : at + 8, :] = new[8 * t : 8 * t + 8]
+
+
+def fill(ext, c, body, xlo, xhi, low, high):
+    zero4 = jnp.zeros((4, 128), F32)
+    ext[rows_of(c, 0, 4), :] = zero4
+    ext[rows_of(c, 4, 4), :] = xlo * low
+    ext[rows_of(c, 8, CX), :] = body
+    ext[rows_of(c, 8 + CX, 4), :] = xhi * high
+    ext[rows_of(c, 12 + CX, 4), :] = zero4
 
 
 def inner_kernel(flags, lat, kap, xlo, xhi, val, var, tiles, value, weight, odd, ext, alpha, ua, ub, kext):
     for c in range(BLOCKS):
-        fill_rows(ext, flags, c * 128, lat[:, lanes(c)], xlo[:, lanes(c)], xhi[:, lanes(c)])
+        fill(ext, c, lat[:, lanes(c)], xlo[:, lanes(c)], xhi[:, lanes(c)], flags[0:1, :], flags[1:2, :])
     kappa_rows(kext, kap, xlo, xhi)
     spread_kappa(alpha, kext[0:TALL, :] - CENTRE, BLOCKS, 0)
-    top = BLOCKS - 1
-    sweep(ext, ext, alpha, 0, top, COEFFS[3], COEFFS[4], keep_rows(ua, flags))
-    sweep(ua, ext, alpha, 1, top - 1, COEFFS[2], 1.0, keep_rows(ub, flags))
-    sweep(ub, ext, alpha, 1, top - 1, COEFFS[1], 1.0, keep_rows(ua, flags))
-    sweep(ua, ext, alpha, 2, top - 2, COEFFS[0], 1.0, lambda c, new: into_tiles(tiles, c, new))
+    top, inside = BLOCKS - 1, (8, 8 + CX)
+    sweep(ext, ext, alpha, BLOCKS, 0, top, COEFFS[3], COEFFS[4], keep_rows(ua, flags))
+    sweep(ua, ext, alpha, BLOCKS, 1, top - 1, COEFFS[2], 1.0, keep_rows(ub, flags))
+    sweep(ub, ext, alpha, BLOCKS, 1, top - 1, COEFFS[1], 1.0, keep_rows(ua, flags))
+    sweep(ua, ext, alpha, BLOCKS, 2, top - 2, COEFFS[0], 1.0, lambda c, new: into_tiles(tiles, c, new), inside)
 
     def column(row):
         pieces = [jnp.transpose(jnp.broadcast_to(row[i : i + 1, :], (128, 128))) for i in range(OBS // 128)]
@@ -157,32 +164,31 @@
 
 
 def rim_kernel(
-    flags, cell_hbm, lat0, lat1, kap, xlo, xhi, ylo, yhi, value, weight, odd, held,
-    tiles, stat, cell, sems, ext, alpha, ua, ub, kext, pbuf,
+    flags, cell_vmem, lat0, lat1, kap, xlo, xhi, ylo, yhi, value, weight, odd, held,
+    tiles, stat, cell, sem, ext, alpha, ua, ub, kext, pbuf,
 ):
-    copies = [pltpu.make_async_copy(cell_hbm, cell, sems.at[CX // 8])]
-    for t in range(CX // 8):
-        at = pl.ds((t * BLOCKS + 2) * 8, (BLOCKS - 4) * 8)
-        copies.append(pltpu.make_async_copy(held.at[at, :], tiles.at[at, :], sems.at[t]))
-    for copy in copies:
-        copy.start()
+    fetch = pltpu.make_async_copy(cell_vmem, cell, sem)
+    fetch.start()
     kappa_rows(kext, kap, xlo, xhi)
     own = jnp.transpose(kext[...])
-    near = RIM * 128 - EDGE
+    near = RIM - 2
     for side, (lat, msg) in enumerate(((lat0, ylo), (lat1, yhi))):
         flag = flags[2 + side : 3 + side, :]
-        at = 0 if side == 0 else WIDTH - near
-        here, there = (EDGE, 0) if side == 0 else (0, near)
-        fill_rows(ext, flags, here, lat[...], xlo[:, at : at + near], xhi[:, at : at + near])
-        fill_rows(ext, flags, there, msg[0:CX, :], msg[CX : CX + 4, :], msg[CX + 4 : CX + 8, :], flag)
+        low, high = flags[0:1, :], flags[1:2, :]
+        for i in range(near):
+            at = lanes(i if side == 0 else BLOCKS - near + i)
+            fill(ext, i + 2 if side == 0 else i, lat[:, lanes(i)], xlo[:, at], xhi[:, at], low, high)
+        for i in range(2):
+            body = msg[0:CX, lanes(i)] * flag
+            halo = msg[CX : CX + 4, lanes(i)], msg[CX + 4 : CX + 8, lanes(i)]
+            fill(ext, i if side == 0 else near + i, body, *halo, low * flag, high * flag)
         if side == 0:
             kext[0:4, :] = msg[CX + 8 : CX + 12, 0:128]
             kext[4:16, :] = own[0:12, :]
         else:
             kext[0:8, :] = own[CY - 8 : CY, :]
             kext[8:12, :] = msg[CX + 8 : CX + 12, 0:128]
-        shifted = jnp.transpose(kext[...])[0:TALL, :] - CENTRE
-        spread_kappa(alpha, shifted, RIM, 0)
+        spread_kappa(alpha, jnp.transpose(kext[...])[0:TALL, :] - CENTRE, RIM, 0)
 
         def keep(dst):
             plain = keep_rows(dst, flags)
@@ -192,18 +198,14 @@
         def finish(c, new):
             into_tiles(tiles, c - 2 if side == 0 else c + BLOCKS - RIM + 2, new)
 
-        sweep(ext, ext, alpha, 0, RIM - 1, COEFFS[3], COEFFS[4], keep(ua))
-        sweep(ua, ext, alpha, 1, RIM - 2, COEFFS[2], 1.0, keep(ub))
-        sweep(ub, ext, alpha, 1, RIM - 2, COEFFS[1], 1.0, keep(ua))
-        sweep(ua, ext, alpha, 2, RIM - 3, COEFFS[0], 1.0, finish)
-
-    for copy in copies:
-        copy.wait()
+        sweep(ext, ext, alpha, RIM, 0, RIM - 1, COEFFS[3], COEFFS[4], keep(ua))
+        sweep(ua, ext, alpha, RIM, 1, RIM - 2, COEFFS[2], 1.0, keep(ub))
+        sweep(ub, ext, alpha, RIM, 1, RIM - 2, COEFFS[1], 1.0, keep(ua))
+        sweep(ua, ext, alpha, RIM, 2, RIM - 3, COEFFS[0], 1.0, finish, (8, 8 + CX))
+
+    fetch.wait()
     for j in range(OBS):
-        at = cell[j]
-        x, y = lax.shift_right_logical(at, 6), lax.bitwise_and(at, CY - 1)
-        row = lax.bitwise_and(x, 56) * BLOCKS + lax.bitwise_and(y, CY - 2) * 4 + lax.bitwise_and(x, 7)
-        pbuf[j : j + 1, :] = tiles[pl.ds(row, 1), :]
+        pbuf[j : j + 1, :] = tiles[pl.ds(cell[j], 1), :]
     both = pbuf[...]
     lane = lax.broadcasted_iota(jnp.int32, (OBS, 128), 1)
     member = lane < MEMBERS
@@ -230,19 +232,32 @@
 
 
 def eliminate(aug):
-    size = MEMBERS
+    size = 8
     row = lax.broadcasted_iota(jnp.int32, (size, 128), 0)
-    for start in range(0, size, 4):
-        columns = [jnp.broadcast_to(aug[:, k : k + 1], (size, 128)) for k in range(start, start + 4)]
-        for i in range(4):
-            k = start + i
-            here = row == k
-            inverse = 1.0 / columns[i][k : k + 1, :]
-            for j in range(i + 1, 4):
-                scaled = columns[j][k : k + 1, :] * inverse
-                columns[j] = jnp.where(here, scaled, columns[j] - columns[i] * scaled)
-            scaled = aug[k : k + 1, :] * inverse
-            aug = jnp.where(here, scaled, aug - columns[i] * scaled)
+    for start in range(0, MEMBERS, size):
+        columns = [jnp.broadcast_to(aug[:, k : k + 1], (MEMBERS, 128)) for k in range(start, start + size)]
+        block = [column[start : start + size] for column in columns]
+        pivot_rows = aug[start : start + size]
+        for i in range(size):
+            here = row == i
+            inverse = 1.0 / block[i][i : i + 1]
+
+            def clear(a):
+                scaled = a[i : i + 1] * inverse
+                return jnp.where(here, scaled, a - block[i] * scaled)
+
+            block = block[: i + 1] + [clear(a) for a in block[i + 1 :]]
+            pivot_rows = clear(pivot_rows)
+        pieces = []
+        for at in range(0, MEMBERS, size):
+            if at == start:
+                pieces.append(pivot_rows)
+                continue
+            terms = [column[at : at + size] * pivot_rows[i : i + 1] for i, column in enumerate(columns)]
+            while len(terms) > 1:
+                terms = [a + b for a, b in zip(terms[0::2], terms[1::2])]
+            pieces.append(aug[at : at + size] - terms[0])
+        aug = jnp.concatenate(pieces, axis=0)
     return aug
 
 
@@ -336,7 +351,9 @@
     last_x, last_y = lax.axis_size("gx") - 1, lax.axis_size("gy") - 1
     inside = jnp.stack([gx > 0, gx < last_x, gy > 0, gy < last_y] * 2).astype(F32)
     flags = jnp.broadcast_to(inside[:, None], (8, 128))
-    odd = (obs_cell % 2).astype(F32)
+    odd = (obs_cell & 1).astype(F32)
+    obs_x, obs_y = obs_cell >> 6, obs_cell & (CY - 1)
+    obs_row = (obs_x & 56) * BLOCKS + (obs_y >> 1) * 8 + (obs_x & 7)
     val = jnp.concatenate([obs_value.reshape(2, 128), odd.reshape(2, 128)], axis=0)
     var = obs_var.reshape(2, 128)
     vmem, anywhere = pl.BlockSpec(memory_space=VMEM), pl.BlockSpec(memory_space=pl.ANY)
@@ -350,10 +367,10 @@
         out_shape=(arr(HALO, WIDTH + 128),) * 2,
         in_specs=[hbm, hbm],
         out_specs=(vmem, vmem),
-        scratch_shapes=[buf(8, WIDTH), buf(8, WIDTH), buf(CX, CY), pltpu.SemaphoreType.DMA((3,))],
+        scratch_shapes=[buf(16, CY), pltpu.SemaphoreType.DMA((4,))],
         compiler_params=params(4),
         name="rows",
-    )(latent, kappa)
+    )(*(pltpu.with_memory_space_constraint(a, pltpu.MemorySpace.HBM) for a in (latent, kappa)))
     xlo = lax.ppermute(to_hi, "gx", ring("gx", 1))
     xhi = lax.ppermute(to_lo, "gx", ring("gx", -1))
 
@@ -376,13 +393,14 @@
         out_shape=(arr(CX * BLOCKS, 128), arr(OBS, 128), arr(OBS, 128), arr(OBS, 128)),
         in_specs=[vmem] * 7,
         out_specs=(vmem,) * 4,
-        scratch_shapes=[buf(TALL, WIDTH)] * 4 + [buf(128, 128)],
+        scratch_shapes=[stencil_buf(BLOCKS)] * 4 + [buf(128, 128)],
         compiler_params=params(12),
         cost_estimate=cost(20_000_000, 12_000_000),
         name="inner",
     )(flags, latent, kappa, xlo, xhi, val, var)
 
     near = RIM * 128 - EDGE
+    obs_row = obs_row.astype(jnp.int32)
     whole_of = lambda a: part(a.shape, *([0] * a.ndim))
     operands = (kappa, xlo, xhi, ylo, yhi, value, weight, odd, tiles)
     tiles, stat = pl.pallas_call(
@@ -398,12 +416,13 @@
             vmem,
         ],
         out_specs=(vmem, part((STAT, 128), 0, 0)),
-        scratch_shapes=[pltpu.SMEM((OBS,), jnp.int32), pltpu.SemaphoreType.DMA((CX // 8 + 1,))]
-        + [buf(TALL, RIM * 128)] * 4
+        scratch_shapes=[pltpu.SMEM((OBS,), jnp.int32), pltpu.SemaphoreType.DMA]
+        + [stencil_buf(RIM)] * 4
         + [buf(128, 128), buf(OBS, 128)],
+        input_output_aliases={12: 0},
         compiler_params=params(12),
         name="rim",
-    )(flags, obs_cell, latent, latent, *operands)
+    )(flags, obs_row, latent, latent, *operands)
 
     stat = stat[:, None, :]
     for axis in ("gy", "gx"):

time: 58.1 us -> 54.7 us (0.941)
  Pallas kernels: 11.3 us -> 9.25 us
  local copies, waits for them, and re-layouts: 2.92 us -> 1.62 us
    pallas_call x1, Pallas kernels: 3.83 us -> 2.01 us  [per_device(): pl.pallas_call(rim_kernel, grid=(1,), out_shape=(arr(CX * BLOCKS, 128), a...]
    unnamed x14 -> x10, local copies, waits for them, and re-layouts: 2.6 us -> 1.3 us
    pallas_call x1, Pallas kernels: 2.83 us -> 2.14 us  [per_device(): pl.pallas_call(inner_kernel, out_shape=(arr(CX * BLOCKS, 128), arr(OBS, 1...]
    pallas_call x1, Pallas kernels: 0.4 us -> 1.03 us  [per_device(): pl.pallas_call(rows_kernel, out_shape=(arr(HALO, WIDTH + 128),) * 2, in_s...]
  transfers between devices with their start and end apart: 4 -> 4, of which waited for: 2 -> 2; matrix products, arithmetic and copies ran while one was open for 0% -> 0% of each run, Pallas kernels for 5% -> 4%
where the time goes in v3:
time: 54.7 us; the launch traced here: 54.5 us
  blocking collectives  31.1 us (57%)
  Pallas kernels  9.25 us (17%)
  starting transfers between devices  8.35 us (15%)
  waiting for transfers between devices  3.35 us (6%)
  local copies, waits for them, and re-layouts  1.62 us (3%)
  between operations  0.72 us (1%)
    all_to_all x2, blocking collectives, per_device(): lax.all_to_all(jnp.broadcast_to(stat[None], (count,) + stat.shape), axis,...  31.1 us
    pallas_call x1, Pallas kernels, per_device(): pl.pallas_call(update_kernel, out_shape=(arr(CX * BLOCKS, 128),) * 2, in_...  4 us
    ppermute x1, starting transfers between devices, per_device(): yhi = lax.ppermute(to_lo, 'gy', ring('gy', -1))  3.81 us
    ppermute x1, starting transfers between devices, per_device(): xlo = lax.ppermute(to_hi, 'gx', ring('gx', 1))  3.04 us
    ppermute x1, waiting for transfers between devices, per_device(): xhi = lax.ppermute(to_lo, 'gx', ring('gx', -1))  2.36 us
    pallas_call x1, Pallas kernels, per_device(): pl.pallas_call(inner_kernel, out_shape=(arr(CX * BLOCKS, 128), arr(OBS, 1...  2.14 us
    pallas_call x1, Pallas kernels, per_device(): pl.pallas_call(rim_kernel, grid=(1,), out_shape=(arr(CX * BLOCKS, 128), a...  2.01 us
    unnamed x10, local copies, waits for them, and re-layouts  1.3 us
  transfers between devices with their start and end apart: 4, of which 2 were waited for; matrix products, arithmetic and copies ran while one was open for 0% of the time, Pallas kernels for 4%

profile of v3, /device:TPU:1, one launch (start us, length us, event | category | flops | bytes accessed | tf_op | source)
XLA Modules:
  0.0 54.5 jit_solution(12043727294241490259)
XLA Ops:
  0.6 0.0 copy-start
  0.6 0.0 copy-start.3
  0.6 1.0 %rows.1 = (f32[4,4224]{1,0:T(4,128)S(1)}, f32[4,4224]{1,0:T(4,128)S(1)}) custom-call(f32[64,4096]{1,0:T(8,128)} %lat1.1, f32[64,64]{1,0:T(8,128)} %kap.5), custom_call_target="tpu_custom_call" | custom-call | tf_op jit(solution)/shard_map/rows/pallas_call | solution.py:365
  1.7 0.0 copy-start.1
  1.7 3.0 %collective-permute-start = (f32[4,4224]{1,0:T(4,128)S(1)}, f32[4,4224]{1,0:T(4,128)S(1)}, u32[]{:S(2)}, u32[]{:S(2)}) collective-permute-start(f32[4,4224]{1,0:T(4,128)S(1)} %get-tuple-element.14), channel_id=1, source_target_pairs={{0,16},{16,32},{32,48},{48,64},{64,80},{80,96},{96,112},{112,128},... | collective-permute-start | bytes 202760 | tf_op jit(solution)/shard_map/ppermute | solution.py:374
  4.7 0.2 collective-permute-start.1
  5.0 0.0 copy-done.3
  5.0 0.1 stack.23
  5.1 1.0 %collective-permute-done.xlo = f32[4,4224]{1,0:T(4,128)S(1)} collective-permute-done((f32[4,4224]{1,0:T(4,128)S(1)}, f32[4,4224]{1,0:T(4,128)S(1)}, u32[]{:S(2)}, u32[]{:S(2)}) %collective-permute-start) | collective-permute-done | bytes 67616 | tf_op jit(solution)/shard_map/ppermute | solution.py:374
  6.1 2.4 %collective-permute-done.1.xhi = f32[4,4224]{1,0:T(4,128)S(1)} collective-permute-done((f32[4,4224]{1,0:T(4,128)S(1)}, f32[4,4224]{1,0:T(4,128)S(1)}, u32[]{:S(2)}, u32[]{:S(2)}) %collective-permute-start.1) | collective-permute-done | bytes 67616 | tf_op jit(solution)/shard_map/ppermute | solution.py:375
  8.5 0.0 copy-done
  8.5 0.0 copy-done.1
  8.5 0.1 cols.1
  8.5 1.3 %collective-permute-start.2 = (f32[80,256]{1,0:T(8,128)S(1)}, f32[80,256]{1,0:T(8,128)S(1)}, u32[]{:S(2)}, u32[]{:S(2)}) collective-permute-start(f32[80,256]{1,0:T(8,128)S(1)} %get-tuple-element.16), channel_id=1, source_target_pairs={{0,1},{1,2},{2,3},{3,4},{4,5},{5,6},{6,7},{7,8},{8,9},{9,10},{10,1... | collective-permute-start | bytes 245768 | tf_op jit(solution)/shard_map/ppermute | solution.py:388
  9.8 3.8 %collective-permute-start.3 = (f32[80,256]{1,0:T(8,128)S(1)}, f32[80,256]{1,0:T(8,128)S(1)}, u32[]{:S(2)}, u32[]{:S(2)}) collective-permute-start(f32[80,256]{1,0:T(8,128)S(1)} %get-tuple-element.17), channel_id=1, source_target_pairs={{0,15},{1,0},{2,1},{3,2},{4,3},{5,4},{6,5},{7,6},{8,7},{9,8},{10,9... | collective-permute-start | bytes 245768 | tf_op jit(solution)/shard_map/ppermute | solution.py:389
  13.6 0.0 copy-start.4
  13.6 0.7 %copy-done.4 = f32[256]{0:T(256)S(1)} copy-done((f32[256]{0:T(256)S(1)}, f32[256]{0:T(256)}, u32[]{:S(2)}) %copy-start.4) | copy-done | bytes 1048
  14.3 0.0 copy-start.2
  14.3 0.1 broadcast_in_dim.6.flags
  14.4 0.6 %copy-done.2 = f32[256]{0:T(256)S(1)} copy-done((f32[256]{0:T(256)S(1)}, f32[256]{0:T(256)}, u32[]{:S(2)}) %copy-start.2) | copy-done | bytes 1048
  15.0 2.1 %inner.1 = (f32[2048,128]{1,0:T(8,128)S(1)}, f32[256,128]{1,0:T(8,128)S(1)}, f32[256,128]{1,0:T(8,128)S(1)}, f32[256,128]{1,0:T(8,128)S(1)}) custom-call(f32[8,128]{1,0:T(8,128)S(1)} %broadcast_in_dim.6.flags, f32[64,4096]{1,0:T(8,128)S(1)} %copy-done, f32[64,64]{1,0:T(8,128)S(1)} %copy-done.1, f32[4,4224]{1,0:T(4,128)S(1)} %collective-permute-done.xlo, ...), custom_call_target="tpu_custom_call" | custom-call | flops 20000000 | bytes 12000000 | tf_op jit(solution)/shard_map/inner/pallas_call | solution.py:391
  17.1 0.0 collective-permute-done.2.ylo
  17.1 0.0 collective-permute-done.3.yhi
  17.1 2.0 %rim.1 = (f32[2048,128]{1,0:T(8,128)S(1)}, f32[17,128]{1,0:T(8,128)S(1)}) custom-call(f32[8,128]{1,0:T(8,128)S(1)} %broadcast_in_dim.6.flags, s32[256]{0:T(256)S(1)} %get-tuple-element.27.cell_vmem, f32[64,4096]{1,0:T(8,128)S(1)} %copy-done, f32[64,4096]{1,0:T(8,128)S(1)} %copy-done, f32[64,64]{1,0:T(8,128)S(1)} %copy-done.1, ...), custom_call_target="tpu_custom_call", output_to_operand_aliasing={{0}: (12, {})} | custom-call | tf_op jit(solution)/shard_map/rim/pallas_call | solution.py:406
  19.2 0.1 broadcast_in_dim.7
  19.2 11.1 %all_to_all.10 = f32[16,17,1,128]{3,2,1,0:T(1,128)S(1)} all-to-all(f32[16,17,1,128]{3,2,1,0:T(1,128)S(1)} %broadcast_in_dim.7), channel_id=1, replica_groups=mesh['gx'=16,'gy'=16] {'gy'}, dimensions={0} | all-to-all | bytes 278528 | tf_op jit(solution)/shard_map/all_to_all | solution.py:430
  30.4 0.1 reduce_sum.9
  30.5 0.1 broadcast_in_dim.8
  30.6 20.0 %all_to_all.11.parts = f32[16,17,1,128]{3,2,1,0:T(1,128)S(1)} all-to-all(f32[16,17,1,128]{3,2,1,0:T(1,128)S(1)} %broadcast_in_dim.8), channel_id=1, replica_groups=mesh['gx'=16,'gy'=16] {'gx'}, dimensions={0} | all-to-all | bytes 278528 | tf_op jit(solution)/shard_map/all_to_all | solution.py:430
  50.5 4.0 %update.1 = (f32[2048,128]{1,0:T(8,128)}, f32[2048,128]{1,0:T(8,128)}) custom-call(f32[16,17,1,128]{3,2,1,0:T(1,128)S(1)} %all_to_all.11.parts, f32[2048,128]{1,0:T(8,128)S(1)} %bitcast.23, f32[2048,128]{1,0:T(8,128)S(1)} %get-tuple-element.23.tiles), custom_call_target="tpu_custom_call" | custom-call | tf_op jit(solution)/shard_map/update/pallas_call | solution.py:434
  (3 shorter events, 0.0 us)
Async XLA Ops:
  0.6 7.8 %copy-start = (f32[64,4096]{1,0:T(8,128)S(1)}, f32[64,4096]{1,0:T(8,128)}, u32[]{:S(2)}) copy-start(f32[64,4096]{1,0:T(8,128)} %lat1.1) | copy-start | bytes 3145732
  0.6 4.3 %copy-start.3 = (s32[256]{0:T(256)S(1)}, s32[256]{0:T(256)}, u32[]{:S(2)}) copy-start(s32[256]{0:T(256)} %param.7) | copy-start | bytes 3076
  1.7 6.8 %copy-start.1 = (f32[64,64]{1,0:T(8,128)S(1)}, f32[64,64]{1,0:T(8,128)}, u32[]{:S(2)}) copy-start(f32[64,64]{1,0:T(8,128)} %kap.5) | copy-start | bytes 49156
  1.7 4.4 %collective-permute-start = (f32[4,4224]{1,0:T(4,128)S(1)}, f32[4,4224]{1,0:T(4,128)S(1)}, u32[]{:S(2)}, u32[]{:S(2)}) collective-permute-start(f32[4,4224]{1,0:T(4,128)S(1)} %get-tuple-element.14), channel_id=1, source_target_pairs={{0,16},{16,32},{32,48},{48,64},{64,80},{80,96},{96,112},{112,128},... | collective-permute-start | bytes 202760 | tf_op jit(solution)/shard_map/ppermute | solution.py:374
  4.7 3.7 %collective-permute-start.1 = (f32[4,4224]{1,0:T(4,128)S(1)}, f32[4,4224]{1,0:T(4,128)S(1)}, u32[]{:S(2)}, u32[]{:S(2)}) collective-permute-start(f32[4,4224]{1,0:T(4,128)S(1)} %get-tuple-element.15), channel_id=1, source_target_pairs={{0,240},{16,0},{32,16},{48,32},{64,48},{80,64},{96,80},{112,96},{1... | collective-permute-start | bytes 202760 | tf_op jit(solution)/shard_map/ppermute | solution.py:375
  8.5 8.6 %collective-permute-start.2 = (f32[80,256]{1,0:T(8,128)S(1)}, f32[80,256]{1,0:T(8,128)S(1)}, u32[]{:S(2)}, u32[]{:S(2)}) collective-permute-start(f32[80,256]{1,0:T(8,128)S(1)} %get-tuple-element.16), channel_id=1, source_target_pairs={{0,1},{1,2},{2,3},{3,4},{4,5},{5,6},{6,7},{7,8},{8,9},{9,10},{10,1... | collective-permute-start | bytes 245768 | tf_op jit(solution)/shard_map/ppermute | solution.py:388
  9.8 7.3 %collective-permute-start.3 = (f32[80,256]{1,0:T(8,128)S(1)}, f32[80,256]{1,0:T(8,128)S(1)}, u32[]{:S(2)}, u32[]{:S(2)}) collective-permute-start(f32[80,256]{1,0:T(8,128)S(1)} %get-tuple-element.17), channel_id=1, source_target_pairs={{0,15},{1,0},{2,1},{3,2},{4,3},{5,4},{6,5},{7,6},{8,7},{9,8},{10,9... | collective-permute-start | bytes 245768 | tf_op jit(solution)/shard_map/ppermute | solution.py:389
  13.6 0.7 %copy-start.4 = (f32[256]{0:T(256)S(1)}, f32[256]{0:T(256)}, u32[]{:S(2)}) copy-start(f32[256]{0:T(256)} %param.8) | copy-start | bytes 3076
  14.3 0.7 %copy-start.2 = (f32[256]{0:T(256)S(1)}, f32[256]{0:T(256)}, u32[]{:S(2)}) copy-start(f32[256]{0:T(256)} %param.9) | copy-start | bytes 3076

commit v4 on v3

--- a/solution.py
+++ b/solution.py
@@ -18,7 +18,6 @@
 WIDTH = CY * MEMBERS
 BLOCKS = WIDTH // 128
 EDGE = HALO * MEMBERS
-RIM = 6
 STAT = 17
 HALF = MEMBERS // 2
 VMEM = pltpu.MemorySpace.VMEM
@@ -56,24 +55,22 @@
     return slice(at, at + count)
 
 
-def sweep(src, xi, alpha, blocks, first, last, coeff, scale, store, tiles=(0, TALL)):
-    at, count = tiles[0], tiles[1] - tiles[0]
+def sweep(get, xi, alpha, order, coeff, scale, store, at=0, count=TALL):
     low_half = lax.broadcasted_iota(jnp.int32, (count, 128), 1) < MEMBERS
+    turned = {}
 
     def turn(c):
-        return pltpu.roll(src[rows_of(min(max(c, 0), blocks - 1), at, count), :], 64, 1)
-
-    before, here = turn(first - 1), turn(first)
-    for c in range(first, last + 1):
-        after = turn(c + 1)
-        here_rows = rows_of(c, at, count)
-        beside = here + jnp.where(low_half, before, after)
-        beside = beside + (src[rows_of(c, at - 1, count), :] + src[rows_of(c, at + 1, count), :])
-        applied = alpha[here_rows, :] * src[here_rows, :] - beside
+        if c not in turned:
+            turned[c] = pltpu.roll(get(c, at), 64, 1)
+        return turned[c]
+
+    for c, lower, upper in order:
+        beside = turn(c) + jnp.where(low_half, turn(lower), turn(upper))
+        beside = beside + (get(c, at - 1) + get(c, at + 1))
+        applied = alpha(c) * get(c, at) - beside
         if scale != 1.0:
             applied = applied * scale
-        store(c, coeff * xi[here_rows, :] + applied)
-        before, here = here, after
+        store(c, coeff * xi(c) + applied)
 
 
 def spread_kappa(alpha, shifted, count, start):
@@ -143,16 +140,23 @@
     ext[rows_of(c, 12 + CX, 4), :] = zero4
 
 
-def inner_kernel(flags, lat, kap, xlo, xhi, val, var, tiles, value, weight, odd, ext, alpha, ua, ub, kext):
+def inner_kernel(flags, lat, kap, xlo, xhi, val, var, tiles, value, weight, odd, ext, alpha, u3, u2, u1, kext):
     for c in range(BLOCKS):
         fill(ext, c, lat[:, lanes(c)], xlo[:, lanes(c)], xhi[:, lanes(c)], flags[0:1, :], flags[1:2, :])
     kappa_rows(kext, kap, xlo, xhi)
     spread_kappa(alpha, kext[0:TALL, :] - CENTRE, BLOCKS, 0)
-    top, inside = BLOCKS - 1, (8, 8 + CX)
-    sweep(ext, ext, alpha, BLOCKS, 0, top, COEFFS[3], COEFFS[4], keep_rows(ua, flags))
-    sweep(ua, ext, alpha, BLOCKS, 1, top - 1, COEFFS[2], 1.0, keep_rows(ub, flags))
-    sweep(ub, ext, alpha, BLOCKS, 1, top - 1, COEFFS[1], 1.0, keep_rows(ua, flags))
-    sweep(ua, ext, alpha, BLOCKS, 2, top - 2, COEFFS[0], 1.0, lambda c, new: into_tiles(tiles, c, new), inside)
+
+    def run(src, depth, step, scale, store, at=0, count=TALL):
+        order = [(c, max(c - 1, 0), min(c + 1, BLOCKS - 1)) for c in range(depth, BLOCKS - depth)]
+        get = lambda c, shift: src[rows_of(c, shift, count), :]
+        xi = lambda c: ext[rows_of(c, at, count), :]
+        diag = lambda c: alpha[rows_of(c, at, count), :]
+        sweep(get, xi, diag, order, COEFFS[step], scale, store, at, count)
+
+    run(ext, 0, 3, COEFFS[4], keep_rows(u3, flags))
+    run(u3, 1, 2, 1.0, keep_rows(u2, flags))
+    run(u2, 1, 1, 1.0, keep_rows(u1, flags))
+    run(u1, 2, 0, 1.0, lambda c, new: into_tiles(tiles, c, new), 8, CX)
 
     def column(row):
         pieces = [jnp.transpose(jnp.broadcast_to(row[i : i + 1, :], (128, 128))) for i in range(OBS // 128)]
@@ -164,44 +168,47 @@
 
 
 def rim_kernel(
-    flags, cell_vmem, lat0, lat1, kap, xlo, xhi, ylo, yhi, value, weight, odd, held,
-    tiles, stat, cell, sem, ext, alpha, ua, ub, kext, pbuf,
+    flags, cell_vmem, ylo, yhi, value, weight, odd, ext, alpha, u3, u2, u1, held,
+    tiles, stat, cell, sem, ext_out, alpha_out, v3, v2, v1, kext, pbuf,
 ):
     fetch = pltpu.make_async_copy(cell_vmem, cell, sem)
     fetch.start()
-    kappa_rows(kext, kap, xlo, xhi)
-    own = jnp.transpose(kext[...])
-    near = RIM - 2
-    for side, (lat, msg) in enumerate(((lat0, ylo), (lat1, yhi))):
+    low, high = flags[0:1, :], flags[1:2, :]
+    kext[...] = jnp.zeros((128, 128), F32)
+    for side, msg in enumerate((ylo, yhi)):
         flag = flags[2 + side : 3 + side, :]
-        low, high = flags[0:1, :], flags[1:2, :]
-        for i in range(near):
-            at = lanes(i if side == 0 else BLOCKS - near + i)
-            fill(ext, i + 2 if side == 0 else i, lat[:, lanes(i)], xlo[:, at], xhi[:, at], low, high)
-        for i in range(2):
-            body = msg[0:CX, lanes(i)] * flag
+        kext[0:4, :] = msg[CX + 8 : CX + 12, 0:128]
+        shifted = jnp.transpose(kext[...])[0:TALL, :] - CENTRE
+        upper = (lax.broadcasted_iota(jnp.int32, (TALL, 128), 1) >= MEMBERS).astype(jnp.int32)
+        for p in (-2, -1):
+            i = p + 2 if side == 0 else -1 - p
             halo = msg[CX : CX + 4, lanes(i)], msg[CX + 4 : CX + 8, lanes(i)]
-            fill(ext, i if side == 0 else near + i, body, *halo, low * flag, high * flag)
-        if side == 0:
-            kext[0:4, :] = msg[CX + 8 : CX + 12, 0:128]
-            kext[4:16, :] = own[0:12, :]
-        else:
-            kext[0:8, :] = own[CY - 8 : CY, :]
-            kext[8:12, :] = msg[CX + 8 : CX + 12, 0:128]
-        spread_kappa(alpha, jnp.transpose(kext[...])[0:TALL, :] - CENTRE, RIM, 0)
+            fill(ext_out, p + 2, msg[0:CX, lanes(i)] * flag, *halo, low * flag, high * flag)
+            alpha_out[rows_of(p + 2), :] = jnp.take_along_axis(shifted, upper + 2 * i, axis=1)
+
+        def local(p):
+            return p if side == 0 else BLOCKS - 1 - p
+
+        def run(near, far, mine, first, last, step, scale, store, at=0, count=TALL):
+            def pick(p, here, there, ours, start):
+                return here[rows_of(p + 2, start, count), :] if p in ours else there[rows_of(local(p), start, count), :]
+
+            get = lambda p, shift: pick(p, near, far, mine, shift)
+            xi = lambda p: pick(p, ext_out, ext, (-2, -1), at)
+            diag = lambda p: pick(p, alpha_out, alpha, (-2, -1), at)
+            order = [(p, max(p - 1, -2), p + 1) for p in range(first, last + 1)]
+            if side == 1:
+                order = [(p, b, a) for p, a, b in order]
+            sweep(get, xi, diag, order, COEFFS[step], scale, store, at, count)
 
         def keep(dst):
             plain = keep_rows(dst, flags)
-            outside = (0, 1) if side == 0 else (RIM - 2, RIM - 1)
-            return lambda c, new: plain(c, new * flag if c in outside else new)
-
-        def finish(c, new):
-            into_tiles(tiles, c - 2 if side == 0 else c + BLOCKS - RIM + 2, new)
-
-        sweep(ext, ext, alpha, RIM, 0, RIM - 1, COEFFS[3], COEFFS[4], keep(ua))
-        sweep(ua, ext, alpha, RIM, 1, RIM - 2, COEFFS[2], 1.0, keep(ub))
-        sweep(ub, ext, alpha, RIM, 1, RIM - 2, COEFFS[1], 1.0, keep(ua))
-        sweep(ua, ext, alpha, RIM, 2, RIM - 3, COEFFS[0], 1.0, finish, (8, 8 + CX))
+            return lambda p, new: plain(p + 2, new * flag if p < 0 else new)
+
+        run(ext_out, ext, (-2, -1), -2, 0, 3, COEFFS[4], keep(v3))
+        run(v3, u3, (-2, -1, 0), -1, 0, 2, 1.0, keep(v2))
+        run(v2, u2, (-2, -1, 0), -1, 1, 1, 1.0, keep(v1))
+        run(v1, u1, (-2, -1, 0, 1), 0, 1, 0, 1.0, lambda p, new: into_tiles(tiles, local(p), new), 8, CX)
 
     fetch.wait()
     for j in range(OBS):
@@ -261,9 +268,14 @@
     return aug
 
 
-def update_kernel(parts, lat, tiles, out_hbm, prior_hbm, total, out, sems):
-    copies = [pltpu.make_async_copy(tiles, prior_hbm, sems.at[CX // 8])]
-    copies[0].start()
+def split(a):
+    hi = a.astype(jnp.bfloat16)
+    return hi, (a - hi.astype(F32)).astype(jnp.bfloat16)
+
+
+def solve_kernel(parts, tiles, weights_out, prior_hbm, total, sem):
+    copy = pltpu.make_async_copy(tiles, prior_hbm, sem)
+    copy.start()
     for i in range(STAT):
         row = parts[0, i]
         for d in range(1, parts.shape[0]):
@@ -298,19 +310,22 @@
         [jnp.where(low, pltpu.roll(gain, 64, 1), 0.0), jnp.where(low, 0.0, gain)], axis=0
     )
 
-    def split(a):
-        hi = a.astype(jnp.bfloat16)
-        return hi, (a - hi.astype(F32)).astype(jnp.bfloat16)
-
-    def dot(a, b):
-        return jnp.dot(a, b, preferred_element_type=F32)
-
     w_hi, w_lo = split(weights)
+    weights_out[0:128, 0:128] = w_hi
+    weights_out[0:128, 128:256] = w_lo
+    weights_out[128:256, 0:128] = w_hi
+    weights_out[128:256, 128:256] = jnp.zeros((128, 128), jnp.bfloat16)
+    copy.wait()
+
+
+def update_kernel(lat, weights, out_hbm, out, sems):
+    both = weights[...]
+    copies = []
     for t in range(CX // 8):
         at = slice(t * 256, (t + 1) * 256)
         x = lat[at, :]
-        x_hi, x_lo = split(x)
-        out[at, :] = x + ((dot(x_lo, w_hi) + dot(x_hi, w_lo)) + dot(x_hi, w_hi))
+        product = jnp.dot(jnp.concatenate(split(x), axis=1), both, preferred_element_type=F32)
+        out[at, :] = x + (product[:, 0:128] + product[:, 128:256])
         copies.append(pltpu.make_async_copy(out.at[at, :], out_hbm.at[at, :], sems.at[t]))
         copies[-1].start()
     for copy in copies:
@@ -388,41 +403,30 @@
     ylo = lax.ppermute(to_hi, "gy", ring("gy", 1))
     yhi = lax.ppermute(to_lo, "gy", ring("gy", -1))
 
-    tiles, value, weight, odd = pl.pallas_call(
+    field = arr(BLOCKS * TALL + 2 * PAD, 128)
+    tiles, *rest = pl.pallas_call(
         inner_kernel,
-        out_shape=(arr(CX * BLOCKS, 128), arr(OBS, 128), arr(OBS, 128), arr(OBS, 128)),
+        out_shape=(arr(CX * BLOCKS, 128),) + (arr(OBS, 128),) * 3 + (field,) * 5,
         in_specs=[vmem] * 7,
-        out_specs=(vmem,) * 4,
-        scratch_shapes=[stencil_buf(BLOCKS)] * 4 + [buf(128, 128)],
+        out_specs=(vmem,) * 9,
+        scratch_shapes=[buf(128, 128)],
         compiler_params=params(12),
         cost_estimate=cost(20_000_000, 12_000_000),
         name="inner",
     )(flags, latent, kappa, xlo, xhi, val, var)
 
-    near = RIM * 128 - EDGE
-    obs_row = obs_row.astype(jnp.int32)
-    whole_of = lambda a: part(a.shape, *([0] * a.ndim))
-    operands = (kappa, xlo, xhi, ylo, yhi, value, weight, odd, tiles)
     tiles, stat = pl.pallas_call(
         rim_kernel,
-        grid=(1,),
         out_shape=(arr(CX * BLOCKS, 128), arr(STAT, 128)),
-        in_specs=[
-            whole_of(flags),
-            anywhere,
-            part((CX, near), 0, 0),
-            part((CX, near), 0, WIDTH // near - 1),
-            *(whole_of(a) for a in operands[:-1]),
-            vmem,
-        ],
-        out_specs=(vmem, part((STAT, 128), 0, 0)),
+        in_specs=[vmem, anywhere] + [vmem] * 11,
+        out_specs=(vmem, vmem),
         scratch_shapes=[pltpu.SMEM((OBS,), jnp.int32), pltpu.SemaphoreType.DMA]
-        + [stencil_buf(RIM)] * 4
+        + [stencil_buf(4)] * 5
         + [buf(128, 128), buf(OBS, 128)],
         input_output_aliases={12: 0},
         compiler_params=params(12),
         name="rim",
-    )(flags, obs_row, latent, latent, *operands)
+    )(flags, obs_row, ylo, yhi, *rest, tiles)
 
     stat = stat[:, None, :]
     for axis in ("gy", "gx"):
@@ -431,15 +435,24 @@
         if axis == "gy":
             stat = jnp.sum(parts, axis=0)
 
-    latent_new, prior = pl.pallas_call(
+    weights, prior = pl.pallas_call(
+        solve_kernel,
+        out_shape=(jax.ShapeDtypeStruct((256, 256), jnp.bfloat16), arr(CX * BLOCKS, 128)),
+        in_specs=[vmem] * 2,
+        out_specs=(vmem, anywhere),
+        scratch_shapes=[buf(24, 128), pltpu.SemaphoreType.DMA],
+        compiler_params=params(12),
+        name="solve",
+    )(parts, tiles)
+    latent_new = pl.pallas_call(
         update_kernel,
-        out_shape=(arr(CX * BLOCKS, 128),) * 2,
-        in_specs=[vmem] * 3,
-        out_specs=(anywhere,) * 2,
-        scratch_shapes=[buf(24, 128), buf(CX * BLOCKS, 128), pltpu.SemaphoreType.DMA((CX // 8 + 1,))],
+        out_shape=arr(CX * BLOCKS, 128),
+        in_specs=[vmem] * 2,
+        out_specs=anywhere,
+        scratch_shapes=[buf(CX * BLOCKS, 128), pltpu.SemaphoreType.DMA((CX // 8,))],
         compiler_params=params(12),
         name="update",
-    )(parts, to_tiles(latent), tiles)
+    )(to_tiles(latent), weights)
     return (from_tiles(latent_new), from_tiles(prior))
 
 

time: 54.7 us -> 54.2 us (level)
  other arithmetic: 0.11 us -> 0.79 us
  waiting for transfers between devices: 3.35 us -> 2.68 us
    reshape x1, other arithmetic: 0.01 us -> 0.68 us  [per_device(): odd.reshape(2, 128)]
    ppermute x1, waiting for transfers between devices: 0.99 us -> 0.31 us  [per_device(): xlo = lax.ppermute(to_hi, 'gx', ring('gx', 1))]
    pallas_call x3 -> x4, Pallas kernels: 8.15 us -> 7.63 us  [the longest x1 2.95 us: per_device(): pl.pallas_call(inner_kernel, out_shape=(arr(CX * BLOCKS, 128),) + (arr(OB...]
  transfers between devices with their start and end apart: 4 -> 4, of which waited for: 2 -> 2; matrix products, arithmetic and copies ran while one was open for 0% -> 2% of each run, Pallas kernels for 4% -> 5%
where the time goes in v4:
time: 54.2 us; the launch traced here: 54 us
  blocking collectives  31.6 us (58%)
  Pallas kernels  8.73 us (16%)
  starting transfers between devices  8.35 us (15%)
  waiting for transfers between devices  2.68 us (5%)
  local copies, waits for them, and re-layouts  1.1 us (2%)
  other arithmetic  0.79 us (1%)
  between operations  0.74 us (1%)
    all_to_all x2, blocking collectives, per_device(): lax.all_to_all(jnp.broadcast_to(stat[None], (count,) + stat.shape), axis,...  31.6 us
    ppermute x1, starting transfers between devices, per_device(): yhi = lax.ppermute(to_lo, 'gy', ring('gy', -1))  3.81 us
    ppermute x1, starting transfers between devices, per_device(): xlo = lax.ppermute(to_hi, 'gx', ring('gx', 1))  3.04 us
    pallas_call x1, Pallas kernels, per_device(): pl.pallas_call(inner_kernel, out_shape=(arr(CX * BLOCKS, 128),) + (arr(OB...  2.95 us
    ppermute x1, waiting for transfers between devices, per_device(): xhi = lax.ppermute(to_lo, 'gx', ring('gx', -1))  2.36 us
    pallas_call x1, Pallas kernels, per_device(): pl.pallas_call(solve_kernel, out_shape=(jax.ShapeDtypeStruct((256, 256),...  1.82 us
    pallas_call x1, Pallas kernels, per_device(): pl.pallas_call(rim_kernel, out_shape=(arr(CX * BLOCKS, 128), arr(STAT, 12...  1.58 us
    pallas_call x1, Pallas kernels, per_device(): pl.pallas_call(update_kernel, out_shape=arr(CX * BLOCKS, 128), in_specs=[...  1.28 us
  transfers between devices with their start and end apart: 4, of which 2 were waited for; matrix products, arithmetic and copies ran while one was open for 2% of the time, Pallas kernels for 5%

profile of v4, /device:TPU:1, one launch (start us, length us, event | category | flops | bytes accessed | tf_op | source)
XLA Modules:
  0.0 54.0 jit_solution(1369479950416302703)
XLA Ops:
  0.6 0.0 copy-start
  0.6 1.0 %rows.1 = (f32[4,4224]{1,0:T(4,128)S(1)}, f32[4,4224]{1,0:T(4,128)S(1)}) custom-call(f32[64,4096]{1,0:T(8,128)} %lat.1, f32[64,64]{1,0:T(8,128)} %kap.3), custom_call_target="tpu_custom_call" | custom-call | tf_op jit(solution)/shard_map/rows/pallas_call | solution.py:380
  1.7 0.0 copy-start.4
  1.7 0.0 copy-start.2
  1.7 0.0 copy-start.3
  1.7 3.0 %collective-permute-start = (f32[4,4224]{1,0:T(4,128)S(1)}, f32[4,4224]{1,0:T(4,128)S(1)}, u32[]{:S(2)}, u32[]{:S(2)}) collective-permute-start(f32[4,4224]{1,0:T(4,128)S(1)} %get-tuple-element.19), channel_id=1, source_target_pairs={{0,16},{16,32},{32,48},{48,64},{64,80},{80,96},{96,112},{112,128},... | collective-permute-start | bytes 202760 | tf_op jit(solution)/shard_map/ppermute | solution.py:389
  4.8 0.2 collective-permute-start.1
  5.0 0.7 %convert_bitcast_fusion = (f32[2,128]{1,0:T(2,128)S(1)}, s32[256]{0:T(256)S(1)}) fusion(s32[256]{0:T(256)} %param.7), kind=kLoop, calls=%fused_computation.1 | loop fusion | flops 2816 | bytes 3072 | tf_op jit(solution)/shard_map/reshape | solution.py:372
  5.7 0.1 stack.23
  5.8 0.3 collective-permute-done.xlo
  6.1 2.4 %collective-permute-done.1.xhi = f32[4,4224]{1,0:T(4,128)S(1)} collective-permute-done((f32[4,4224]{1,0:T(4,128)S(1)}, f32[4,4224]{1,0:T(4,128)S(1)}, u32[]{:S(2)}, u32[]{:S(2)}) %collective-permute-start.1) | collective-permute-done | bytes 67616 | tf_op jit(solution)/shard_map/ppermute | solution.py:390
  8.5 0.0 copy-done
  8.5 0.0 copy-start.1
  8.5 0.8 %copy-done.1 = f32[64,64]{1,0:T(8,128)S(1)} copy-done((f32[64,64]{1,0:T(8,128)S(1)}, f32[64,64]{1,0:T(8,128)}, u32[]{:S(2)}) %copy-start.1) | copy-done | bytes 16408
  9.2 0.1 cols.1
  9.3 1.3 %collective-permute-start.2 = (f32[80,256]{1,0:T(8,128)S(1)}, f32[80,256]{1,0:T(8,128)S(1)}, u32[]{:S(2)}, u32[]{:S(2)}) collective-permute-start(f32[80,256]{1,0:T(8,128)S(1)} %get-tuple-element.21), channel_id=1, source_target_pairs={{0,1},{1,2},{2,3},{3,4},{4,5},{5,6},{6,7},{7,8},{8,9},{9,10},{10,1... | collective-permute-start | bytes 245768 | tf_op jit(solution)/shard_map/ppermute | solution.py:403
  10.6 3.8 %collective-permute-start.3 = (f32[80,256]{1,0:T(8,128)S(1)}, f32[80,256]{1,0:T(8,128)S(1)}, u32[]{:S(2)}, u32[]{:S(2)}) collective-permute-start(f32[80,256]{1,0:T(8,128)S(1)} %get-tuple-element.22), channel_id=1, source_target_pairs={{0,15},{1,0},{2,1},{3,2},{4,3},{5,4},{6,5},{7,6},{8,7},{9,8},{10,9... | collective-permute-start | bytes 245768 | tf_op jit(solution)/shard_map/ppermute | solution.py:404
  14.4 0.0 copy-done.4
  14.4 0.1 broadcast_in_dim.6.flags
  14.5 0.0 copy-done.2
  14.5 0.0 copy-done.3
  14.5 3.0 %inner.1 = (f32[2048,128]{1,0:T(8,128)S(1)}, f32[256,128]{1,0:T(8,128)S(1)}, f32[256,128]{1,0:T(8,128)S(1)}, f32[256,128]{1,0:T(8,128)S(1)}, f32[2576,128]{1,0:T...) custom-call(f32[8,128]{1,0:T(8,128)S(1)} %broadcast_in_dim.6.flags, ...), custom_call_target="tpu_custom_call" | custom-call | flops 20000000 | bytes 12000000 | tf_op jit(solution)/shard_map/inner/pallas_call | solution.py:407
  17.4 0.0 collective-permute-done.2.ylo
  17.4 0.0 collective-permute-done.3.yhi
  17.4 1.6 %rim.1 = (f32[2048,128]{1,0:T(8,128)S(1)}, f32[17,128]{1,0:T(8,128)S(1)}) custom-call(f32[8,128]{1,0:T(8,128)S(1)} %broadcast_in_dim.6.flags, s32[256]{0:T(256)S(1)} %get-tuple-element.37.cell_vmem, f32[80,256]{1,0:T(8,128)S(1)} %collective-permute-done.2.ylo, f32[80,256]{1,0:T(8,128)S(1)} %collective-permute-done.3.yhi, ...), custom_call_target="tpu_custom_call", output_to_operand_aliasing={{0}: (12, {})} | custom-call | tf_op jit(solution)/shard_map/rim/pallas_call | solution.py:418
  19.0 0.1 broadcast_in_dim.7
  19.1 11.6 %all_to_all.10 = f32[16,17,1,128]{3,2,1,0:T(1,128)S(1)} all-to-all(f32[16,17,1,128]{3,2,1,0:T(1,128)S(1)} %broadcast_in_dim.7), channel_id=1, replica_groups=mesh['gx'=16,'gy'=16] {'gy'}, dimensions={0} | all-to-all | bytes 278528 | tf_op jit(solution)/shard_map/all_to_all | solution.py:434
  30.7 0.1 reduce_sum.9
  30.8 0.1 broadcast_in_dim.8
  30.9 20.0 %all_to_all.11.parts = f32[16,17,1,128]{3,2,1,0:T(1,128)S(1)} all-to-all(f32[16,17,1,128]{3,2,1,0:T(1,128)S(1)} %broadcast_in_dim.8), channel_id=1, replica_groups=mesh['gx'=16,'gy'=16] {'gx'}, dimensions={0} | all-to-all | bytes 278528 | tf_op jit(solution)/shard_map/all_to_all | solution.py:434
  50.8 1.8 %solve.1 = (bf16[256,256]{1,0:T(8,128)(2,1)S(1)}, f32[2048,128]{1,0:T(8,128)}) custom-call(f32[16,17,1,128]{3,2,1,0:T(1,128)S(1)} %all_to_all.11.parts, f32[2048,128]{1,0:T(8,128)S(1)} %get-tuple-element.33.tiles), custom_call_target="tpu_custom_call" | custom-call | tf_op jit(solution)/shard_map/solve/pallas_call | solution.py:438
  52.7 1.3 %update.1 = f32[2048,128]{1,0:T(8,128)} custom-call(f32[2048,128]{1,0:T(8,128)S(1)} %bitcast.23, bf16[256,256]{1,0:T(8,128)(2,1)S(1)} %get-tuple-element.34.weights), custom_call_target="tpu_custom_call" | custom-call | tf_op jit(solution)/shard_map/update/pallas_call | solution.py:447
  (2 shorter events, 0.0 us)
Async XLA Ops:
  0.6 7.8 %copy-start = (f32[64,4096]{1,0:T(8,128)S(1)}, f32[64,4096]{1,0:T(8,128)}, u32[]{:S(2)}) copy-start(f32[64,4096]{1,0:T(8,128)} %lat.1) | copy-start | bytes 3145732
  1.7 12.7 %copy-start.4 = (f32[256]{0:T(256)S(1)}, f32[256]{0:T(256)}, u32[]{:S(2)}) copy-start(f32[256]{0:T(256)} %param.8) | copy-start | bytes 3076
  1.7 12.8 %copy-start.2 = (f32[64,64]{1,0:T(8,128)S(1)}, f32[64,64]{1,0:T(8,128)}, u32[]{:S(2)}) copy-start(f32[64,64]{1,0:T(8,128)} %kap.3) | copy-start | bytes 49156
  1.7 12.8 %copy-start.3 = (f32[256]{0:T(256)S(1)}, f32[256]{0:T(256)}, u32[]{:S(2)}) copy-start(f32[256]{0:T(256)} %param.9) | copy-start | bytes 3076
  1.7 4.4 %collective-permute-start = (f32[4,4224]{1,0:T(4,128)S(1)}, f32[4,4224]{1,0:T(4,128)S(1)}, u32[]{:S(2)}, u32[]{:S(2)}) collective-permute-start(f32[4,4224]{1,0:T(4,128)S(1)} %get-tuple-element.19), channel_id=1, source_target_pairs={{0,16},{16,32},{32,48},{48,64},{64,80},{80,96},{96,112},{112,128},... | collective-permute-start | bytes 202760 | tf_op jit(solution)/shard_map/ppermute | solution.py:389
  4.8 3.7 %collective-permute-start.1 = (f32[4,4224]{1,0:T(4,128)S(1)}, f32[4,4224]{1,0:T(4,128)S(1)}, u32[]{:S(2)}, u32[]{:S(2)}) collective-permute-start(f32[4,4224]{1,0:T(4,128)S(1)} %get-tuple-element.20), channel_id=1, source_target_pairs={{0,240},{16,0},{32,16},{48,32},{64,48},{80,64},{96,80},{112,96},{1... | collective-permute-start | bytes 202760 | tf_op jit(solution)/shard_map/ppermute | solution.py:390
  8.5 0.8 %copy-start.1 = (f32[64,64]{1,0:T(8,128)S(1)}, f32[64,64]{1,0:T(8,128)}, u32[]{:S(2)}) copy-start(f32[64,64]{1,0:T(8,128)} %kap.3) | copy-start | bytes 49156
  9.3 8.1 %collective-permute-start.2 = (f32[80,256]{1,0:T(8,128)S(1)}, f32[80,256]{1,0:T(8,128)S(1)}, u32[]{:S(2)}, u32[]{:S(2)}) collective-permute-start(f32[80,256]{1,0:T(8,128)S(1)} %get-tuple-element.21), channel_id=1, source_target_pairs={{0,1},{1,2},{2,3},{3,4},{4,5},{5,6},{6,7},{7,8},{8,9},{9,10},{10,1... | collective-permute-start | bytes 245768 | tf_op jit(solution)/shard_map/ppermute | solution.py:403
  10.6 6.9 %collective-permute-start.3 = (f32[80,256]{1,0:T(8,128)S(1)}, f32[80,256]{1,0:T(8,128)S(1)}, u32[]{:S(2)}, u32[]{:S(2)}) collective-permute-start(f32[80,256]{1,0:T(8,128)S(1)} %get-tuple-element.22), channel_id=1, source_target_pairs={{0,15},{1,0},{2,1},{3,2},{4,3},{5,4},{6,5},{7,6},{8,7},{9,8},{10,9... | collective-permute-start | bytes 245768 | tf_op jit(solution)/shard_map/ppermute | solution.py:404

commit v5 on v4

--- a/solution.py
+++ b/solution.py
@@ -81,20 +81,18 @@
 
 def rows_kernel(lat_hbm, kap_hbm, to_lo, to_hi, kap, sems):
     copies = [
-        pltpu.make_async_copy(kap_hbm.at[0:8, :], kap.at[0:8, :], sems.at[0]),
-        pltpu.make_async_copy(kap_hbm.at[CX - 8 : CX, :], kap.at[8:16, :], sems.at[1]),
-        pltpu.make_async_copy(lat_hbm.at[0:HALO, :], to_lo.at[:, 0:WIDTH], sems.at[2]),
-        pltpu.make_async_copy(lat_hbm.at[CX - HALO : CX, :], to_hi.at[:, 0:WIDTH], sems.at[3]),
+        pltpu.make_async_copy(kap_hbm, kap, sems.at[0]),
+        pltpu.make_async_copy(lat_hbm.at[0:HALO, :], to_lo.at[:, 0:WIDTH], sems.at[1]),
+        pltpu.make_async_copy(lat_hbm.at[CX - HALO : CX, :], to_hi.at[:, 0:WIDTH], sems.at[2]),
     ]
     for copy in copies:
         copy.start()
     copies[0].wait()
-    copies[1].wait()
     blank = jnp.zeros((HALO, 128 - CY), F32)
     to_lo[:, WIDTH:] = jnp.concatenate([kap[0:HALO, :], blank], axis=1)
-    to_hi[:, WIDTH:] = jnp.concatenate([kap[16 - HALO : 16, :], blank], axis=1)
+    to_hi[:, WIDTH:] = jnp.concatenate([kap[CX - HALO : CX, :], blank], axis=1)
+    copies[1].wait()
     copies[2].wait()
-    copies[3].wait()
 
 
 def kappa_rows(dst, kap, xlo, xhi):
@@ -104,16 +102,21 @@
     dst[8 + CX : 12 + CX, :] = xhi[:, WIDTH:]
 
 
-def cols_kernel(first, last, kap, xlo, xhi, to_lo, to_hi, kext):
+def cols_kernel(flags, first, last, kap, xhi, xlo, to_odd, to_even, kext):
     kappa_rows(kext, kap, xlo, xhi)
     turned = jnp.transpose(kext[...])
-    for dst, src, at in ((to_lo, first, 0), (to_hi, last, CY - HALO)):
-        dst[0:CX, :] = src[...]
-        dst[CX : CX + 4, :] = xlo[:, at * MEMBERS : at * MEMBERS + EDGE]
-        dst[CX + 4 : CX + 8, :] = xhi[:, at * MEMBERS : at * MEMBERS + EDGE]
+    at = (0, CY - HALO)
+    spans = [slice(a * MEMBERS, a * MEMBERS + EDGE) for a in at]
+    odd = jnp.broadcast_to(flags[4:5, :], (8, 128)) > 0.5
+    wide = jnp.concatenate([odd, odd], axis=1)
+    for dst, pick in ((to_odd, lambda low, high, mask: jnp.where(mask, high, low)), (to_even, lambda low, high, mask: jnp.where(mask, low, high))):
+        for r in range(0, CX, 8):
+            dst[r : r + 8, :] = pick(first[r : r + 8, :], last[r : r + 8, :], wide)
+        for r, halo in ((CX, xlo), (CX + 4, xhi)):
+            dst[r : r + 4, :] = pick(halo[:, spans[0]], halo[:, spans[1]], wide[0:4])
         dst[CX + 8 : CX + 16, 128:256] = jnp.zeros((8, 128), F32)
         dst[CX + 12 : CX + 16, 0:128] = jnp.zeros((4, 128), F32)
-        dst[CX + 8 : CX + 12, 0:128] = turned[at : at + HALO, :]
+        dst[CX + 8 : CX + 12, 0:128] = pick(turned[0:HALO, :], turned[CY - HALO : CY, :], odd[0:4])
 
 
 def keep_rows(dst, flags):
@@ -140,7 +143,7 @@
     ext[rows_of(c, 12 + CX, 4), :] = zero4
 
 
-def inner_kernel(flags, lat, kap, xlo, xhi, val, var, tiles, value, weight, odd, ext, alpha, u3, u2, u1, kext):
+def inner_kernel(flags, lat, kap, xhi, xlo, val, var, tiles, value, weight, odd, ext, alpha, u3, u2, u1, kext):
     for c in range(BLOCKS):
         fill(ext, c, lat[:, lanes(c)], xlo[:, lanes(c)], xhi[:, lanes(c)], flags[0:1, :], flags[1:2, :])
     kappa_rows(kext, kap, xlo, xhi)
@@ -168,14 +171,18 @@
 
 
 def rim_kernel(
-    flags, cell_vmem, ylo, yhi, value, weight, odd, ext, alpha, u3, u2, u1, held,
+    flags, cell_vmem, y_odd, y_even, value, weight, odd, ext, alpha, u3, u2, u1, held,
     tiles, stat, cell, sem, ext_out, alpha_out, v3, v2, v1, kext, pbuf,
 ):
     fetch = pltpu.make_async_copy(cell_vmem, cell, sem)
     fetch.start()
     low, high = flags[0:1, :], flags[1:2, :]
     kext[...] = jnp.zeros((128, 128), F32)
-    for side, msg in enumerate((ylo, yhi)):
+    is_odd = jnp.broadcast_to(flags[4:5, :], (CX + 16, 128)) > 0.5
+    is_odd = jnp.concatenate([is_odd, is_odd], axis=1)
+    for side in range(2):
+        lower, upper = (y_even, y_odd) if side == 0 else (y_odd, y_even)
+        msg = jnp.where(is_odd, lower[...], upper[...])
         flag = flags[2 + side : 3 + side, :]
         kext[0:4, :] = msg[CX + 8 : CX + 12, 0:128]
         shifted = jnp.transpose(kext[...])[0:TALL, :] - CENTRE
@@ -337,6 +344,12 @@
     return [(i, (i + step) % count) for i in range(count)]
 
 
+def pairs(axis, first):
+    count = lax.axis_size(axis)
+    ends = [(i % count, (i + 1) % count) for i in range(first, count + first, 2)]
+    return sorted(ends + [(b, a) for a, b in ends])
+
+
 def arr(*shape):
     return jax.ShapeDtypeStruct(shape, F32)
 
@@ -364,8 +377,8 @@
 def per_device(latent, kappa, obs_cell, obs_value, obs_var):
     gx, gy = lax.axis_index("gx"), lax.axis_index("gy")
     last_x, last_y = lax.axis_size("gx") - 1, lax.axis_size("gy") - 1
-    inside = jnp.stack([gx > 0, gx < last_x, gy > 0, gy < last_y] * 2).astype(F32)
-    flags = jnp.broadcast_to(inside[:, None], (8, 128))
+    states = [gx > 0, gx < last_x, gy > 0, gy < last_y, gy % 2 == 1]
+    flags = jnp.broadcast_to(jnp.stack(states + states[:3]).astype(F32)[:, None], (8, 128))
     odd = (obs_cell & 1).astype(F32)
     obs_x, obs_y = obs_cell >> 6, obs_cell & (CY - 1)
     obs_row = (obs_x & 56) * BLOCKS + (obs_y >> 1) * 8 + (obs_x & 7)
@@ -377,31 +390,31 @@
     def part(shape, *at):
         return pl.BlockSpec(shape, lambda i: at)
 
-    to_lo, to_hi = pl.pallas_call(
+    to_lo, to_hi, kappa = pl.pallas_call(
         rows_kernel,
-        out_shape=(arr(HALO, WIDTH + 128),) * 2,
+        out_shape=(arr(HALO, WIDTH + 128),) * 2 + (arr(CX, CY),),
         in_specs=[hbm, hbm],
-        out_specs=(vmem, vmem),
-        scratch_shapes=[buf(16, CY), pltpu.SemaphoreType.DMA((4,))],
+        out_specs=(vmem,) * 3,
+        scratch_shapes=[pltpu.SemaphoreType.DMA((3,))],
         compiler_params=params(4),
         name="rows",
     )(*(pltpu.with_memory_space_constraint(a, pltpu.MemorySpace.HBM) for a in (latent, kappa)))
+    xhi = lax.ppermute(to_lo, "gx", ring("gx", -1))
     xlo = lax.ppermute(to_hi, "gx", ring("gx", 1))
-    xhi = lax.ppermute(to_lo, "gx", ring("gx", -1))
 
     whole = part((HALO, WIDTH + 128), 0, 0)
-    to_lo, to_hi = pl.pallas_call(
+    to_odd, to_even = pl.pallas_call(
         cols_kernel,
         grid=(1,),
         out_shape=(arr(CX + 16, EDGE),) * 2,
-        in_specs=[part((CX, EDGE), 0, 0), part((CX, EDGE), 0, WIDTH // EDGE - 1), part((CX, CY), 0, 0), whole, whole],
+        in_specs=[part((8, 128), 0, 0), part((CX, EDGE), 0, 0), part((CX, EDGE), 0, WIDTH // EDGE - 1), part((CX, CY), 0, 0), whole, whole],
         out_specs=(part((CX + 16, EDGE), 0, 0),) * 2,
         scratch_shapes=[buf(128, 128)],
         compiler_params=params(4),
         name="cols",
-    )(latent, latent, kappa, xlo, xhi)
-    ylo = lax.ppermute(to_hi, "gy", ring("gy", 1))
-    yhi = lax.ppermute(to_lo, "gy", ring("gy", -1))
+    )(flags, latent, latent, kappa, xhi, xlo)
+    y_odd = lax.ppermute(to_odd, "gy", pairs("gy", 1))
+    y_even = lax.ppermute(to_even, "gy", pairs("gy", 0))
 
     field = arr(BLOCKS * TALL + 2 * PAD, 128)
     tiles, *rest = pl.pallas_call(
@@ -413,7 +426,7 @@
         compiler_params=params(12),
         cost_estimate=cost(20_000_000, 12_000_000),
         name="inner",
-    )(flags, latent, kappa, xlo, xhi, val, var)
+    )(flags, latent, kappa, xhi, xlo, val, var)
 
     tiles, stat = pl.pallas_call(
         rim_kernel,
@@ -426,14 +439,17 @@
         input_output_aliases={12: 0},
         compiler_params=params(12),
         name="rim",
-    )(flags, obs_row, ylo, yhi, *rest, tiles)
+    )(flags, obs_row, y_odd, y_even, *rest, tiles)
 
     stat = stat[:, None, :]
-    for axis in ("gy", "gx"):
-        count = lax.axis_size(axis)
-        parts = lax.all_to_all(jnp.broadcast_to(stat[None], (count,) + stat.shape), axis, 0, 0)
-        if axis == "gy":
-            stat = jnp.sum(parts, axis=0)
+    stat = stat + lax.ppermute(stat, "gx", pairs("gx", 0))
+    width = lax.axis_size("gy")
+    parts = lax.all_to_all(jnp.broadcast_to(stat[None], (width,) + stat.shape), "gy", 0, 0)
+    stat = jnp.sum(parts, axis=0)
+    count = lax.axis_size("gx")
+    groups = [list(range(i, count, 2)) for i in range(2)]
+    parts = jnp.broadcast_to(stat[None], (count // 2,) + stat.shape)
+    parts = lax.all_to_all(parts, "gx", 0, 0, axis_index_groups=groups)
 
     weights, prior = pl.pallas_call(
         solve_kernel,

time: 54.2 us -> 51.1 us (0.943)
  the two profiles are of different devices: /device:TPU:1 before, /device:TPU:2 now
where the time goes in v5:
time: 51.1 us; the launch traced here: 51 us
  blocking collectives  23.9 us (47%)
  starting transfers between devices  11.2 us (22%)
  Pallas kernels  8.7 us (17%)
  waiting for transfers between devices  5.29 us (10%)
  other arithmetic  0.8 us (2%)
  between operations  0.74 us (1%)
    all_to_all x1, blocking collectives, per_device(): lax.all_to_all(jnp.broadcast_to(stat[None], (width,) + stat.shape), 'gy',...  12.5 us
    all_to_all x1, blocking collectives, per_device(): parts = lax.all_to_all(parts, 'gx', 0, 0, axis_index_groups=groups)  11.4 us
    ppermute x1, starting transfers between devices, per_device(): xhi = lax.ppermute(to_lo, 'gx', ring('gx', -1))  5.31 us
    ppermute x1, starting transfers between devices, per_device(): y_even = lax.ppermute(to_even, 'gy', pairs('gy', 0))  4.25 us
    ppermute x1, waiting for transfers between devices, per_device(): xlo = lax.ppermute(to_hi, 'gx', ring('gx', 1))  3 us
    pallas_call x1, Pallas kernels, per_device(): pl.pallas_call(inner_kernel, out_shape=(arr(CX * BLOCKS, 128),) + (arr(OB...  2.95 us
    pallas_call x1, Pallas kernels, per_device(): pl.pallas_call(solve_kernel, out_shape=(jax.ShapeDtypeStruct((256, 256),...  1.79 us
    pallas_call x1, Pallas kernels, per_device(): pl.pallas_call(rim_kernel, out_shape=(arr(CX * BLOCKS, 128), arr(STAT, 12...  1.59 us
  transfers between devices with their start and end apart: 5, of which 3 were waited for; matrix products, arithmetic and copies ran while one was open for 2% of the time, Pallas kernels for 6%

profile of v5, /device:TPU:2, one launch (start us, length us, event | category | flops | bytes accessed | tf_op | source)
XLA Modules:
  0.0 51.0 jit_solution(17355475532347294305)
XLA Ops:
  0.6 0.0 copy-start
  0.6 1.0 %rows.1 = (f32[4,4224]{1,0:T(4,128)S(1)}, f32[4,4224]{1,0:T(4,128)S(1)}, f32[64,64]{1,0:T(8,128)S(1)}) custom-call(f32[64,4096]{1,0:T(8,128)} %lat.1, f32[64,64]{1,0:T(8,128)} %kap_hbm.1), custom_call_target="tpu_custom_call" | custom-call | tf_op jit(solution)/shard_map/rows/pallas_call | solution.py:393
  1.6 0.0 copy-start.2
  1.7 0.0 copy-start.1
  1.7 5.3 %collective-permute-start = (f32[4,4224]{1,0:T(4,128)S(1)}, f32[4,4224]{1,0:T(4,128)S(1)}, u32[]{:S(2)}, u32[]{:S(2)}) collective-permute-start(f32[4,4224]{1,0:T(4,128)S(1)} %get-tuple-element.21), channel_id=1, source_target_pairs={{0,240},{16,0},{32,16},{48,32},{64,48},{80,64},{96,80},{112,96},{1... | collective-permute-start | bytes 202760 | tf_op jit(solution)/shard_map/ppermute | solution.py:402
  7.0 0.0 collective-permute-start.1
  7.0 0.7 %convert_bitcast_fusion = (f32[2,128]{1,0:T(2,128)S(1)}, s32[256]{0:T(256)S(1)}) fusion(s32[256]{0:T(256)} %param.7), kind=kLoop, calls=%fused_computation.2 | loop fusion | flops 2816 | bytes 3072 | tf_op jit(solution)/shard_map/reshape | solution.py:385
  7.7 0.1 stack.26
  7.8 1.1 %collective-permute-done.xhi = f32[4,4224]{1,0:T(4,128)S(1)} collective-permute-done((f32[4,4224]{1,0:T(4,128)S(1)}, f32[4,4224]{1,0:T(4,128)S(1)}, u32[]{:S(2)}, u32[]{:S(2)}) %collective-permute-start) | collective-permute-done | bytes 67616 | tf_op jit(solution)/shard_map/ppermute | solution.py:402
  8.9 3.0 %collective-permute-done.1.xlo = f32[4,4224]{1,0:T(4,128)S(1)} collective-permute-done((f32[4,4224]{1,0:T(4,128)S(1)}, f32[4,4224]{1,0:T(4,128)S(1)}, u32[]{:S(2)}, u32[]{:S(2)}) %collective-permute-start.1) | collective-permute-done | bytes 67616 | tf_op jit(solution)/shard_map/ppermute | solution.py:403
  11.9 0.1 broadcast_in_dim.10.flags
  12.0 0.0 copy-done
  12.0 0.1 cols.1
  12.1 1.5 %collective-permute-start.2 = (f32[80,256]{1,0:T(8,128)S(1)}, f32[80,256]{1,0:T(8,128)S(1)}, u32[]{:S(2)}, u32[]{:S(2)}) collective-permute-start(f32[80,256]{1,0:T(8,128)S(1)} %get-tuple-element.23), channel_id=1, source_target_pairs={{0,15},{1,2},{2,1},{3,4},{4,3},{5,6},{6,5},{7,8},{8,7},{9,10},{10,... | collective-permute-start | bytes 245768 | tf_op jit(solution)/shard_map/ppermute | solution.py:416
  13.6 4.3 %collective-permute-start.3 = (f32[80,256]{1,0:T(8,128)S(1)}, f32[80,256]{1,0:T(8,128)S(1)}, u32[]{:S(2)}, u32[]{:S(2)}) collective-permute-start(f32[80,256]{1,0:T(8,128)S(1)} %get-tuple-element.24), channel_id=1, source_target_pairs={{0,1},{1,0},{2,3},{3,2},{4,5},{5,4},{6,7},{7,6},{8,9},{9,8},{10,11... | collective-permute-start | bytes 245768 | tf_op jit(solution)/shard_map/ppermute | solution.py:417
  17.9 0.0 copy-done.2
  17.9 0.0 copy-done.1
  17.9 3.0 %inner.1 = (f32[2048,128]{1,0:T(8,128)S(1)}, f32[256,128]{1,0:T(8,128)S(1)}, f32[256,128]{1,0:T(8,128)S(1)}, f32[256,128]{1,0:T(8,128)S(1)}, f32[2576,128]{1,0:T...) custom-call(f32[8,128]{1,0:T(8,128)S(1)} %broadcast_in_dim.10.flags,, ...), custom_call_target="tpu_custom_call" | custom-call | flops 20000000 | bytes 12000000 | tf_op jit(solution)/shard_map/inner/pallas_call | solution.py:420
  20.8 0.0 collective-permute-done.2.y_odd
  20.8 0.0 collective-permute-done.3.y_even
  20.9 1.6 %rim.1 = (f32[2048,128]{1,0:T(8,128)S(1)}, f32[17,128]{1,0:T(8,128)S(1)}) custom-call(f32[8,128]{1,0:T(8,128)S(1)} %broadcast_in_dim.10.flags, s32[256]{0:T(256)S(1)} %get-tuple-element.39.cell_vmem, f32[80,256]{1,0:T(8,128)S(1)} %collective-permute-done.2.y_odd, f32[80,256]{1,0:T(8,128)S(1)} %collective-permute-done.3.y_even, ...), custom_call_target="tpu_custom_call", output_to_operand_aliasing={{0}: (12, {})} | custom-call | tf_op jit(solution)/shard_map/rim/pallas_call | solution.py:431
  22.5 0.1 collective-permute-start.4
  22.6 1.2 %collective-permute-done.4 = f32[17,1,128]{2,0,1:T(8,128)S(1)} collective-permute-done((f32[17,1,128]{2,0,1:T(8,128)S(1)}, f32[17,1,128]{2,0,1:T(8,128)S(1)}, u32[]{:S(2)}, u32[]{:S(2)}) %collective-permute-start.4) | collective-permute-done | bytes 8736 | tf_op jit(solution)/shard_map/ppermute | solution.py:445
  23.7 0.1 broadcast_in_dim.26
  23.8 12.5 %all_to_all.10 = f32[16,17,1,128]{3,2,1,0:T(1,128)S(1)} all-to-all(f32[16,17,1,128]{3,2,1,0:T(1,128)S(1)} %broadcast_in_dim.26), channel_id=1, replica_groups=mesh['gx'=16,'gy'=16] {'gy'}, dimensions={0} | all-to-all | bytes 278528 | tf_op jit(solution)/shard_map/all_to_all | solution.py:447
  36.3 0.1 reduce_sum.9
  36.5 11.4 %all_to_all.11.parts = f32[8,17,1,128]{3,2,1,0:T(1,128)S(1)} all-to-all(f32[8,17,1,128]{3,2,1,0:T(1,128)S(1)} %broadcast_in_dim.27), channel_id=1, replica_groups={{0,32,64,96,128,160,192,224},{16,48,80,112,144,176,208,240},{1,33,65,97..., dimensions={0} | all-to-all | bytes 139264 | tf_op jit(solution)/shard_map/all_to_all | solution.py:452
  47.9 1.8 %solve.1 = (bf16[256,256]{1,0:T(8,128)(2,1)S(1)}, f32[2048,128]{1,0:T(8,128)}) custom-call(f32[8,17,1,128]{3,2,1,0:T(1,128)S(1)} %all_to_all.11.parts, f32[2048,128]{1,0:T(8,128)S(1)} %get-tuple-element.35.tiles), custom_call_target="tpu_custom_call" | custom-call | tf_op jit(solution)/shard_map/solve/pallas_call | solution.py:454
  49.7 1.3 %update.1 = f32[2048,128]{1,0:T(8,128)} custom-call(f32[2048,128]{1,0:T(8,128)S(1)} %bitcast.28, bf16[256,256]{1,0:T(8,128)(2,1)S(1)} %get-tuple-element.36.weights), custom_call_target="tpu_custom_call" | custom-call | tf_op jit(solution)/shard_map/update/pallas_call | solution.py:463
  (4 shorter events, 0.1 us)
Async XLA Ops:
  0.6 11.3 %copy-start = (f32[64,4096]{1,0:T(8,128)S(1)}, f32[64,4096]{1,0:T(8,128)}, u32[]{:S(2)}) copy-start(f32[64,4096]{1,0:T(8,128)} %lat.1) | copy-start | bytes 3145732
  1.6 16.2 %copy-start.2 = (f32[256]{0:T(256)S(1)}, f32[256]{0:T(256)}, u32[]{:S(2)}) copy-start(f32[256]{0:T(256)} %param.8) | copy-start | bytes 3076
  1.7 16.2 %copy-start.1 = (f32[256]{0:T(256)S(1)}, f32[256]{0:T(256)}, u32[]{:S(2)}) copy-start(f32[256]{0:T(256)} %param.9) | copy-start | bytes 3076
  1.7 7.2 %collective-permute-start = (f32[4,4224]{1,0:T(4,128)S(1)}, f32[4,4224]{1,0:T(4,128)S(1)}, u32[]{:S(2)}, u32[]{:S(2)}) collective-permute-start(f32[4,4224]{1,0:T(4,128)S(1)} %get-tuple-element.21), channel_id=1, source_target_pairs={{0,240},{16,0},{32,16},{48,32},{64,48},{80,64},{96,80},{112,96},{1... | collective-permute-start | bytes 202760 | tf_op jit(solution)/shard_map/ppermute | solution.py:402
  7.0 4.9 %collective-permute-start.1 = (f32[4,4224]{1,0:T(4,128)S(1)}, f32[4,4224]{1,0:T(4,128)S(1)}, u32[]{:S(2)}, u32[]{:S(2)}) collective-permute-start(f32[4,4224]{1,0:T(4,128)S(1)} %get-tuple-element.22), channel_id=1, source_target_pairs={{0,16},{16,32},{32,48},{48,64},{64,80},{80,96},{96,112},{112,128},... | collective-permute-start | bytes 202760 | tf_op jit(solution)/shard_map/ppermute | solution.py:403
  12.1 8.8 %collective-permute-start.2 = (f32[80,256]{1,0:T(8,128)S(1)}, f32[80,256]{1,0:T(8,128)S(1)}, u32[]{:S(2)}, u32[]{:S(2)}) collective-permute-start(f32[80,256]{1,0:T(8,128)S(1)} %get-tuple-element.23), channel_id=1, source_target_pairs={{0,15},{1,2},{2,1},{3,4},{4,3},{5,6},{6,5},{7,8},{8,7},{9,10},{10,... | collective-permute-start | bytes 245768 | tf_op jit(solution)/shard_map/ppermute | solution.py:416
  13.6 7.2 %collective-permute-start.3 = (f32[80,256]{1,0:T(8,128)S(1)}, f32[80,256]{1,0:T(8,128)S(1)}, u32[]{:S(2)}, u32[]{:S(2)}) collective-permute-start(f32[80,256]{1,0:T(8,128)S(1)} %get-tuple-element.24), channel_id=1, source_target_pairs={{0,1},{1,0},{2,3},{3,2},{4,5},{5,4},{6,7},{7,6},{8,9},{9,8},{10,11... | collective-permute-start | bytes 245768 | tf_op jit(solution)/shard_map/ppermute | solution.py:417
  22.5 1.3 %collective-permute-start.4 = (f32[17,1,128]{2,0,1:T(8,128)S(1)}, f32[17,1,128]{2,0,1:T(8,128)S(1)}, u32[]{:S(2)}, u32[]{:S(2)}) collective-permute-start(f32[17,1,128]{2,0,1:T(8,128)S(1)} %bitcast.29), channel_id=1, source_target_pairs={{0,16},{16,0},{32,48},{48,32},{64,80},{80,64},{96,112},{112,96},{1... | collective-permute-start | bytes 26120 | tf_op jit(solution)/shard_map/ppermute | solution.py:445

commit v6 on v5

--- a/solution.py
+++ b/solution.py
@@ -79,44 +79,74 @@
         alpha[rows_of(c), :] = jnp.take_along_axis(shifted, upper + (2 * c + start), axis=1)
 
 
-def rows_kernel(lat_hbm, kap_hbm, to_lo, to_hi, kap, sems):
-    copies = [
-        pltpu.make_async_copy(kap_hbm, kap, sems.at[0]),
-        pltpu.make_async_copy(lat_hbm.at[0:HALO, :], to_lo.at[:, 0:WIDTH], sems.at[1]),
-        pltpu.make_async_copy(lat_hbm.at[CX - HALO : CX, :], to_hi.at[:, 0:WIDTH], sems.at[2]),
-    ]
-    for copy in copies:
-        copy.start()
-    copies[0].wait()
+def rows_kernel(lat_hbm, kap_hbm, to_odd, to_even, kap, sems):
+    is_odd = lax.rem(lax.axis_index("gx"), 2) == 1
+    fetch = pltpu.make_async_copy(kap_hbm, kap, sems.at[0])
+    fetch.start()
+
+    def copies(low, high):
+        return (
+            pltpu.make_async_copy(lat_hbm.at[0:HALO, :], low.at[:, 0:WIDTH], sems.at[1]),
+            pltpu.make_async_copy(lat_hbm.at[CX - HALO : CX, :], high.at[:, 0:WIDTH], sems.at[2]),
+        )
+
+    @pl.when(is_odd)
+    def _():
+        for copy in copies(to_even, to_odd):
+            copy.start()
+
+    @pl.when(jnp.logical_not(is_odd))
+    def _():
+        for copy in copies(to_odd, to_even):
+            copy.start()
+
+    fetch.wait()
     blank = jnp.zeros((HALO, 128 - CY), F32)
-    to_lo[:, WIDTH:] = jnp.concatenate([kap[0:HALO, :], blank], axis=1)
-    to_hi[:, WIDTH:] = jnp.concatenate([kap[CX - HALO : CX, :], blank], axis=1)
-    copies[1].wait()
-    copies[2].wait()
+    low = jnp.concatenate([kap[0:HALO, :], blank], axis=1)
+    high = jnp.concatenate([kap[CX - HALO : CX, :], blank], axis=1)
+    to_odd[:, WIDTH:] = jnp.where(is_odd, high, low)
+    to_even[:, WIDTH:] = jnp.where(is_odd, low, high)
+    for copy in copies(to_odd, to_even):
+        copy.wait()
+
+
+class Received:
+    def __init__(self, flags, x_odd, x_even, below):
+        self.is_odd = jnp.broadcast_to(flags[5:6, :], (HALO, 128)) > 0.5
+        self.odd_has, self.even_has = (x_even, x_odd) if below else (x_odd, x_even)
+
+    def __getitem__(self, c):
+        return jnp.where(self.is_odd, self.odd_has[:, lanes(c)], self.even_has[:, lanes(c)])
 
 
 def kappa_rows(dst, kap, xlo, xhi):
     dst[...] = jnp.zeros(dst.shape, F32)
     dst[8 : 8 + CX, 0:CY] = kap[...]
-    dst[4:8, :] = xlo[:, WIDTH:]
-    dst[8 + CX : 12 + CX, :] = xhi[:, WIDTH:]
-
-
-def cols_kernel(flags, first, last, kap, xhi, xlo, to_odd, to_even, kext):
+    dst[4:8, :] = xlo[BLOCKS]
+    dst[8 + CX : 12 + CX, :] = xhi[BLOCKS]
+
+
+def cols_kernel(flags, first, last, kap, x_odd, x_even, to_odd, to_even, kext):
+    xlo, xhi = Received(flags, x_odd, x_even, True), Received(flags, x_odd, x_even, False)
     kappa_rows(kext, kap, xlo, xhi)
     turned = jnp.transpose(kext[...])
-    at = (0, CY - HALO)
-    spans = [slice(a * MEMBERS, a * MEMBERS + EDGE) for a in at]
-    odd = jnp.broadcast_to(flags[4:5, :], (8, 128)) > 0.5
-    wide = jnp.concatenate([odd, odd], axis=1)
-    for dst, pick in ((to_odd, lambda low, high, mask: jnp.where(mask, high, low)), (to_even, lambda low, high, mask: jnp.where(mask, low, high))):
-        for r in range(0, CX, 8):
-            dst[r : r + 8, :] = pick(first[r : r + 8, :], last[r : r + 8, :], wide)
-        for r, halo in ((CX, xlo), (CX + 4, xhi)):
-            dst[r : r + 4, :] = pick(halo[:, spans[0]], halo[:, spans[1]], wide[0:4])
-        dst[CX + 8 : CX + 16, 128:256] = jnp.zeros((8, 128), F32)
-        dst[CX + 12 : CX + 16, 0:128] = jnp.zeros((4, 128), F32)
-        dst[CX + 8 : CX + 12, 0:128] = pick(turned[0:HALO, :], turned[CY - HALO : CY, :], odd[0:4])
+    is_odd = jnp.broadcast_to(flags[4:5, :], (8, 128)) > 0.5
+    far = BLOCKS - 2
+    for dst, swap in ((to_odd, False), (to_even, True)):
+
+        def pick(low, high):
+            low, high = (high, low) if swap else (low, high)
+            return jnp.where(is_odd[0 : low.shape[0]], high, low)
+
+        for i in range(2):
+            for r in range(0, CX, 8):
+                dst[r : r + 8, lanes(i)] = pick(first[r : r + 8, lanes(i)], last[r : r + 8, lanes(i)])
+            dst[CX : CX + 4, lanes(i)] = pick(xlo[i], xlo[far + i])
+            dst[CX + 4 : CX + 8, lanes(i)] = pick(xhi[i], xhi[far + i])
+        columns = pick(turned[0:HALO, :], turned[CY - HALO : CY, :])
+        for i in range(HALO):
+            r = CX if i < 2 else CX + 7
+            dst[r : r + 1, lanes(i % 2)] = columns[i : i + 1]
 
 
 def keep_rows(dst, flags):
@@ -143,9 +173,10 @@
     ext[rows_of(c, 12 + CX, 4), :] = zero4
 
 
-def inner_kernel(flags, lat, kap, xhi, xlo, val, var, tiles, value, weight, odd, ext, alpha, u3, u2, u1, kext):
+def inner_kernel(flags, lat, kap, x_odd, x_even, val, var, tiles, value, weight, odd, ext, alpha, u3, u2, u1, kext):
+    xlo, xhi = Received(flags, x_odd, x_even, True), Received(flags, x_odd, x_even, False)
     for c in range(BLOCKS):
-        fill(ext, c, lat[:, lanes(c)], xlo[:, lanes(c)], xhi[:, lanes(c)], flags[0:1, :], flags[1:2, :])
+        fill(ext, c, lat[:, lanes(c)], xlo[c], xhi[c], flags[0:1, :], flags[1:2, :])
     kappa_rows(kext, kap, xlo, xhi)
     spread_kappa(alpha, kext[0:TALL, :] - CENTRE, BLOCKS, 0)
 
@@ -178,13 +209,15 @@
     fetch.start()
     low, high = flags[0:1, :], flags[1:2, :]
     kext[...] = jnp.zeros((128, 128), F32)
-    is_odd = jnp.broadcast_to(flags[4:5, :], (CX + 16, 128)) > 0.5
+    is_odd = jnp.broadcast_to(flags[4:5, :], (CX + 8, 128)) > 0.5
     is_odd = jnp.concatenate([is_odd, is_odd], axis=1)
     for side in range(2):
         lower, upper = (y_even, y_odd) if side == 0 else (y_odd, y_even)
         msg = jnp.where(is_odd, lower[...], upper[...])
         flag = flags[2 + side : 3 + side, :]
-        kext[0:4, :] = msg[CX + 8 : CX + 12, 0:128]
+        for i in range(HALO):
+            r = CX if i < 2 else CX + 7
+            kext[i : i + 1, :] = msg[r : r + 1, lanes(i % 2)]
         shifted = jnp.transpose(kext[...])[0:TALL, :] - CENTRE
         upper = (lax.broadcasted_iota(jnp.int32, (TALL, 128), 1) >= MEMBERS).astype(jnp.int32)
         for p in (-2, -1):
@@ -339,11 +372,6 @@
         copy.wait()
 
 
-def ring(axis, step):
-    count = lax.axis_size(axis)
-    return [(i, (i + step) % count) for i in range(count)]
-
-
 def pairs(axis, first):
     count = lax.axis_size(axis)
     ends = [(i % count, (i + 1) % count) for i in range(first, count + first, 2)]
@@ -377,8 +405,8 @@
 def per_device(latent, kappa, obs_cell, obs_value, obs_var):
     gx, gy = lax.axis_index("gx"), lax.axis_index("gy")
     last_x, last_y = lax.axis_size("gx") - 1, lax.axis_size("gy") - 1
-    states = [gx > 0, gx < last_x, gy > 0, gy < last_y, gy % 2 == 1]
-    flags = jnp.broadcast_to(jnp.stack(states + states[:3]).astype(F32)[:, None], (8, 128))
+    states = [gx > 0, gx < last_x, gy > 0, gy < last_y, gy % 2 == 1, gx % 2 == 1]
+    flags = jnp.broadcast_to(jnp.stack(states + states[:2]).astype(F32)[:, None], (8, 128))
     odd = (obs_cell & 1).astype(F32)
     obs_x, obs_y = obs_cell >> 6, obs_cell & (CY - 1)
     obs_row = (obs_x & 56) * BLOCKS + (obs_y >> 1) * 8 + (obs_x & 7)
@@ -390,7 +418,7 @@
     def part(shape, *at):
         return pl.BlockSpec(shape, lambda i: at)
 
-    to_lo, to_hi, kappa = pl.pallas_call(
+    to_odd, to_even, kappa = pl.pallas_call(
         rows_kernel,
         out_shape=(arr(HALO, WIDTH + 128),) * 2 + (arr(CX, CY),),
         in_specs=[hbm, hbm],
@@ -399,20 +427,20 @@
         compiler_params=params(4),
         name="rows",
     )(*(pltpu.with_memory_space_constraint(a, pltpu.MemorySpace.HBM) for a in (latent, kappa)))
-    xhi = lax.ppermute(to_lo, "gx", ring("gx", -1))
-    xlo = lax.ppermute(to_hi, "gx", ring("gx", 1))
+    x_odd = lax.ppermute(to_odd, "gx", pairs("gx", 1))
+    x_even = lax.ppermute(to_even, "gx", pairs("gx", 0))
 
     whole = part((HALO, WIDTH + 128), 0, 0)
     to_odd, to_even = pl.pallas_call(
         cols_kernel,
         grid=(1,),
-        out_shape=(arr(CX + 16, EDGE),) * 2,
+        out_shape=(arr(CX + 8, EDGE),) * 2,
         in_specs=[part((8, 128), 0, 0), part((CX, EDGE), 0, 0), part((CX, EDGE), 0, WIDTH // EDGE - 1), part((CX, CY), 0, 0), whole, whole],
-        out_specs=(part((CX + 16, EDGE), 0, 0),) * 2,
+        out_specs=(part((CX + 8, EDGE), 0, 0),) * 2,
         scratch_shapes=[buf(128, 128)],
         compiler_params=params(4),
         name="cols",
-    )(flags, latent, latent, kappa, xhi, xlo)
+    )(flags, latent, latent, kappa, x_odd, x_even)
     y_odd = lax.ppermute(to_odd, "gy", pairs("gy", 1))
     y_even = lax.ppermute(to_even, "gy", pairs("gy", 0))
 
@@ -426,7 +454,7 @@
         compiler_params=params(12),
         cost_estimate=cost(20_000_000, 12_000_000),
         name="inner",
-    )(flags, latent, kappa, xhi, xlo, val, var)
+    )(flags, latent, kappa, x_odd, x_even, val, var)
 
     tiles, stat = pl.pallas_call(
         rim_kernel,

time: 51.1 us -> 51.1 us (level)
  waiting for transfers between devices: 5.29 us -> 2.34 us
  blocking collectives: 23.9 us -> 26.8 us
    ppermute x2, waiting for transfers between devices: 4.12 us -> 1.17 us  [the longest x1 1.17 us: per_device(): x_odd = lax.ppermute(to_odd, 'gx', pairs('gx', 1))]
    all_to_all x1, blocking collectives: 11.4 us -> 14.3 us  [per_device(): parts = lax.all_to_all(parts, 'gx', 0, 0, axis_index_groups=groups)]
  transfers between devices with their start and end apart: 5 -> 5, of which waited for: 3 -> 2; matrix products, arithmetic and copies ran while one was open for 2% -> 2% of each run, Pallas kernels for 6% -> 6%
where the time goes in v6:
time: 51.1 us; the launch traced here: 50.9 us
  blocking collectives  26.8 us (52%)
  starting transfers between devices  11.3 us (22%)
  Pallas kernels  8.7 us (17%)
  waiting for transfers between devices  2.34 us (5%)
  other arithmetic  0.8 us (2%)
  between operations  0.74 us (1%)
    all_to_all x1, blocking collectives, per_device(): parts = lax.all_to_all(parts, 'gx', 0, 0, axis_index_groups=groups)  14.3 us
    all_to_all x1, blocking collectives, per_device(): lax.all_to_all(jnp.broadcast_to(stat[None], (width,) + stat.shape), 'gy',...  12.4 us
    ppermute x1, starting transfers between devices, per_device(): x_odd = lax.ppermute(to_odd, 'gx', pairs('gx', 1))  5.38 us
    ppermute x1, starting transfers between devices, per_device(): y_even = lax.ppermute(to_even, 'gy', pairs('gy', 0))  4.25 us
    pallas_call x1, Pallas kernels, per_device(): pl.pallas_call(inner_kernel, out_shape=(arr(CX * BLOCKS, 128),) + (arr(OB...  2.95 us
    pallas_call x1, Pallas kernels, per_device(): pl.pallas_call(solve_kernel, out_shape=(jax.ShapeDtypeStruct((256, 256),...  1.79 us
    pallas_call x1, Pallas kernels, per_device(): pl.pallas_call(rim_kernel, out_shape=(arr(CX * BLOCKS, 128), arr(STAT, 12...  1.59 us
    ppermute x1, starting transfers between devices, per_device(): y_odd = lax.ppermute(to_odd, 'gy', pairs('gy', 1))  1.57 us
  transfers between devices with their start and end apart: 5, of which 2 were waited for; matrix products, arithmetic and copies ran while one was open for 2% of the time, Pallas kernels for 6%

profile of v6, /device:TPU:2, one launch (start us, length us, event | category | flops | bytes accessed | tf_op | source)
XLA Modules:
  0.0 50.9 jit_solution(6900397288817319921)
XLA Ops:
  0.6 0.0 copy-start
  0.6 1.0 %rows.1 = (f32[4,4224]{1,0:T(4,128)S(1)}, f32[4,4224]{1,0:T(4,128)S(1)}, f32[64,64]{1,0:T(8,128)S(1)}) custom-call(f32[64,4096]{1,0:T(8,128)} %lat.1, f32[64,64]{1,0:T(8,128)} %kap_hbm.1), custom_call_target="tpu_custom_call" | custom-call | tf_op jit(solution)/shard_map/rows/pallas_call | solution.py:421
  1.6 0.0 copy-start.2
  1.7 0.0 copy-start.1
  1.7 5.4 %collective-permute-start = (f32[4,4224]{1,0:T(4,128)S(1)}, f32[4,4224]{1,0:T(4,128)S(1)}, u32[]{:S(2)}, u32[]{:S(2)}) collective-permute-start(f32[4,4224]{1,0:T(4,128)S(1)} %get-tuple-element.21), channel_id=1, source_target_pairs={{0,240},{16,32},{32,16},{48,64},{64,48},{80,96},{96,80},{112,128},... | collective-permute-start | bytes 202760 | tf_op jit(solution)/shard_map/ppermute | solution.py:430
  7.1 0.0 collective-permute-start.1
  7.1 0.7 %convert_bitcast_fusion = (f32[2,128]{1,0:T(2,128)S(1)}, s32[256]{0:T(256)S(1)}) fusion(s32[256]{0:T(256)} %param.7), kind=kLoop, calls=%fused_computation.2 | loop fusion | flops 2816 | bytes 3072 | tf_op jit(solution)/shard_map/reshape | solution.py:413
  7.7 0.1 stack.29
  7.9 1.2 %collective-permute-done.x_odd = f32[4,4224]{1,0:T(4,128)S(1)} collective-permute-done((f32[4,4224]{1,0:T(4,128)S(1)}, f32[4,4224]{1,0:T(4,128)S(1)}, u32[]{:S(2)}, u32[]{:S(2)}) %collective-permute-start) | collective-permute-done | bytes 67616 | tf_op jit(solution)/shard_map/ppermute | solution.py:430
  9.0 0.0 collective-permute-done.1.x_even
  9.0 0.1 broadcast_in_dim.10.flags
  9.1 0.0 copy-done
  9.1 0.1 cols.1
  9.2 1.6 %collective-permute-start.2 = (f32[72,256]{1,0:T(8,128)S(1)}, f32[72,256]{1,0:T(8,128)S(1)}, u32[]{:S(2)}, u32[]{:S(2)}) collective-permute-start(f32[72,256]{1,0:T(8,128)S(1)} %get-tuple-element.23), channel_id=1, source_target_pairs={{0,15},{1,2},{2,1},{3,4},{4,3},{5,6},{6,5},{7,8},{8,7},{9,10},{10,... | collective-permute-start | bytes 221192 | tf_op jit(solution)/shard_map/ppermute | solution.py:444
  10.8 4.3 %collective-permute-start.3 = (f32[72,256]{1,0:T(8,128)S(1)}, f32[72,256]{1,0:T(8,128)S(1)}, u32[]{:S(2)}, u32[]{:S(2)}) collective-permute-start(f32[72,256]{1,0:T(8,128)S(1)} %get-tuple-element.24), channel_id=1, source_target_pairs={{0,1},{1,0},{2,3},{3,2},{4,5},{5,4},{6,7},{7,6},{8,9},{9,8},{10,11... | collective-permute-start | bytes 221192 | tf_op jit(solution)/shard_map/ppermute | solution.py:445
  15.0 0.0 copy-done.2
  15.0 0.0 copy-done.1
  15.0 3.0 %inner.1 = (f32[2048,128]{1,0:T(8,128)S(1)}, f32[256,128]{1,0:T(8,128)S(1)}, f32[256,128]{1,0:T(8,128)S(1)}, f32[256,128]{1,0:T(8,128)S(1)}, f32[2576,128]{1,0:T...) custom-call(f32[8,128]{1,0:T(8,128)S(1)} %broadcast_in_dim.10.flags,, ...), custom_call_target="tpu_custom_call" | custom-call | flops 20000000 | bytes 12000000 | tf_op jit(solution)/shard_map/inner/pallas_call | solution.py:448
  18.0 0.0 collective-permute-done.2.y_odd
  18.0 0.0 collective-permute-done.3.y_even
  18.0 1.6 %rim.1 = (f32[2048,128]{1,0:T(8,128)S(1)}, f32[17,128]{1,0:T(8,128)S(1)}) custom-call(f32[8,128]{1,0:T(8,128)S(1)} %broadcast_in_dim.10.flags, s32[256]{0:T(256)S(1)} %get-tuple-element.39.cell_vmem, f32[72,256]{1,0:T(8,128)S(1)} %collective-permute-done.2.y_odd, f32[72,256]{1,0:T(8,128)S(1)} %collective-permute-done.3.y_even, ...), custom_call_target="tpu_custom_call", output_to_operand_aliasing={{0}: (12, {})} | custom-call | tf_op jit(solution)/shard_map/rim/pallas_call | solution.py:459
  19.6 0.1 collective-permute-start.4
  19.7 1.2 %collective-permute-done.4 = f32[17,1,128]{2,0,1:T(8,128)S(1)} collective-permute-done((f32[17,1,128]{2,0,1:T(8,128)S(1)}, f32[17,1,128]{2,0,1:T(8,128)S(1)}, u32[]{:S(2)}, u32[]{:S(2)}) %collective-permute-start.4) | collective-permute-done | bytes 8736 | tf_op jit(solution)/shard_map/ppermute | solution.py:473
  20.9 0.1 broadcast_in_dim.26
  21.0 12.4 %all_to_all.10 = f32[16,17,1,128]{3,2,1,0:T(1,128)S(1)} all-to-all(f32[16,17,1,128]{3,2,1,0:T(1,128)S(1)} %broadcast_in_dim.26), channel_id=1, replica_groups=mesh['gx'=16,'gy'=16] {'gy'}, dimensions={0} | all-to-all | bytes 278528 | tf_op jit(solution)/shard_map/all_to_all | solution.py:475
  33.4 0.1 reduce_sum.9
  33.5 14.3 %all_to_all.11.parts = f32[8,17,1,128]{3,2,1,0:T(1,128)S(1)} all-to-all(f32[8,17,1,128]{3,2,1,0:T(1,128)S(1)} %broadcast_in_dim.27), channel_id=1, replica_groups={{0,32,64,96,128,160,192,224},{16,48,80,112,144,176,208,240},{1,33,65,97..., dimensions={0} | all-to-all | bytes 139264 | tf_op jit(solution)/shard_map/all_to_all | solution.py:480
  47.9 1.8 %solve.1 = (bf16[256,256]{1,0:T(8,128)(2,1)S(1)}, f32[2048,128]{1,0:T(8,128)}) custom-call(f32[8,17,1,128]{3,2,1,0:T(1,128)S(1)} %all_to_all.11.parts, f32[2048,128]{1,0:T(8,128)S(1)} %get-tuple-element.35.tiles), custom_call_target="tpu_custom_call" | custom-call | tf_op jit(solution)/shard_map/solve/pallas_call | solution.py:482
  49.7 1.3 %update.1 = f32[2048,128]{1,0:T(8,128)} custom-call(f32[2048,128]{1,0:T(8,128)S(1)} %bitcast.29, bf16[256,256]{1,0:T(8,128)(2,1)S(1)} %get-tuple-element.36.weights), custom_call_target="tpu_custom_call" | custom-call | tf_op jit(solution)/shard_map/update/pallas_call | solution.py:491
  (4 shorter events, 0.1 us)
Async XLA Ops:
  0.6 8.5 %copy-start = (f32[64,4096]{1,0:T(8,128)S(1)}, f32[64,4096]{1,0:T(8,128)}, u32[]{:S(2)}) copy-start(f32[64,4096]{1,0:T(8,128)} %lat.1) | copy-start | bytes 3145732
  1.6 13.4 %copy-start.2 = (f32[256]{0:T(256)S(1)}, f32[256]{0:T(256)}, u32[]{:S(2)}) copy-start(f32[256]{0:T(256)} %param.8) | copy-start | bytes 3076
  1.7 13.4 %copy-start.1 = (f32[256]{0:T(256)S(1)}, f32[256]{0:T(256)}, u32[]{:S(2)}) copy-start(f32[256]{0:T(256)} %param.9) | copy-start | bytes 3076
  1.7 7.4 %collective-permute-start = (f32[4,4224]{1,0:T(4,128)S(1)}, f32[4,4224]{1,0:T(4,128)S(1)}, u32[]{:S(2)}, u32[]{:S(2)}) collective-permute-start(f32[4,4224]{1,0:T(4,128)S(1)} %get-tuple-element.21), channel_id=1, source_target_pairs={{0,240},{16,32},{32,16},{48,64},{64,48},{80,96},{96,80},{112,128},... | collective-permute-start | bytes 202760 | tf_op jit(solution)/shard_map/ppermute | solution.py:430
  7.1 2.0 %collective-permute-start.1 = (f32[4,4224]{1,0:T(4,128)S(1)}, f32[4,4224]{1,0:T(4,128)S(1)}, u32[]{:S(2)}, u32[]{:S(2)}) collective-permute-start(f32[4,4224]{1,0:T(4,128)S(1)} %get-tuple-element.22), channel_id=1, source_target_pairs={{0,16},{16,0},{32,48},{48,32},{64,80},{80,64},{96,112},{112,96},{1... | collective-permute-start | bytes 202760 | tf_op jit(solution)/shard_map/ppermute | solution.py:431
  9.2 8.8 %collective-permute-start.2 = (f32[72,256]{1,0:T(8,128)S(1)}, f32[72,256]{1,0:T(8,128)S(1)}, u32[]{:S(2)}, u32[]{:S(2)}) collective-permute-start(f32[72,256]{1,0:T(8,128)S(1)} %get-tuple-element.23), channel_id=1, source_target_pairs={{0,15},{1,2},{2,1},{3,4},{4,3},{5,6},{6,5},{7,8},{8,7},{9,10},{10,... | collective-permute-start | bytes 221192 | tf_op jit(solution)/shard_map/ppermute | solution.py:444
  10.8 7.2 %collective-permute-start.3 = (f32[72,256]{1,0:T(8,128)S(1)}, f32[72,256]{1,0:T(8,128)S(1)}, u32[]{:S(2)}, u32[]{:S(2)}) collective-permute-start(f32[72,256]{1,0:T(8,128)S(1)} %get-tuple-element.24), channel_id=1, source_target_pairs={{0,1},{1,0},{2,3},{3,2},{4,5},{5,4},{6,7},{7,6},{8,9},{9,8},{10,11... | collective-permute-start | bytes 221192 | tf_op jit(solution)/shard_map/ppermute | solution.py:445
  19.6 1.3 %collective-permute-start.4 = (f32[17,1,128]{2,0,1:T(8,128)S(1)}, f32[17,1,128]{2,0,1:T(8,128)S(1)}, u32[]{:S(2)}, u32[]{:S(2)}) collective-permute-start(f32[17,1,128]{2,0,1:T(8,128)S(1)} %bitcast.30), channel_id=1, source_target_pairs={{0,16},{16,0},{32,48},{48,32},{64,80},{80,64},{96,112},{112,96},{1... | collective-permute-start | bytes 26120 | tf_op jit(solution)/shard_map/ppermute | solution.py:473

commit v7 on v6

--- a/solution.py
+++ b/solution.py
@@ -373,9 +373,23 @@
 
 
 def pairs(axis, first):
-    count = lax.axis_size(axis)
-    ends = [(i % count, (i + 1) % count) for i in range(first, count + first, 2)]
-    return sorted(ends + [(b, a) for a, b in ends])
+    count_x, count_y = lax.axis_size("gx"), lax.axis_size("gy")
+    count = count_x if axis == "gx" else count_y
+    moves = []
+    for x in range(count_x):
+        for y in range(count_y):
+            at = x if axis == "gx" else y
+            to = at + 1 if (at - first) % 2 == 0 else at - 1
+            if not 0 <= to < count:
+                target = (x, y ^ 1) if axis == "gx" else (x ^ 1, y)
+            else:
+                target = (to, y) if axis == "gx" else (x, to)
+            moves.append((x * count_y + y, target[0] * count_y + target[1]))
+    return moves
+
+
+def exchange(block, axis, first):
+    return lax.ppermute(block, ("gx", "gy"), pairs(axis, first))
 
 
 def arr(*shape):
@@ -427,8 +441,8 @@
         compiler_params=params(4),
         name="rows",
     )(*(pltpu.with_memory_space_constraint(a, pltpu.MemorySpace.HBM) for a in (latent, kappa)))
-    x_odd = lax.ppermute(to_odd, "gx", pairs("gx", 1))
-    x_even = lax.ppermute(to_even, "gx", pairs("gx", 0))
+    x_odd = exchange(to_odd, "gx", 1)
+    x_even = exchange(to_even, "gx", 0)
 
     whole = part((HALO, WIDTH + 128), 0, 0)
     to_odd, to_even = pl.pallas_call(
@@ -441,8 +455,8 @@
         compiler_params=params(4),
         name="cols",
     )(flags, latent, latent, kappa, x_odd, x_even)
-    y_odd = lax.ppermute(to_odd, "gy", pairs("gy", 1))
-    y_even = lax.ppermute(to_even, "gy", pairs("gy", 0))
+    y_odd = exchange(to_odd, "gy", 1)
+    y_even = exchange(to_even, "gy", 0)
 
     field = arr(BLOCKS * TALL + 2 * PAD, 128)
     tiles, *rest = pl.pallas_call(
@@ -470,7 +484,7 @@
     )(flags, obs_row, y_odd, y_even, *rest, tiles)
 
     stat = stat[:, None, :]
-    stat = stat + lax.ppermute(stat, "gx", pairs("gx", 0))
+    stat = stat + exchange(stat, "gx", 0)
     width = lax.axis_size("gy")
     parts = lax.all_to_all(jnp.broadcast_to(stat[None], (width,) + stat.shape), "gy", 0, 0)
     stat = jnp.sum(parts, axis=0)

time: 51.1 us -> 50.1 us (0.980)
  starting transfers between devices: 11.3 us -> 4.65 us
  blocking collectives: 26.8 us -> 31.6 us
  waiting for transfers between devices: 2.34 us -> 3.11 us
    ppermute x5, starting transfers between devices: 11.3 us -> 4.65 us  [exchange(): return lax.ppermute(block, ('gx', 'gy'), pairs(axis, first))]
    all_to_all x1, blocking collectives: 14.3 us -> 17.3 us  [per_device(): parts = lax.all_to_all(parts, 'gx', 0, 0, axis_index_groups=groups)]
    all_to_all x1, blocking collectives: 12.4 us -> 14.3 us  [per_device(): lax.all_to_all(jnp.broadcast_to(stat[None], (width,) + stat.shape), 'gy',...]
    ppermute x5, waiting for transfers between devices: 2.34 us -> 3.11 us  [exchange(): return lax.ppermute(block, ('gx', 'gy'), pairs(axis, first))]
  transfers between devices with their start and end apart: 5 -> 5, of which waited for: 2 -> 3; matrix products, arithmetic and copies ran while one was open for 2% -> 2% of each run, Pallas kernels for 6% -> 6%
where the time goes in v7:
time: 50.1 us; the launch traced here: 49.9 us
  blocking collectives  31.6 us (63%)
  Pallas kernels  8.69 us (17%)
  starting transfers between devices  4.65 us (9%)
  waiting for transfers between devices  3.11 us (6%)
  other arithmetic  0.8 us (2%)
  between operations  0.73 us (1%)
    all_to_all x1, blocking collectives, per_device(): parts = lax.all_to_all(parts, 'gx', 0, 0, axis_index_groups=groups)  17.3 us
    all_to_all x1, blocking collectives, per_device(): lax.all_to_all(jnp.broadcast_to(stat[None], (width,) + stat.shape), 'gy',...  14.3 us
    ppermute x5, starting transfers between devices, exchange(): return lax.ppermute(block, ('gx', 'gy'), pairs(axis, first))  4.65 us
    ppermute x5, waiting for transfers between devices, exchange(): return lax.ppermute(block, ('gx', 'gy'), pairs(axis, first))  3.11 us
    pallas_call x1, Pallas kernels, per_device(): pl.pallas_call(inner_kernel, out_shape=(arr(CX * BLOCKS, 128),) + (arr(OB...  2.95 us
    pallas_call x1, Pallas kernels, per_device(): pl.pallas_call(solve_kernel, out_shape=(jax.ShapeDtypeStruct((256, 256),...  1.79 us
    pallas_call x1, Pallas kernels, per_device(): pl.pallas_call(rim_kernel, out_shape=(arr(CX * BLOCKS, 128), arr(STAT, 12...  1.58 us
    pallas_call x1, Pallas kernels, per_device(): pl.pallas_call(update_kernel, out_shape=arr(CX * BLOCKS, 128), in_specs=[...  1.28 us
  transfers between devices with their start and end apart: 5, of which 3 were waited for; matrix products, arithmetic and copies ran while one was open for 2% of the time, Pallas kernels for 6%

profile of v7, /device:TPU:2, one launch (start us, length us, event | category | flops | bytes accessed | tf_op | source)
XLA Modules:
  0.0 49.9 jit_solution(13301969398728337054)
XLA Ops:
  0.6 0.0 copy-start
  0.6 1.0 %rows.1 = (f32[4,4224]{1,0:T(4,128)S(1)}, f32[4,4224]{1,0:T(4,128)S(1)}, f32[64,64]{1,0:T(8,128)S(1)}) custom-call(f32[64,4096]{1,0:T(8,128)} %lat.1, f32[64,64]{1,0:T(8,128)} %kap_hbm.1), custom_call_target="tpu_custom_call" | custom-call | tf_op jit(solution)/shard_map/rows/pallas_call | solution.py:435
  1.6 0.0 copy-start.2
  1.7 0.0 copy-start.1
  1.7 2.4 %collective-permute-start = (f32[4,4224]{1,0:T(4,128)S(1)}, f32[4,4224]{1,0:T(4,128)S(1)}, u32[]{:S(2)}, u32[]{:S(2)}) collective-permute-start(f32[4,4224]{1,0:T(4,128)S(1)} %get-tuple-element.21), channel_id=1, source_target_pairs={{0,1},{1,0},{2,3},{3,2},{4,5},{5,4},{6,7},{7,6},{8,9},{9,8},{10,11... | collective-permute-start | bytes 202760 | tf_op jit(solution)/shard_map/ppermute | solution.py:392
  4.0 0.0 collective-permute-start.1
  4.0 0.7 %convert_bitcast_fusion = (f32[2,128]{1,0:T(2,128)S(1)}, s32[256]{0:T(256)S(1)}) fusion(s32[256]{0:T(256)} %param.7), kind=kLoop, calls=%fused_computation.2 | loop fusion | flops 2816 | bytes 3072 | tf_op jit(solution)/shard_map/reshape | solution.py:427
  4.7 0.1 stack.29
  4.8 1.5 %collective-permute-done.x_odd = f32[4,4224]{1,0:T(4,128)S(1)} collective-permute-done((f32[4,4224]{1,0:T(4,128)S(1)}, f32[4,4224]{1,0:T(4,128)S(1)}, u32[]{:S(2)}, u32[]{:S(2)}) %collective-permute-start) | collective-permute-done | bytes 67616 | tf_op jit(solution)/shard_map/ppermute | solution.py:392
  6.3 0.0 collective-permute-done.1.x_even
  6.3 0.1 broadcast_in_dim.10.flags
  6.4 0.0 copy-done
  6.4 0.1 cols.1
  6.5 1.3 %collective-permute-start.2 = (f32[72,256]{1,0:T(8,128)S(1)}, f32[72,256]{1,0:T(8,128)S(1)}, u32[]{:S(2)}, u32[]{:S(2)}) collective-permute-start(f32[72,256]{1,0:T(8,128)S(1)} %get-tuple-element.23), channel_id=1, source_target_pairs={{0,16},{1,2},{2,1},{3,4},{4,3},{5,6},{6,5},{7,8},{8,7},{9,10},{10,... | collective-permute-start | bytes 221192 | tf_op jit(solution)/shard_map/ppermute | solution.py:392
  7.8 0.9 %collective-permute-start.3 = (f32[72,256]{1,0:T(8,128)S(1)}, f32[72,256]{1,0:T(8,128)S(1)}, u32[]{:S(2)}, u32[]{:S(2)}) collective-permute-start(f32[72,256]{1,0:T(8,128)S(1)} %get-tuple-element.24), channel_id=1, source_target_pairs={{0,1},{1,0},{2,3},{3,2},{4,5},{5,4},{6,7},{7,6},{8,9},{9,8},{10,11... | collective-permute-start | bytes 221192 | tf_op jit(solution)/shard_map/ppermute | solution.py:392
  8.7 0.0 copy-done.2
  8.7 0.0 copy-done.1
  8.7 3.0 %inner.1 = (f32[2048,128]{1,0:T(8,128)S(1)}, f32[256,128]{1,0:T(8,128)S(1)}, f32[256,128]{1,0:T(8,128)S(1)}, f32[256,128]{1,0:T(8,128)S(1)}, f32[2576,128]{1,0:T...) custom-call(f32[8,128]{1,0:T(8,128)S(1)} %broadcast_in_dim.10.flags,, ...), custom_call_target="tpu_custom_call" | custom-call | flops 20000000 | bytes 12000000 | tf_op jit(solution)/shard_map/inner/pallas_call | solution.py:462
  11.6 0.0 collective-permute-done.2.y_odd
  11.6 0.5 collective-permute-done.3.y_even
  12.1 1.6 %rim.1 = (f32[2048,128]{1,0:T(8,128)S(1)}, f32[17,128]{1,0:T(8,128)S(1)}) custom-call(f32[8,128]{1,0:T(8,128)S(1)} %broadcast_in_dim.10.flags, s32[256]{0:T(256)S(1)} %get-tuple-element.39.cell_vmem, f32[72,256]{1,0:T(8,128)S(1)} %collective-permute-done.2.y_odd, f32[72,256]{1,0:T(8,128)S(1)} %collective-permute-done.3.y_even, ...), custom_call_target="tpu_custom_call", output_to_operand_aliasing={{0}: (12, {})} | custom-call | tf_op jit(solution)/shard_map/rim/pallas_call | solution.py:473
  13.7 0.1 collective-permute-start.4
  13.8 1.2 %collective-permute-done.4 = f32[17,1,128]{2,0,1:T(8,128)S(1)} collective-permute-done((f32[17,1,128]{2,0,1:T(8,128)S(1)}, f32[17,1,128]{2,0,1:T(8,128)S(1)}, u32[]{:S(2)}, u32[]{:S(2)}) %collective-permute-start.4) | collective-permute-done | bytes 8736 | tf_op jit(solution)/shard_map/ppermute | solution.py:392
  15.0 0.1 broadcast_in_dim.26
  15.1 14.3 %all_to_all.10 = f32[16,17,1,128]{3,2,1,0:T(1,128)S(1)} all-to-all(f32[16,17,1,128]{3,2,1,0:T(1,128)S(1)} %broadcast_in_dim.26), channel_id=1, replica_groups=mesh['gx'=16,'gy'=16] {'gy'}, dimensions={0} | all-to-all | bytes 278528 | tf_op jit(solution)/shard_map/all_to_all | solution.py:489
  29.4 0.1 reduce_sum.9
  29.5 17.3 %all_to_all.11.parts = f32[8,17,1,128]{3,2,1,0:T(1,128)S(1)} all-to-all(f32[8,17,1,128]{3,2,1,0:T(1,128)S(1)} %broadcast_in_dim.27), channel_id=1, replica_groups={{0,32,64,96,128,160,192,224},{16,48,80,112,144,176,208,240},{1,33,65,97..., dimensions={0} | all-to-all | bytes 139264 | tf_op jit(solution)/shard_map/all_to_all | solution.py:494
  46.8 1.8 %solve.1 = (bf16[256,256]{1,0:T(8,128)(2,1)S(1)}, f32[2048,128]{1,0:T(8,128)}) custom-call(f32[8,17,1,128]{3,2,1,0:T(1,128)S(1)} %all_to_all.11.parts, f32[2048,128]{1,0:T(8,128)S(1)} %get-tuple-element.35.tiles), custom_call_target="tpu_custom_call" | custom-call | tf_op jit(solution)/shard_map/solve/pallas_call | solution.py:496
  48.6 1.3 %update.1 = f32[2048,128]{1,0:T(8,128)} custom-call(f32[2048,128]{1,0:T(8,128)S(1)} %bitcast.29, bf16[256,256]{1,0:T(8,128)(2,1)S(1)} %get-tuple-element.36.weights), custom_call_target="tpu_custom_call" | custom-call | tf_op jit(solution)/shard_map/update/pallas_call | solution.py:505
  (4 shorter events, 0.1 us)
Async XLA Ops:
  0.6 5.7 %copy-start = (f32[64,4096]{1,0:T(8,128)S(1)}, f32[64,4096]{1,0:T(8,128)}, u32[]{:S(2)}) copy-start(f32[64,4096]{1,0:T(8,128)} %lat.1) | copy-start | bytes 3145732
  1.6 7.0 %copy-start.2 = (f32[256]{0:T(256)S(1)}, f32[256]{0:T(256)}, u32[]{:S(2)}) copy-start(f32[256]{0:T(256)} %param.8) | copy-start | bytes 3076
  1.7 7.0 %copy-start.1 = (f32[256]{0:T(256)S(1)}, f32[256]{0:T(256)}, u32[]{:S(2)}) copy-start(f32[256]{0:T(256)} %param.9) | copy-start | bytes 3076
  1.7 4.6 %collective-permute-start = (f32[4,4224]{1,0:T(4,128)S(1)}, f32[4,4224]{1,0:T(4,128)S(1)}, u32[]{:S(2)}, u32[]{:S(2)}) collective-permute-start(f32[4,4224]{1,0:T(4,128)S(1)} %get-tuple-element.21), channel_id=1, source_target_pairs={{0,1},{1,0},{2,3},{3,2},{4,5},{5,4},{6,7},{7,6},{8,9},{9,8},{10,11... | collective-permute-start | bytes 202760 | tf_op jit(solution)/shard_map/ppermute | solution.py:392
  4.0 2.3 %collective-permute-start.1 = (f32[4,4224]{1,0:T(4,128)S(1)}, f32[4,4224]{1,0:T(4,128)S(1)}, u32[]{:S(2)}, u32[]{:S(2)}) collective-permute-start(f32[4,4224]{1,0:T(4,128)S(1)} %get-tuple-element.22), channel_id=1, source_target_pairs={{0,16},{1,17},{2,18},{3,19},{4,20},{5,21},{6,22},{7,23},{8,24},{9,... | collective-permute-start | bytes 202760 | tf_op jit(solution)/shard_map/ppermute | solution.py:392
  6.5 5.2 %collective-permute-start.2 = (f32[72,256]{1,0:T(8,128)S(1)}, f32[72,256]{1,0:T(8,128)S(1)}, u32[]{:S(2)}, u32[]{:S(2)}) collective-permute-start(f32[72,256]{1,0:T(8,128)S(1)} %get-tuple-element.23), channel_id=1, source_target_pairs={{0,16},{1,2},{2,1},{3,4},{4,3},{5,6},{6,5},{7,8},{8,7},{9,10},{10,... | collective-permute-start | bytes 221192 | tf_op jit(solution)/shard_map/ppermute | solution.py:392
  7.8 4.4 %collective-permute-start.3 = (f32[72,256]{1,0:T(8,128)S(1)}, f32[72,256]{1,0:T(8,128)S(1)}, u32[]{:S(2)}, u32[]{:S(2)}) collective-permute-start(f32[72,256]{1,0:T(8,128)S(1)} %get-tuple-element.24), channel_id=1, source_target_pairs={{0,1},{1,0},{2,3},{3,2},{4,5},{5,4},{6,7},{7,6},{8,9},{9,8},{10,11... | collective-permute-start | bytes 221192 | tf_op jit(solution)/shard_map/ppermute | solution.py:392
  13.7 1.3 %collective-permute-start.4 = (f32[17,1,128]{2,0,1:T(8,128)S(1)}, f32[17,1,128]{2,0,1:T(8,128)S(1)}, u32[]{:S(2)}, u32[]{:S(2)}) collective-permute-start(f32[17,1,128]{2,0,1:T(8,128)S(1)} %bitcast.30), channel_id=1, source_target_pairs={{0,16},{1,17},{2,18},{3,19},{4,20},{5,21},{6,22},{7,23},{8,24},{9,... | collective-permute-start | bytes 26120 | tf_op jit(solution)/shard_map/ppermute | solution.py:392

commit v8 on v7

--- a/solution.py
+++ b/solution.py
@@ -203,52 +203,66 @@
 
 def rim_kernel(
     flags, cell_vmem, y_odd, y_even, value, weight, odd, ext, alpha, u3, u2, u1, held,
-    tiles, stat, cell, sem, ext_out, alpha_out, v3, v2, v1, kext, pbuf,
+    tiles, stat, cell, sem, kext, pbuf, *own,
 ):
     fetch = pltpu.make_async_copy(cell_vmem, cell, sem)
     fetch.start()
     low, high = flags[0:1, :], flags[1:2, :]
-    kext[...] = jnp.zeros((128, 128), F32)
     is_odd = jnp.broadcast_to(flags[4:5, :], (CX + 8, 128)) > 0.5
     is_odd = jnp.concatenate([is_odd, is_odd], axis=1)
-    for side in range(2):
-        lower, upper = (y_even, y_odd) if side == 0 else (y_odd, y_even)
-        msg = jnp.where(is_odd, lower[...], upper[...])
-        flag = flags[2 + side : 3 + side, :]
+    odd_has, even_has = y_odd[...], y_even[...]
+    messages = (jnp.where(is_odd, even_has, odd_has), jnp.where(is_odd, odd_has, even_has))
+    kext[...] = jnp.zeros((128, 128), F32)
+    for side, msg in enumerate(messages):
         for i in range(HALO):
             r = CX if i < 2 else CX + 7
-            kext[i : i + 1, :] = msg[r : r + 1, lanes(i % 2)]
-        shifted = jnp.transpose(kext[...])[0:TALL, :] - CENTRE
-        upper = (lax.broadcasted_iota(jnp.int32, (TALL, 128), 1) >= MEMBERS).astype(jnp.int32)
+            kext[side * HALO + i : side * HALO + i + 1, :] = msg[r : r + 1, lanes(i % 2)]
+    shifted = jnp.transpose(kext[...])[0:TALL, :] - CENTRE
+    upper = (lax.broadcasted_iota(jnp.int32, (TALL, 128), 1) >= MEMBERS).astype(jnp.int32)
+    bufs = (own[0:5], own[5:10])
+
+    def local(side, p):
+        return p if side == 0 else BLOCKS - 1 - p
+
+    for side, msg in enumerate(messages):
+        flag = flags[2 + side : 3 + side, :]
+        ext_out, alpha_out = bufs[side][0:2]
         for p in (-2, -1):
             i = p + 2 if side == 0 else -1 - p
             halo = msg[CX : CX + 4, lanes(i)], msg[CX + 4 : CX + 8, lanes(i)]
             fill(ext_out, p + 2, msg[0:CX, lanes(i)] * flag, *halo, low * flag, high * flag)
-            alpha_out[rows_of(p + 2), :] = jnp.take_along_axis(shifted, upper + 2 * i, axis=1)
-
-        def local(p):
-            return p if side == 0 else BLOCKS - 1 - p
-
-        def run(near, far, mine, first, last, step, scale, store, at=0, count=TALL):
-            def pick(p, here, there, ours, start):
-                return here[rows_of(p + 2, start, count), :] if p in ours else there[rows_of(local(p), start, count), :]
-
-            get = lambda p, shift: pick(p, near, far, mine, shift)
-            xi = lambda p: pick(p, ext_out, ext, (-2, -1), at)
-            diag = lambda p: pick(p, alpha_out, alpha, (-2, -1), at)
-            order = [(p, max(p - 1, -2), p + 1) for p in range(first, last + 1)]
-            if side == 1:
-                order = [(p, b, a) for p, a, b in order]
-            sweep(get, xi, diag, order, COEFFS[step], scale, store, at, count)
-
-        def keep(dst):
-            plain = keep_rows(dst, flags)
-            return lambda p, new: plain(p + 2, new * flag if p < 0 else new)
-
-        run(ext_out, ext, (-2, -1), -2, 0, 3, COEFFS[4], keep(v3))
-        run(v3, u3, (-2, -1, 0), -1, 0, 2, 1.0, keep(v2))
-        run(v2, u2, (-2, -1, 0), -1, 1, 1, 1.0, keep(v1))
-        run(v1, u1, (-2, -1, 0, 1), 0, 1, 0, 1.0, lambda p, new: into_tiles(tiles, local(p), new), 8, CX)
+            alpha_out[rows_of(p + 2), :] = jnp.take_along_axis(shifted, upper + (side * HALO + 2 * i), axis=1)
+
+    def run(side, near, far, mine, first, last, step, scale, store, at=0, count=TALL):
+        def pick(p, here, there, ours, start):
+            return here[rows_of(p + 2, start, count), :] if p in ours else there[rows_of(local(side, p), start, count), :]
+
+        ext_out, alpha_out = bufs[side][0:2]
+        get = lambda p, shift: pick(p, near, far, mine, shift)
+        xi = lambda p: pick(p, ext_out, ext, (-2, -1), at)
+        diag = lambda p: pick(p, alpha_out, alpha, (-2, -1), at)
+        order = [(p, max(p - 1, -2), p + 1) for p in range(first, last + 1)]
+        if side == 1:
+            order = [(p, b, a) for p, a, b in order]
+        sweep(get, xi, diag, order, COEFFS[step], scale, store, at, count)
+
+    def keep(side, dst):
+        plain = keep_rows(dst, flags)
+        flag = flags[2 + side : 3 + side, :]
+        return lambda p, new: plain(p + 2, new * flag if p < 0 else new)
+
+    for side in range(2):
+        ext_out, _, v3, _, _ = bufs[side]
+        run(side, ext_out, ext, (-2, -1), -2, 0, 3, COEFFS[4], keep(side, v3))
+    for side in range(2):
+        _, _, v3, v2, _ = bufs[side]
+        run(side, v3, u3, (-2, -1, 0), -1, 0, 2, 1.0, keep(side, v2))
+    for side in range(2):
+        _, _, _, v2, v1 = bufs[side]
+        run(side, v2, u2, (-2, -1, 0), -1, 1, 1, 1.0, keep(side, v1))
+    for side in range(2):
+        finish = lambda p, new, side=side: into_tiles(tiles, local(side, p), new)
+        run(side, bufs[side][4], u1, (-2, -1, 0, 1), 0, 1, 0, 1.0, finish, 8, CX)
 
     fetch.wait()
     for j in range(OBS):
@@ -476,8 +490,8 @@
         in_specs=[vmem, anywhere] + [vmem] * 11,
         out_specs=(vmem, vmem),
         scratch_shapes=[pltpu.SMEM((OBS,), jnp.int32), pltpu.SemaphoreType.DMA]
-        + [stencil_buf(4)] * 5
-        + [buf(128, 128), buf(OBS, 128)],
+        + [buf(128, 128), buf(OBS, 128)]
+        + [stencil_buf(4)] * 10,
         input_output_aliases={12: 0},
         compiler_params=params(12),
         name="rim",

time: 50.1 us -> 50.5 us (level)
  no operation moved by 1% of the time
where the time goes in v8:
time: 50.5 us; the launch traced here: 50.3 us
  blocking collectives  31.6 us (63%)
  Pallas kernels  9.05 us (18%)
  starting transfers between devices  4.65 us (9%)
  waiting for transfers between devices  3.11 us (6%)
  other arithmetic  0.8 us (2%)
  between operations  0.73 us (1%)
    all_to_all x1, blocking collectives, per_device(): parts = lax.all_to_all(parts, 'gx', 0, 0, axis_index_groups=groups)  17.3 us
    all_to_all x1, blocking collectives, per_device(): lax.all_to_all(jnp.broadcast_to(stat[None], (width,) + stat.shape), 'gy',...  14.3 us
    ppermute x5, starting transfers between devices, exchange(): return lax.ppermute(block, ('gx', 'gy'), pairs(axis, first))  4.65 us
    ppermute x5, waiting for transfers between devices, exchange(): return lax.ppermute(block, ('gx', 'gy'), pairs(axis, first))  3.11 us
    pallas_call x1, Pallas kernels, per_device(): pl.pallas_call(inner_kernel, out_shape=(arr(CX * BLOCKS, 128),) + (arr(OB...  2.95 us
    pallas_call x1, Pallas kernels, per_device(): pl.pallas_call(rim_kernel, out_shape=(arr(CX * BLOCKS, 128), arr(STAT, 12...  1.93 us
    pallas_call x1, Pallas kernels, per_device(): pl.pallas_call(solve_kernel, out_shape=(jax.ShapeDtypeStruct((256, 256),...  1.79 us
    pallas_call x1, Pallas kernels, per_device(): pl.pallas_call(update_kernel, out_shape=arr(CX * BLOCKS, 128), in_specs=[...  1.29 us
  transfers between devices with their start and end apart: 5, of which 3 were waited for; matrix products, arithmetic and copies ran while one was open for 2% of the time, Pallas kernels for 6%

profile of v8, /device:TPU:2, one launch (start us, length us, event | category | flops | bytes accessed | tf_op | source)
XLA Modules:
  0.0 50.3 jit_solution(2868639649424548480)
XLA Ops:
  0.6 0.0 copy-start
  0.6 1.0 %rows.1 = (f32[4,4224]{1,0:T(4,128)S(1)}, f32[4,4224]{1,0:T(4,128)S(1)}, f32[64,64]{1,0:T(8,128)S(1)}) custom-call(f32[64,4096]{1,0:T(8,128)} %lat.1, f32[64,64]{1,0:T(8,128)} %kap_hbm.1), custom_call_target="tpu_custom_call" | custom-call | tf_op jit(solution)/shard_map/rows/pallas_call | solution.py:449
  1.6 0.0 copy-start.2
  1.7 0.0 copy-start.1
  1.7 2.4 %collective-permute-start = (f32[4,4224]{1,0:T(4,128)S(1)}, f32[4,4224]{1,0:T(4,128)S(1)}, u32[]{:S(2)}, u32[]{:S(2)}) collective-permute-start(f32[4,4224]{1,0:T(4,128)S(1)} %get-tuple-element.21), channel_id=1, source_target_pairs={{0,1},{1,0},{2,3},{3,2},{4,5},{5,4},{6,7},{7,6},{8,9},{9,8},{10,11... | collective-permute-start | bytes 202760 | tf_op jit(solution)/shard_map/ppermute | solution.py:406
  4.0 0.0 collective-permute-start.1
  4.0 0.7 %convert_bitcast_fusion = (f32[2,128]{1,0:T(2,128)S(1)}, s32[256]{0:T(256)S(1)}) fusion(s32[256]{0:T(256)} %param.7), kind=kLoop, calls=%fused_computation.2 | loop fusion | flops 2816 | bytes 3072 | tf_op jit(solution)/shard_map/reshape | solution.py:441
  4.7 0.1 stack.29
  4.8 1.5 %collective-permute-done.x_odd = f32[4,4224]{1,0:T(4,128)S(1)} collective-permute-done((f32[4,4224]{1,0:T(4,128)S(1)}, f32[4,4224]{1,0:T(4,128)S(1)}, u32[]{:S(2)}, u32[]{:S(2)}) %collective-permute-start) | collective-permute-done | bytes 67616 | tf_op jit(solution)/shard_map/ppermute | solution.py:406
  6.3 0.0 collective-permute-done.1.x_even
  6.3 0.1 broadcast_in_dim.10.flags
  6.4 0.0 copy-done
  6.4 0.1 cols.1
  6.5 1.3 %collective-permute-start.2 = (f32[72,256]{1,0:T(8,128)S(1)}, f32[72,256]{1,0:T(8,128)S(1)}, u32[]{:S(2)}, u32[]{:S(2)}) collective-permute-start(f32[72,256]{1,0:T(8,128)S(1)} %get-tuple-element.23), channel_id=1, source_target_pairs={{0,16},{1,2},{2,1},{3,4},{4,3},{5,6},{6,5},{7,8},{8,7},{9,10},{10,... | collective-permute-start | bytes 221192 | tf_op jit(solution)/shard_map/ppermute | solution.py:406
  7.8 0.9 %collective-permute-start.3 = (f32[72,256]{1,0:T(8,128)S(1)}, f32[72,256]{1,0:T(8,128)S(1)}, u32[]{:S(2)}, u32[]{:S(2)}) collective-permute-start(f32[72,256]{1,0:T(8,128)S(1)} %get-tuple-element.24), channel_id=1, source_target_pairs={{0,1},{1,0},{2,3},{3,2},{4,5},{5,4},{6,7},{7,6},{8,9},{9,8},{10,11... | collective-permute-start | bytes 221192 | tf_op jit(solution)/shard_map/ppermute | solution.py:406
  8.7 0.0 copy-done.2
  8.7 0.0 copy-done.1
  8.7 3.0 %inner.1 = (f32[2048,128]{1,0:T(8,128)S(1)}, f32[256,128]{1,0:T(8,128)S(1)}, f32[256,128]{1,0:T(8,128)S(1)}, f32[256,128]{1,0:T(8,128)S(1)}, f32[2576,128]{1,0:T...) custom-call(f32[8,128]{1,0:T(8,128)S(1)} %broadcast_in_dim.10.flags,, ...), custom_call_target="tpu_custom_call" | custom-call | flops 20000000 | bytes 12000000 | tf_op jit(solution)/shard_map/inner/pallas_call | solution.py:476
  11.6 0.0 collective-permute-done.2.y_odd
  11.6 0.5 collective-permute-done.3.y_even
  12.1 1.9 %rim.1 = (f32[2048,128]{1,0:T(8,128)S(1)}, f32[17,128]{1,0:T(8,128)S(1)}) custom-call(f32[8,128]{1,0:T(8,128)S(1)} %broadcast_in_dim.10.flags, s32[256]{0:T(256)S(1)} %get-tuple-element.39.cell_vmem, f32[72,256]{1,0:T(8,128)S(1)} %collective-permute-done.2.y_odd, f32[72,256]{1,0:T(8,128)S(1)} %collective-permute-done.3.y_even, ...), custom_call_target="tpu_custom_call", output_to_operand_aliasing={{0}: (12, {})} | custom-call | tf_op jit(solution)/shard_map/rim/pallas_call | solution.py:487
  14.1 0.1 collective-permute-start.4
  14.2 1.2 %collective-permute-done.4 = f32[17,1,128]{2,0,1:T(8,128)S(1)} collective-permute-done((f32[17,1,128]{2,0,1:T(8,128)S(1)}, f32[17,1,128]{2,0,1:T(8,128)S(1)}, u32[]{:S(2)}, u32[]{:S(2)}) %collective-permute-start.4) | collective-permute-done | bytes 8736 | tf_op jit(solution)/shard_map/ppermute | solution.py:406
  15.3 0.1 broadcast_in_dim.26
  15.4 14.3 %all_to_all.10 = f32[16,17,1,128]{3,2,1,0:T(1,128)S(1)} all-to-all(f32[16,17,1,128]{3,2,1,0:T(1,128)S(1)} %broadcast_in_dim.26), channel_id=1, replica_groups=mesh['gx'=16,'gy'=16] {'gy'}, dimensions={0} | all-to-all | bytes 278528 | tf_op jit(solution)/shard_map/all_to_all | solution.py:503
  29.7 0.1 reduce_sum.9
  29.9 17.3 %all_to_all.11.parts = f32[8,17,1,128]{3,2,1,0:T(1,128)S(1)} all-to-all(f32[8,17,1,128]{3,2,1,0:T(1,128)S(1)} %broadcast_in_dim.27), channel_id=1, replica_groups={{0,32,64,96,128,160,192,224},{16,48,80,112,144,176,208,240},{1,33,65,97..., dimensions={0} | all-to-all | bytes 139264 | tf_op jit(solution)/shard_map/all_to_all | solution.py:508
  47.2 1.8 %solve.1 = (bf16[256,256]{1,0:T(8,128)(2,1)S(1)}, f32[2048,128]{1,0:T(8,128)}) custom-call(f32[8,17,1,128]{3,2,1,0:T(1,128)S(1)} %all_to_all.11.parts, f32[2048,128]{1,0:T(8,128)S(1)} %get-tuple-element.35.tiles), custom_call_target="tpu_custom_call" | custom-call | tf_op jit(solution)/shard_map/solve/pallas_call | solution.py:510
  49.0 1.3 %update.1 = f32[2048,128]{1,0:T(8,128)} custom-call(f32[2048,128]{1,0:T(8,128)S(1)} %bitcast.29, bf16[256,256]{1,0:T(8,128)(2,1)S(1)} %get-tuple-element.36.weights), custom_call_target="tpu_custom_call" | custom-call | tf_op jit(solution)/shard_map/update/pallas_call | solution.py:519
  (4 shorter events, 0.1 us)
Async XLA Ops:
  0.6 5.7 %copy-start = (f32[64,4096]{1,0:T(8,128)S(1)}, f32[64,4096]{1,0:T(8,128)}, u32[]{:S(2)}) copy-start(f32[64,4096]{1,0:T(8,128)} %lat.1) | copy-start | bytes 3145732
  1.6 7.0 %copy-start.2 = (f32[256]{0:T(256)S(1)}, f32[256]{0:T(256)}, u32[]{:S(2)}) copy-start(f32[256]{0:T(256)} %param.8) | copy-start | bytes 3076
  1.7 7.0 %copy-start.1 = (f32[256]{0:T(256)S(1)}, f32[256]{0:T(256)}, u32[]{:S(2)}) copy-start(f32[256]{0:T(256)} %param.9) | copy-start | bytes 3076
  1.7 4.6 %collective-permute-start = (f32[4,4224]{1,0:T(4,128)S(1)}, f32[4,4224]{1,0:T(4,128)S(1)}, u32[]{:S(2)}, u32[]{:S(2)}) collective-permute-start(f32[4,4224]{1,0:T(4,128)S(1)} %get-tuple-element.21), channel_id=1, source_target_pairs={{0,1},{1,0},{2,3},{3,2},{4,5},{5,4},{6,7},{7,6},{8,9},{9,8},{10,11... | collective-permute-start | bytes 202760 | tf_op jit(solution)/shard_map/ppermute | solution.py:406
  4.0 2.3 %collective-permute-start.1 = (f32[4,4224]{1,0:T(4,128)S(1)}, f32[4,4224]{1,0:T(4,128)S(1)}, u32[]{:S(2)}, u32[]{:S(2)}) collective-permute-start(f32[4,4224]{1,0:T(4,128)S(1)} %get-tuple-element.22), channel_id=1, source_target_pairs={{0,16},{1,17},{2,18},{3,19},{4,20},{5,21},{6,22},{7,23},{8,24},{9,... | collective-permute-start | bytes 202760 | tf_op jit(solution)/shard_map/ppermute | solution.py:406
  6.5 5.2 %collective-permute-start.2 = (f32[72,256]{1,0:T(8,128)S(1)}, f32[72,256]{1,0:T(8,128)S(1)}, u32[]{:S(2)}, u32[]{:S(2)}) collective-permute-start(f32[72,256]{1,0:T(8,128)S(1)} %get-tuple-element.23), channel_id=1, source_target_pairs={{0,16},{1,2},{2,1},{3,4},{4,3},{5,6},{6,5},{7,8},{8,7},{9,10},{10,... | collective-permute-start | bytes 221192 | tf_op jit(solution)/shard_map/ppermute | solution.py:406
  7.8 4.4 %collective-permute-start.3 = (f32[72,256]{1,0:T(8,128)S(1)}, f32[72,256]{1,0:T(8,128)S(1)}, u32[]{:S(2)}, u32[]{:S(2)}) collective-permute-start(f32[72,256]{1,0:T(8,128)S(1)} %get-tuple-element.24), channel_id=1, source_target_pairs={{0,1},{1,0},{2,3},{3,2},{4,5},{5,4},{6,7},{7,6},{8,9},{9,8},{10,11... | collective-permute-start | bytes 221192 | tf_op jit(solution)/shard_map/ppermute | solution.py:406
  14.1 1.3 %collective-permute-start.4 = (f32[17,1,128]{2,0,1:T(8,128)S(1)}, f32[17,1,128]{2,0,1:T(8,128)S(1)}, u32[]{:S(2)}, u32[]{:S(2)}) collective-permute-start(f32[17,1,128]{2,0,1:T(8,128)S(1)} %bitcast.30), channel_id=1, source_target_pairs={{0,16},{1,17},{2,18},{3,19},{4,20},{5,21},{6,22},{7,23},{8,24},{9,... | collective-permute-start | bytes 26120 | tf_op jit(solution)/shard_map/ppermute | solution.py:406

commit v9 on v7

--- a/solution.py
+++ b/solution.py
@@ -173,7 +173,7 @@
     ext[rows_of(c, 12 + CX, 4), :] = zero4
 
 
-def inner_kernel(flags, lat, kap, x_odd, x_even, val, var, tiles, value, weight, odd, ext, alpha, u3, u2, u1, kext):
+def inner_kernel(flags, lat, kap, x_odd, x_even, val, var, tiles, value, weight, odd, parts, ext, alpha, u3, u2, u1, kext):
     xlo, xhi = Received(flags, x_odd, x_even, True), Received(flags, x_odd, x_even, False)
     for c in range(BLOCKS):
         fill(ext, c, lat[:, lanes(c)], xlo[c], xhi[c], flags[0:1, :], flags[1:2, :])
@@ -196,6 +196,12 @@
         pieces = [jnp.transpose(jnp.broadcast_to(row[i : i + 1, :], (128, 128))) for i in range(OBS // 128)]
         return jnp.concatenate(pieces, axis=0)
 
+    for t in range(CX // 8):
+        for c in range(0, BLOCKS, 2):
+            rows = slice(8 * t, 8 * t + 8)
+            pair = jnp.concatenate([lat[rows, lanes(c)], lat[rows, lanes(c + 1)]], axis=0)
+            at = (t * BLOCKS + c) * 8
+            parts[at : at + 16, 0:128], parts[at : at + 16, 128:256] = split(pair)
     value[...] = column(val[0:2, :])
     odd[...] = column(val[2:4, :])
     weight[...] = 1.0 / column(var[0:2, :])
@@ -358,14 +364,13 @@
     copy.wait()
 
 
-def update_kernel(lat, weights, out_hbm, out, sems):
+def update_kernel(lat, parts, weights, out_hbm, out, sems):
     both = weights[...]
     copies = []
     for t in range(CX // 8):
         at = slice(t * 256, (t + 1) * 256)
-        x = lat[at, :]
-        product = jnp.dot(jnp.concatenate(split(x), axis=1), both, preferred_element_type=F32)
-        out[at, :] = x + (product[:, 0:128] + product[:, 128:256])
+        product = jnp.dot(parts[at, :], both, preferred_element_type=F32)
+        out[at, :] = lat[at, :] + (product[:, 0:128] + product[:, 128:256])
         copies.append(pltpu.make_async_copy(out.at[at, :], out_hbm.at[at, :], sems.at[t]))
         copies[-1].start()
     for copy in copies:
@@ -459,11 +464,13 @@
     y_even = exchange(to_even, "gy", 0)
 
     field = arr(BLOCKS * TALL + 2 * PAD, 128)
-    tiles, *rest = pl.pallas_call(
+    tiles, value, weight, odd, split_latent, *rest = pl.pallas_call(
         inner_kernel,
-        out_shape=(arr(CX * BLOCKS, 128),) + (arr(OBS, 128),) * 3 + (field,) * 5,
+        out_shape=(arr(CX * BLOCKS, 128),) + (arr(OBS, 128),) * 3
+        + (jax.ShapeDtypeStruct((CX * BLOCKS, 256), jnp.bfloat16),)
+        + (field,) * 5,
         in_specs=[vmem] * 7,
-        out_specs=(vmem,) * 9,
+        out_specs=(vmem,) * 10,
         scratch_shapes=[buf(128, 128)],
         compiler_params=params(12),
         cost_estimate=cost(20_000_000, 12_000_000),
@@ -481,7 +488,7 @@
         input_output_aliases={12: 0},
         compiler_params=params(12),
         name="rim",
-    )(flags, obs_row, y_odd, y_even, *rest, tiles)
+    )(flags, obs_row, y_odd, y_even, value, weight, odd, *rest, tiles)
 
     stat = stat[:, None, :]
     stat = stat + exchange(stat, "gx", 0)
@@ -505,12 +512,12 @@
     latent_new = pl.pallas_call(
         update_kernel,
         out_shape=arr(CX * BLOCKS, 128),
-        in_specs=[vmem] * 2,
+        in_specs=[vmem] * 3,
         out_specs=anywhere,
         scratch_shapes=[buf(CX * BLOCKS, 128), pltpu.SemaphoreType.DMA((CX // 8,))],
         compiler_params=params(12),
         name="update",
-    )(to_tiles(latent), weights)
+    )(to_tiles(latent), split_latent, weights)
     return (from_tiles(latent_new), from_tiles(prior))
 
 

time: 50.1 us -> 50.1 us (level)
    add x0 -> x1, other arithmetic: none -> 0.69 us  [per_device(): obs_row = (obs_x & 56) * BLOCKS + (obs_y >> 1) * 8 + (obs_x & 7)]
    reshape x1 -> x0, other arithmetic: 0.69 us -> none  [per_device(): odd.reshape(2, 128)]
where the time goes in v9:
time: 50.1 us; the launch traced here: 49.9 us
  blocking collectives  31.6 us (63%)
  Pallas kernels  8.74 us (17%)
  starting transfers between devices  4.65 us (9%)
  waiting for transfers between devices  3.05 us (6%)
  other arithmetic  0.8 us (2%)
  between operations  0.73 us (1%)
    all_to_all x1, blocking collectives, per_device(): parts = lax.all_to_all(parts, 'gx', 0, 0, axis_index_groups=groups)  17.3 us
    all_to_all x1, blocking collectives, per_device(): lax.all_to_all(jnp.broadcast_to(stat[None], (width,) + stat.shape), 'gy',...  14.3 us
    ppermute x5, starting transfers between devices, exchange(): return lax.ppermute(block, ('gx', 'gy'), pairs(axis, first))  4.65 us
    ppermute x5, waiting for transfers between devices, exchange(): return lax.ppermute(block, ('gx', 'gy'), pairs(axis, first))  3.05 us
    pallas_call x1, Pallas kernels, per_device(): pl.pallas_call(inner_kernel, out_shape=(arr(CX * BLOCKS, 128),) + (arr(OB...  3.01 us
    pallas_call x1, Pallas kernels, per_device(): pl.pallas_call(solve_kernel, out_shape=(jax.ShapeDtypeStruct((256, 256),...  1.79 us
    pallas_call x1, Pallas kernels, per_device(): pl.pallas_call(rim_kernel, out_shape=(arr(CX * BLOCKS, 128), arr(STAT, 12...  1.59 us
    pallas_call x1, Pallas kernels, per_device(): pl.pallas_call(update_kernel, out_shape=arr(CX * BLOCKS, 128), in_specs=[...  1.26 us
  transfers between devices with their start and end apart: 5, of which 3 were waited for; matrix products, arithmetic and copies ran while one was open for 2% of the time, Pallas kernels for 6%

profile of v9, /device:TPU:2, one launch (start us, length us, event | category | flops | bytes accessed | tf_op | source)
XLA Modules:
  0.0 49.9 jit_solution(8499961462839177620)
XLA Ops:
  0.6 0.0 copy-start
  0.6 1.0 %rows.1 = (f32[4,4224]{1,0:T(4,128)S(1)}, f32[4,4224]{1,0:T(4,128)S(1)}, f32[64,64]{1,0:T(8,128)S(1)}) custom-call(f32[64,4096]{1,0:T(8,128)} %last.1, f32[64,64]{1,0:T(8,128)} %kap_hbm.1), custom_call_target="tpu_custom_call" | custom-call | tf_op jit(solution)/shard_map/rows/pallas_call | solution.py:440
  1.6 0.0 copy-start.2
  1.7 0.0 copy-start.1
  1.7 2.4 %collective-permute-start = (f32[4,4224]{1,0:T(4,128)S(1)}, f32[4,4224]{1,0:T(4,128)S(1)}, u32[]{:S(2)}, u32[]{:S(2)}) collective-permute-start(f32[4,4224]{1,0:T(4,128)S(1)} %get-tuple-element.22), channel_id=1, source_target_pairs={{0,1},{1,0},{2,3},{3,2},{4,5},{5,4},{6,7},{7,6},{8,9},{9,8},{10,11... | collective-permute-start | bytes 202760 | tf_op jit(solution)/shard_map/ppermute | solution.py:397
  4.0 0.0 collective-permute-start.1
  4.0 0.7 %and_add_fusion = (s32[256]{0:T(256)S(1)}, f32[2,128]{1,0:T(2,128)S(1)}) fusion(s32[256]{0:T(256)} %param.7), kind=kLoop, calls=%fused_computation.2 | loop fusion | flops 2816 | bytes 3072 | tf_op jit(solution)/shard_map/add | solution.py:431
  4.7 0.1 stack.29
  4.8 1.5 %collective-permute-done.x_odd = f32[4,4224]{1,0:T(4,128)S(1)} collective-permute-done((f32[4,4224]{1,0:T(4,128)S(1)}, f32[4,4224]{1,0:T(4,128)S(1)}, u32[]{:S(2)}, u32[]{:S(2)}) %collective-permute-start) | collective-permute-done | bytes 67616 | tf_op jit(solution)/shard_map/ppermute | solution.py:397
  6.3 0.0 collective-permute-done.1.x_even
  6.3 0.1 broadcast_in_dim.10.flags
  6.4 0.0 copy-done
  6.4 0.1 cols.1
  6.5 1.3 %collective-permute-start.2 = (f32[72,256]{1,0:T(8,128)S(1)}, f32[72,256]{1,0:T(8,128)S(1)}, u32[]{:S(2)}, u32[]{:S(2)}) collective-permute-start(f32[72,256]{1,0:T(8,128)S(1)} %get-tuple-element.25), channel_id=1, source_target_pairs={{0,16},{1,2},{2,1},{3,4},{4,3},{5,6},{6,5},{7,8},{8,7},{9,10},{10,... | collective-permute-start | bytes 221192 | tf_op jit(solution)/shard_map/ppermute | solution.py:397
  7.8 0.9 %collective-permute-start.3 = (f32[72,256]{1,0:T(8,128)S(1)}, f32[72,256]{1,0:T(8,128)S(1)}, u32[]{:S(2)}, u32[]{:S(2)}) collective-permute-start(f32[72,256]{1,0:T(8,128)S(1)} %get-tuple-element.26), channel_id=1, source_target_pairs={{0,1},{1,0},{2,3},{3,2},{4,5},{5,4},{6,7},{7,6},{8,9},{9,8},{10,11... | collective-permute-start | bytes 221192 | tf_op jit(solution)/shard_map/ppermute | solution.py:397
  8.7 0.0 copy-done.2
  8.7 0.0 copy-done.1
  8.7 3.0 %inner.1 = (f32[2048,128]{1,0:T(8,128)S(1)}, f32[256,128]{1,0:T(8,128)S(1)}, f32[256,128]{1,0:T(8,128)S(1)}, f32[256,128]{1,0:T(8,128)S(1)}, bf16[2048,256]{1,0:...) custom-call(f32[8,128]{1,0:T(8,128)S(1)} %broadcast_in_dim.10.flags,, ...), custom_call_target="tpu_custom_call" | custom-call | flops 20000000 | bytes 12000000 | tf_op jit(solution)/shard_map/inner/pallas_call | solution.py:467
  11.7 0.0 collective-permute-done.2.y_odd
  11.7 0.4 collective-permute-done.3.y_even
  12.1 1.6 %rim.1 = (f32[2048,128]{1,0:T(8,128)S(1)}, f32[17,128]{1,0:T(8,128)S(1)}) custom-call(f32[8,128]{1,0:T(8,128)S(1)} %broadcast_in_dim.10.flags, s32[256]{0:T(256)S(1)} %get-tuple-element.40.cell_vmem, f32[72,256]{1,0:T(8,128)S(1)} %collective-permute-done.2.y_odd, f32[72,256]{1,0:T(8,128)S(1)} %collective-permute-done.3.y_even, ...), custom_call_target="tpu_custom_call", output_to_operand_aliasing={{0}: (12, {})} | custom-call | tf_op jit(solution)/shard_map/rim/pallas_call | solution.py:480
  13.7 0.1 collective-permute-start.4
  13.8 1.2 %collective-permute-done.4 = f32[17,1,128]{2,0,1:T(8,128)S(1)} collective-permute-done((f32[17,1,128]{2,0,1:T(8,128)S(1)}, f32[17,1,128]{2,0,1:T(8,128)S(1)}, u32[]{:S(2)}, u32[]{:S(2)}) %collective-permute-start.4) | collective-permute-done | bytes 8736 | tf_op jit(solution)/shard_map/ppermute | solution.py:397
  15.0 0.1 broadcast_in_dim.26
  15.1 14.3 %all_to_all.10 = f32[16,17,1,128]{3,2,1,0:T(1,128)S(1)} all-to-all(f32[16,17,1,128]{3,2,1,0:T(1,128)S(1)} %broadcast_in_dim.26), channel_id=1, replica_groups=mesh['gx'=16,'gy'=16] {'gy'}, dimensions={0} | all-to-all | bytes 278528 | tf_op jit(solution)/shard_map/all_to_all | solution.py:496
  29.4 0.1 reduce_sum.9
  29.5 17.3 %all_to_all.11.parts = f32[8,17,1,128]{3,2,1,0:T(1,128)S(1)} all-to-all(f32[8,17,1,128]{3,2,1,0:T(1,128)S(1)} %broadcast_in_dim.27), channel_id=1, replica_groups={{0,32,64,96,128,160,192,224},{16,48,80,112,144,176,208,240},{1,33,65,97..., dimensions={0} | all-to-all | bytes 139264 | tf_op jit(solution)/shard_map/all_to_all | solution.py:501
  46.8 1.8 %solve.1 = (bf16[256,256]{1,0:T(8,128)(2,1)S(1)}, f32[2048,128]{1,0:T(8,128)}) custom-call(f32[8,17,1,128]{3,2,1,0:T(1,128)S(1)} %all_to_all.11.parts, f32[2048,128]{1,0:T(8,128)S(1)} %get-tuple-element.37.tiles), custom_call_target="tpu_custom_call" | custom-call | tf_op jit(solution)/shard_map/solve/pallas_call | solution.py:503
  48.6 1.3 %update.1 = f32[2048,128]{1,0:T(8,128)} custom-call(f32[2048,128]{1,0:T(8,128)S(1)} %bitcast.29, bf16[2048,256]{1,0:T(8,128)(2,1)S(1)} %get-tuple-element.24.parts, bf16[256,256]{1,0:T(8,128)(2,1)S(1)} %get-tuple-element.38.weights), custom_call_target="tpu_custom_call" | custom-call | tf_op jit(solution)/shard_map/update/pallas_call | solution.py:512
  (4 shorter events, 0.1 us)
Async XLA Ops:
  0.6 5.7 %copy-start = (f32[64,4096]{1,0:T(8,128)S(1)}, f32[64,4096]{1,0:T(8,128)}, u32[]{:S(2)}) copy-start(f32[64,4096]{1,0:T(8,128)} %last.1) | copy-start | bytes 3145732
  1.6 7.0 %copy-start.2 = (f32[256]{0:T(256)S(1)}, f32[256]{0:T(256)}, u32[]{:S(2)}) copy-start(f32[256]{0:T(256)} %param.8) | copy-start | bytes 3076
  1.7 7.0 %copy-start.1 = (f32[256]{0:T(256)S(1)}, f32[256]{0:T(256)}, u32[]{:S(2)}) copy-start(f32[256]{0:T(256)} %param.9) | copy-start | bytes 3076
  1.7 4.6 %collective-permute-start = (f32[4,4224]{1,0:T(4,128)S(1)}, f32[4,4224]{1,0:T(4,128)S(1)}, u32[]{:S(2)}, u32[]{:S(2)}) collective-permute-start(f32[4,4224]{1,0:T(4,128)S(1)} %get-tuple-element.22), channel_id=1, source_target_pairs={{0,1},{1,0},{2,3},{3,2},{4,5},{5,4},{6,7},{7,6},{8,9},{9,8},{10,11... | collective-permute-start | bytes 202760 | tf_op jit(solution)/shard_map/ppermute | solution.py:397
  4.0 2.3 %collective-permute-start.1 = (f32[4,4224]{1,0:T(4,128)S(1)}, f32[4,4224]{1,0:T(4,128)S(1)}, u32[]{:S(2)}, u32[]{:S(2)}) collective-permute-start(f32[4,4224]{1,0:T(4,128)S(1)} %get-tuple-element.23), channel_id=1, source_target_pairs={{0,16},{1,17},{2,18},{3,19},{4,20},{5,21},{6,22},{7,23},{8,24},{9,... | collective-permute-start | bytes 202760 | tf_op jit(solution)/shard_map/ppermute | solution.py:397
  6.5 5.2 %collective-permute-start.2 = (f32[72,256]{1,0:T(8,128)S(1)}, f32[72,256]{1,0:T(8,128)S(1)}, u32[]{:S(2)}, u32[]{:S(2)}) collective-permute-start(f32[72,256]{1,0:T(8,128)S(1)} %get-tuple-element.25), channel_id=1, source_target_pairs={{0,16},{1,2},{2,1},{3,4},{4,3},{5,6},{6,5},{7,8},{8,7},{9,10},{10,... | collective-permute-start | bytes 221192 | tf_op jit(solution)/shard_map/ppermute | solution.py:397
  7.8 4.4 %collective-permute-start.3 = (f32[72,256]{1,0:T(8,128)S(1)}, f32[72,256]{1,0:T(8,128)S(1)}, u32[]{:S(2)}, u32[]{:S(2)}) collective-permute-start(f32[72,256]{1,0:T(8,128)S(1)} %get-tuple-element.26), channel_id=1, source_target_pairs={{0,1},{1,0},{2,3},{3,2},{4,5},{5,4},{6,7},{7,6},{8,9},{9,8},{10,11... | collective-permute-start | bytes 221192 | tf_op jit(solution)/shard_map/ppermute | solution.py:397
  13.7 1.3 %collective-permute-start.4 = (f32[17,1,128]{2,0,1:T(8,128)S(1)}, f32[17,1,128]{2,0,1:T(8,128)S(1)}, u32[]{:S(2)}, u32[]{:S(2)}) collective-permute-start(f32[17,1,128]{2,0,1:T(8,128)S(1)} %bitcast.30), channel_id=1, source_target_pairs={{0,16},{1,17},{2,18},{3,19},{4,20},{5,21},{6,22},{7,23},{8,24},{9,... | collective-permute-start | bytes 26120 | tf_op jit(solution)/shard_map/ppermute | solution.py:397

commit v10 on v7

--- a/solution.py
+++ b/solution.py
@@ -79,8 +79,9 @@
         alpha[rows_of(c), :] = jnp.take_along_axis(shifted, upper + (2 * c + start), axis=1)
 
 
-def rows_kernel(lat_hbm, kap_hbm, to_odd, to_even, kap, sems):
-    is_odd = lax.rem(lax.axis_index("gx"), 2) == 1
+def edges_kernel(lat_hbm, kap_hbm, to_odd, to_even, y_to_odd, y_to_even, kap, sems):
+    odds = [lax.rem(lax.axis_index(axis), 2) == 1 for axis in ("gx", "gy")]
+    is_odd = odds[0]
     fetch = pltpu.make_async_copy(kap_hbm, kap, sems.at[0])
     fetch.start()
 
@@ -90,15 +91,24 @@
             pltpu.make_async_copy(lat_hbm.at[CX - HALO : CX, :], high.at[:, 0:WIDTH], sems.at[2]),
         )
 
-    @pl.when(is_odd)
-    def _():
-        for copy in copies(to_even, to_odd):
-            copy.start()
-
-    @pl.when(jnp.logical_not(is_odd))
-    def _():
-        for copy in copies(to_odd, to_even):
-            copy.start()
+    def columns(low, high):
+        return (
+            pltpu.make_async_copy(lat_hbm.at[:, 0:EDGE], low, sems.at[3]),
+            pltpu.make_async_copy(lat_hbm.at[:, WIDTH - EDGE : WIDTH], high, sems.at[4]),
+        )
+
+    ways = ((odds[0], copies, to_odd, to_even), (odds[1], columns, y_to_odd, y_to_even))
+    for odd, make, first, second in ways:
+
+        @pl.when(odd)
+        def _(make=make, first=first, second=second):
+            for copy in make(second, first):
+                copy.start()
+
+        @pl.when(jnp.logical_not(odd))
+        def _(make=make, first=first, second=second):
+            for copy in make(first, second):
+                copy.start()
 
     fetch.wait()
     blank = jnp.zeros((HALO, 128 - CY), F32)
@@ -106,7 +116,7 @@
     high = jnp.concatenate([kap[CX - HALO : CX, :], blank], axis=1)
     to_odd[:, WIDTH:] = jnp.where(is_odd, high, low)
     to_even[:, WIDTH:] = jnp.where(is_odd, low, high)
-    for copy in copies(to_odd, to_even):
+    for copy in copies(to_odd, to_even) + columns(y_to_odd, y_to_even):
         copy.wait()
 
 
@@ -126,26 +136,24 @@
     dst[8 + CX : 12 + CX, :] = xhi[BLOCKS]
 
 
-def cols_kernel(flags, first, last, kap, x_odd, x_even, to_odd, to_even, kext):
+def corners_kernel(flags, kap, x_odd, x_even, to_odd, to_even, kext):
     xlo, xhi = Received(flags, x_odd, x_even, True), Received(flags, x_odd, x_even, False)
     kappa_rows(kext, kap, xlo, xhi)
     turned = jnp.transpose(kext[...])
-    is_odd = jnp.broadcast_to(flags[4:5, :], (8, 128)) > 0.5
+    is_odd = jnp.broadcast_to(flags[4:5, :], (HALO, 128)) > 0.5
     far = BLOCKS - 2
     for dst, swap in ((to_odd, False), (to_even, True)):
 
         def pick(low, high):
             low, high = (high, low) if swap else (low, high)
-            return jnp.where(is_odd[0 : low.shape[0]], high, low)
+            return jnp.where(is_odd, high, low)
 
         for i in range(2):
-            for r in range(0, CX, 8):
-                dst[r : r + 8, lanes(i)] = pick(first[r : r + 8, lanes(i)], last[r : r + 8, lanes(i)])
-            dst[CX : CX + 4, lanes(i)] = pick(xlo[i], xlo[far + i])
-            dst[CX + 4 : CX + 8, lanes(i)] = pick(xhi[i], xhi[far + i])
+            dst[0:4, lanes(i)] = pick(xlo[i], xlo[far + i])
+            dst[4:8, lanes(i)] = pick(xhi[i], xhi[far + i])
         columns = pick(turned[0:HALO, :], turned[CY - HALO : CY, :])
         for i in range(HALO):
-            r = CX if i < 2 else CX + 7
+            r = 0 if i < 2 else 7
             dst[r : r + 1, lanes(i % 2)] = columns[i : i + 1]
 
 
@@ -202,28 +210,30 @@
 
 
 def rim_kernel(
-    flags, cell_vmem, y_odd, y_even, value, weight, odd, ext, alpha, u3, u2, u1, held,
+    flags, cell_vmem, y_odd, y_even, corner_odd, corner_even, value, weight, odd, ext, alpha, u3, u2, u1, held,
     tiles, stat, cell, sem, ext_out, alpha_out, v3, v2, v1, kext, pbuf,
 ):
     fetch = pltpu.make_async_copy(cell_vmem, cell, sem)
     fetch.start()
     low, high = flags[0:1, :], flags[1:2, :]
     kext[...] = jnp.zeros((128, 128), F32)
-    is_odd = jnp.broadcast_to(flags[4:5, :], (CX + 8, 128)) > 0.5
+    is_odd = jnp.broadcast_to(flags[4:5, :], (CX, 128)) > 0.5
     is_odd = jnp.concatenate([is_odd, is_odd], axis=1)
     for side in range(2):
         lower, upper = (y_even, y_odd) if side == 0 else (y_odd, y_even)
         msg = jnp.where(is_odd, lower[...], upper[...])
+        lower, upper = (corner_even, corner_odd) if side == 0 else (corner_odd, corner_even)
+        corner = jnp.where(is_odd[0:8], lower[...], upper[...])
         flag = flags[2 + side : 3 + side, :]
         for i in range(HALO):
-            r = CX if i < 2 else CX + 7
-            kext[i : i + 1, :] = msg[r : r + 1, lanes(i % 2)]
+            r = 0 if i < 2 else 7
+            kext[i : i + 1, :] = corner[r : r + 1, lanes(i % 2)]
         shifted = jnp.transpose(kext[...])[0:TALL, :] - CENTRE
         upper = (lax.broadcasted_iota(jnp.int32, (TALL, 128), 1) >= MEMBERS).astype(jnp.int32)
         for p in (-2, -1):
             i = p + 2 if side == 0 else -1 - p
-            halo = msg[CX : CX + 4, lanes(i)], msg[CX + 4 : CX + 8, lanes(i)]
-            fill(ext_out, p + 2, msg[0:CX, lanes(i)] * flag, *halo, low * flag, high * flag)
+            halo = corner[0:4, lanes(i)], corner[4:8, lanes(i)]
+            fill(ext_out, p + 2, msg[:, lanes(i)] * flag, *halo, low * flag, high * flag)
             alpha_out[rows_of(p + 2), :] = jnp.take_along_axis(shifted, upper + 2 * i, axis=1)
 
         def local(p):
@@ -429,34 +439,31 @@
     vmem, anywhere = pl.BlockSpec(memory_space=VMEM), pl.BlockSpec(memory_space=pl.ANY)
     hbm = pl.BlockSpec(memory_space=pltpu.MemorySpace.HBM)
 
-    def part(shape, *at):
-        return pl.BlockSpec(shape, lambda i: at)
-
-    to_odd, to_even, kappa = pl.pallas_call(
-        rows_kernel,
-        out_shape=(arr(HALO, WIDTH + 128),) * 2 + (arr(CX, CY),),
+    to_odd, to_even, y_to_odd, y_to_even, kappa = pl.pallas_call(
+        edges_kernel,
+        out_shape=(arr(HALO, WIDTH + 128),) * 2 + (arr(CX, EDGE),) * 2 + (arr(CX, CY),),
         in_specs=[hbm, hbm],
-        out_specs=(vmem,) * 3,
-        scratch_shapes=[pltpu.SemaphoreType.DMA((3,))],
+        out_specs=(vmem,) * 5,
+        scratch_shapes=[pltpu.SemaphoreType.DMA((5,))],
         compiler_params=params(4),
-        name="rows",
+        name="edges",
     )(*(pltpu.with_memory_space_constraint(a, pltpu.MemorySpace.HBM) for a in (latent, kappa)))
     x_odd = exchange(to_odd, "gx", 1)
     x_even = exchange(to_even, "gx", 0)
-
-    whole = part((HALO, WIDTH + 128), 0, 0)
+    y_odd = exchange(y_to_odd, "gy", 1)
+    y_even = exchange(y_to_even, "gy", 0)
+
     to_odd, to_even = pl.pallas_call(
-        cols_kernel,
-        grid=(1,),
-        out_shape=(arr(CX + 8, EDGE),) * 2,
-        in_specs=[part((8, 128), 0, 0), part((CX, EDGE), 0, 0), part((CX, EDGE), 0, WIDTH // EDGE - 1), part((CX, CY), 0, 0), whole, whole],
-        out_specs=(part((CX + 8, EDGE), 0, 0),) * 2,
+        corners_kernel,
+        out_shape=(arr(8, EDGE),) * 2,
+        in_specs=[vmem] * 4,
+        out_specs=(vmem,) * 2,
         scratch_shapes=[buf(128, 128)],
         compiler_params=params(4),
-        name="cols",
-    )(flags, latent, latent, kappa, x_odd, x_even)
-    y_odd = exchange(to_odd, "gy", 1)
-    y_even = exchange(to_even, "gy", 0)
+        name="corners",
+    )(flags, kappa, x_odd, x_even)
+    corner_odd = exchange(to_odd, "gy", 1)
+    corner_even = exchange(to_even, "gy", 0)
 
     field = arr(BLOCKS * TALL + 2 * PAD, 128)
     tiles, *rest = pl.pallas_call(
@@ -473,15 +480,15 @@
     tiles, stat = pl.pallas_call(
         rim_kernel,
         out_shape=(arr(CX * BLOCKS, 128), arr(STAT, 128)),
-        in_specs=[vmem, anywhere] + [vmem] * 11,
+        in_specs=[vmem, anywhere] + [vmem] * 13,
         out_specs=(vmem, vmem),
         scratch_shapes=[pltpu.SMEM((OBS,), jnp.int32), pltpu.SemaphoreType.DMA]
         + [stencil_buf(4)] * 5
         + [buf(128, 128), buf(OBS, 128)],
-        input_output_aliases={12: 0},
+        input_output_aliases={14: 0},
         compiler_params=params(12),
         name="rim",
-    )(flags, obs_row, y_odd, y_even, *rest, tiles)
+    )(flags, obs_row, y_odd, y_even, corner_odd, corner_even, *rest, tiles)
 
     stat = stat[:, None, :]
     stat = stat + exchange(stat, "gx", 0)

time: 50.1 us -> 52.4 us (1.046)
  waiting for transfers between devices: 3.11 us -> 4.13 us
  starting transfers between devices: 4.65 us -> 5.61 us
    ppermute x5 -> x7, waiting for transfers between devices: 3.11 us -> 4.13 us  [exchange(): return lax.ppermute(block, ('gx', 'gy'), pairs(axis, first))]
    ppermute x5 -> x7, starting transfers between devices: 4.65 us -> 5.61 us  [exchange(): return lax.ppermute(block, ('gx', 'gy'), pairs(axis, first))]
    all_to_all x1, blocking collectives: 14.3 us -> 15.2 us  [per_device(): lax.all_to_all(jnp.broadcast_to(stat[None], (width,) + stat.shape), 'gy',...]
    all_to_all x1, blocking collectives: 17.3 us -> 16.7 us  [per_device(): parts = lax.all_to_all(parts, 'gx', 0, 0, axis_index_groups=groups)]
  transfers between devices with their start and end apart: 5 -> 7, of which waited for: 3 -> 3; matrix products, arithmetic and copies ran while one was open for 2% -> 2% of each run, Pallas kernels for 6% -> 6%
where the time goes in v10:
time: 52.4 us; the launch traced here: 52.2 us
  blocking collectives  31.8 us (61%)
  Pallas kernels  8.77 us (17%)
  starting transfers between devices  5.61 us (11%)
  waiting for transfers between devices  4.13 us (8%)
  other arithmetic  0.8 us (2%)
  between operations  0.76 us (1%)
    all_to_all x1, blocking collectives, per_device(): parts = lax.all_to_all(parts, 'gx', 0, 0, axis_index_groups=groups)  16.7 us
    all_to_all x1, blocking collectives, per_device(): lax.all_to_all(jnp.broadcast_to(stat[None], (width,) + stat.shape), 'gy',...  15.2 us
    ppermute x7, starting transfers between devices, exchange(): return lax.ppermute(block, ('gx', 'gy'), pairs(axis, first))  5.61 us
    ppermute x7, waiting for transfers between devices, exchange(): return lax.ppermute(block, ('gx', 'gy'), pairs(axis, first))  4.13 us
    pallas_call x1, Pallas kernels, per_device(): pl.pallas_call(inner_kernel, out_shape=(arr(CX * BLOCKS, 128),) + (arr(OB...  2.95 us
    pallas_call x1, Pallas kernels, per_device(): pl.pallas_call(solve_kernel, out_shape=(jax.ShapeDtypeStruct((256, 256),...  1.79 us
    pallas_call x1, Pallas kernels, per_device(): pl.pallas_call(rim_kernel, out_shape=(arr(CX * BLOCKS, 128), arr(STAT, 12...  1.59 us
    pallas_call x1, Pallas kernels, per_device(): pl.pallas_call(update_kernel, out_shape=arr(CX * BLOCKS, 128), in_specs=[...  1.28 us
  transfers between devices with their start and end apart: 7, of which 3 were waited for; matrix products, arithmetic and copies ran while one was open for 2% of the time, Pallas kernels for 6%

profile of v10, /device:TPU:2, one launch (start us, length us, event | category | flops | bytes accessed | tf_op | source)
XLA Modules:
  0.0 52.2 jit_solution(3617143201411192513)
XLA Ops:
  0.6 0.0 copy-start
  0.6 0.0 copy-start.2
  0.7 0.0 copy-start.1
  0.7 1.1 %edges.1 = (f32[4,4224]{1,0:T(4,128)S(1)}, f32[4,4224]{1,0:T(4,128)S(1)}, f32[64,256]{1,0:T(8,128)S(1)}, f32[64,256]{1,0:T(8,128)S(1)}, f32[64,64]{1,0:T(8,128)S(1)}) custom-call(f32[64,4096]{1,0:T(8,128)} %lat.1, f32[64,64]{1,0:T(8,128)} %kap_hbm.1), custom_call_target="tpu_custom_call" | custom-call | tf_op jit(solution)/shard_map/edges/pallas_call | solution.py:442
  1.7 1.6 %collective-permute-start = (f32[64,256]{1,0:T(8,128)S(1)}, f32[64,256]{1,0:T(8,128)S(1)}, u32[]{:S(2)}, u32[]{:S(2)}) collective-permute-start(f32[64,256]{1,0:T(8,128)S(1)} %get-tuple-element.22), channel_id=1, source_target_pairs={{0,16},{1,2},{2,1},{3,4},{4,3},{5,6},{6,5},{7,8},{8,7},{9,10},{10,... | collective-permute-start | bytes 196616 | tf_op jit(solution)/shard_map/ppermute | solution.py:402
  3.3 0.9 %collective-permute-start.1 = (f32[64,256]{1,0:T(8,128)S(1)}, f32[64,256]{1,0:T(8,128)S(1)}, u32[]{:S(2)}, u32[]{:S(2)}) collective-permute-start(f32[64,256]{1,0:T(8,128)S(1)} %get-tuple-element.23), channel_id=1, source_target_pairs={{0,1},{1,0},{2,3},{3,2},{4,5},{5,4},{6,7},{7,6},{8,9},{9,8},{10,11... | collective-permute-start | bytes 196616 | tf_op jit(solution)/shard_map/ppermute | solution.py:402
  4.2 1.1 %collective-permute-start.2 = (f32[4,4224]{1,0:T(4,128)S(1)}, f32[4,4224]{1,0:T(4,128)S(1)}, u32[]{:S(2)}, u32[]{:S(2)}) collective-permute-start(f32[4,4224]{1,0:T(4,128)S(1)} %get-tuple-element.25), channel_id=1, source_target_pairs={{0,1},{1,0},{2,3},{3,2},{4,5},{5,4},{6,7},{7,6},{8,9},{9,8},{10,11... | collective-permute-start | bytes 202760 | tf_op jit(solution)/shard_map/ppermute | solution.py:402
  5.4 0.0 collective-permute-start.3
  5.4 0.7 %convert_bitcast_fusion = (f32[2,128]{1,0:T(2,128)S(1)}, s32[256]{0:T(256)S(1)}) fusion(s32[256]{0:T(256)} %param.7), kind=kLoop, calls=%fused_computation.2 | loop fusion | flops 2816 | bytes 3072 | tf_op jit(solution)/shard_map/reshape | solution.py:437
  6.0 0.1 stack.29
  6.2 2.3 %collective-permute-done.2.x_odd = f32[4,4224]{1,0:T(4,128)S(1)} collective-permute-done((f32[4,4224]{1,0:T(4,128)S(1)}, f32[4,4224]{1,0:T(4,128)S(1)}, u32[]{:S(2)}, u32[]{:S(2)}) %collective-permute-start.2) | collective-permute-done | bytes 67616 | tf_op jit(solution)/shard_map/ppermute | solution.py:402
  8.5 0.0 collective-permute-done.3.x_even
  8.5 0.1 broadcast_in_dim.10.flags
  8.6 0.1 corners.1
  8.6 1.9 %collective-permute-start.4 = (f32[8,256]{1,0:T(8,128)S(1)}, f32[8,256]{1,0:T(8,128)S(1)}, u32[]{:S(2)}, u32[]{:S(2)}) collective-permute-start(f32[8,256]{1,0:T(8,128)S(1)} %get-tuple-element.27), channel_id=1, source_target_pairs={{0,16},{1,2},{2,1},{3,4},{4,3},{5,6},{6,5},{7,8},{8,7},{9,10},{10,... | collective-permute-start | bytes 24584 | tf_op jit(solution)/shard_map/ppermute | solution.py:402
  10.5 0.0 collective-permute-start.5
  10.5 0.0 copy-done
  10.6 0.0 copy-done.1
  10.6 3.0 %inner.1 = (f32[2048,128]{1,0:T(8,128)S(1)}, f32[256,128]{1,0:T(8,128)S(1)}, f32[256,128]{1,0:T(8,128)S(1)}, f32[256,128]{1,0:T(8,128)S(1)}, f32[2576,128]{1,0:T...) custom-call(f32[8,128]{1,0:T(8,128)S(1)} %broadcast_in_dim.10.flags,, ...), custom_call_target="tpu_custom_call" | custom-call | flops 20000000 | bytes 12000000 | tf_op jit(solution)/shard_map/inner/pallas_call | solution.py:469
  13.5 0.0 collective-permute-done.y_odd
  13.5 0.0 collective-permute-done.1.y_even
  13.6 0.0 collective-permute-done.4.corner_odd
  13.6 0.6 %collective-permute-done.5.corner_even = f32[8,256]{1,0:T(8,128)S(1)} collective-permute-done((f32[8,256]{1,0:T(8,128)S(1)}, f32[8,256]{1,0:T(8,128)S(1)}, u32[]{:S(2)}, u32[]{:S(2)}) %collective-permute-start.5) | collective-permute-done | bytes 8224 | tf_op jit(solution)/shard_map/ppermute | solution.py:402
  14.2 1.6 %rim.1 = (f32[2048,128]{1,0:T(8,128)S(1)}, f32[17,128]{1,0:T(8,128)S(1)}) custom-call(f32[8,128]{1,0:T(8,128)S(1)} %broadcast_in_dim.10.flags, s32[256]{0:T(256)S(1)} %get-tuple-element.43.cell_vmem, f32[64,256]{1,0:T(8,128)S(1)} %collective-permute-done.y_odd, f32[64,256]{1,0:T(8,128)S(1)} %collective-permute-done.1.y_even, ...), custom_call_target="tpu_custom_call", output_to_operand_aliasing={{0}: (14, {})} | custom-call | tf_op jit(solution)/shard_map/rim/pallas_call | solution.py:480
  15.8 0.1 collective-permute-start.6
  15.9 1.2 %collective-permute-done.6 = f32[17,1,128]{2,0,1:T(8,128)S(1)} collective-permute-done((f32[17,1,128]{2,0,1:T(8,128)S(1)}, f32[17,1,128]{2,0,1:T(8,128)S(1)}, u32[]{:S(2)}, u32[]{:S(2)}) %collective-permute-start.6) | collective-permute-done | bytes 8736 | tf_op jit(solution)/shard_map/ppermute | solution.py:402
  17.0 0.1 broadcast_in_dim.26
  17.1 15.2 %all_to_all.10 = f32[16,17,1,128]{3,2,1,0:T(1,128)S(1)} all-to-all(f32[16,17,1,128]{3,2,1,0:T(1,128)S(1)} %broadcast_in_dim.26), channel_id=1, replica_groups=mesh['gx'=16,'gy'=16] {'gy'}, dimensions={0} | all-to-all | bytes 278528 | tf_op jit(solution)/shard_map/all_to_all | solution.py:496
  32.3 0.1 reduce_sum.9
  32.5 16.7 %all_to_all.11.parts = f32[8,17,1,128]{3,2,1,0:T(1,128)S(1)} all-to-all(f32[8,17,1,128]{3,2,1,0:T(1,128)S(1)} %broadcast_in_dim.27), channel_id=1, replica_groups={{0,32,64,96,128,160,192,224},{16,48,80,112,144,176,208,240},{1,33,65,97..., dimensions={0} | all-to-all | bytes 139264 | tf_op jit(solution)/shard_map/all_to_all | solution.py:501
  49.1 1.8 %solve.1 = (bf16[256,256]{1,0:T(8,128)(2,1)S(1)}, f32[2048,128]{1,0:T(8,128)}) custom-call(f32[8,17,1,128]{3,2,1,0:T(1,128)S(1)} %all_to_all.11.parts, f32[2048,128]{1,0:T(8,128)S(1)} %get-tuple-element.39.tiles), custom_call_target="tpu_custom_call" | custom-call | tf_op jit(solution)/shard_map/solve/pallas_call | solution.py:503
  50.9 1.3 %update.1 = f32[2048,128]{1,0:T(8,128)} custom-call(f32[2048,128]{1,0:T(8,128)S(1)} %bitcast.29, bf16[256,256]{1,0:T(8,128)(2,1)S(1)} %get-tuple-element.40.weights), custom_call_target="tpu_custom_call" | custom-call | tf_op jit(solution)/shard_map/update/pallas_call | solution.py:512
  (5 shorter events, 0.1 us)
Async XLA Ops:
  0.6 9.9 %copy-start = (f32[64,4096]{1,0:T(8,128)S(1)}, f32[64,4096]{1,0:T(8,128)}, u32[]{:S(2)}) copy-start(f32[64,4096]{1,0:T(8,128)} %lat.1) | copy-start | bytes 3145732
  0.6 9.9 %copy-start.2 = (f32[256]{0:T(256)S(1)}, f32[256]{0:T(256)}, u32[]{:S(2)}) copy-start(f32[256]{0:T(256)} %param.8) | copy-start | bytes 3076
  0.7 9.9 %copy-start.1 = (f32[256]{0:T(256)S(1)}, f32[256]{0:T(256)}, u32[]{:S(2)}) copy-start(f32[256]{0:T(256)} %param.9) | copy-start | bytes 3076
  1.7 11.8 %collective-permute-start = (f32[64,256]{1,0:T(8,128)S(1)}, f32[64,256]{1,0:T(8,128)S(1)}, u32[]{:S(2)}, u32[]{:S(2)}) collective-permute-start(f32[64,256]{1,0:T(8,128)S(1)} %get-tuple-element.22), channel_id=1, source_target_pairs={{0,16},{1,2},{2,1},{3,4},{4,3},{5,6},{6,5},{7,8},{8,7},{9,10},{10,... | collective-permute-start | bytes 196616 | tf_op jit(solution)/shard_map/ppermute | solution.py:402
  3.3 10.2 %collective-permute-start.1 = (f32[64,256]{1,0:T(8,128)S(1)}, f32[64,256]{1,0:T(8,128)S(1)}, u32[]{:S(2)}, u32[]{:S(2)}) collective-permute-start(f32[64,256]{1,0:T(8,128)S(1)} %get-tuple-element.23), channel_id=1, source_target_pairs={{0,1},{1,0},{2,3},{3,2},{4,5},{5,4},{6,7},{7,6},{8,9},{9,8},{10,11... | collective-permute-start | bytes 196616 | tf_op jit(solution)/shard_map/ppermute | solution.py:402
  4.2 4.3 %collective-permute-start.2 = (f32[4,4224]{1,0:T(4,128)S(1)}, f32[4,4224]{1,0:T(4,128)S(1)}, u32[]{:S(2)}, u32[]{:S(2)}) collective-permute-start(f32[4,4224]{1,0:T(4,128)S(1)} %get-tuple-element.25), channel_id=1, source_target_pairs={{0,1},{1,0},{2,3},{3,2},{4,5},{5,4},{6,7},{7,6},{8,9},{9,8},{10,11... | collective-permute-start | bytes 202760 | tf_op jit(solution)/shard_map/ppermute | solution.py:402
  5.4 3.1 %collective-permute-start.3 = (f32[4,4224]{1,0:T(4,128)S(1)}, f32[4,4224]{1,0:T(4,128)S(1)}, u32[]{:S(2)}, u32[]{:S(2)}) collective-permute-start(f32[4,4224]{1,0:T(4,128)S(1)} %get-tuple-element.26), channel_id=1, source_target_pairs={{0,16},{1,17},{2,18},{3,19},{4,20},{5,21},{6,22},{7,23},{8,24},{9,... | collective-permute-start | bytes 202760 | tf_op jit(solution)/shard_map/ppermute | solution.py:402
  8.6 4.9 %collective-permute-start.4 = (f32[8,256]{1,0:T(8,128)S(1)}, f32[8,256]{1,0:T(8,128)S(1)}, u32[]{:S(2)}, u32[]{:S(2)}) collective-permute-start(f32[8,256]{1,0:T(8,128)S(1)} %get-tuple-element.27), channel_id=1, source_target_pairs={{0,16},{1,2},{2,1},{3,4},{4,3},{5,6},{6,5},{7,8},{8,7},{9,10},{10,... | collective-permute-start | bytes 24584 | tf_op jit(solution)/shard_map/ppermute | solution.py:402
  10.5 3.7 %collective-permute-start.5 = (f32[8,256]{1,0:T(8,128)S(1)}, f32[8,256]{1,0:T(8,128)S(1)}, u32[]{:S(2)}, u32[]{:S(2)}) collective-permute-start(f32[8,256]{1,0:T(8,128)S(1)} %get-tuple-element.28), channel_id=1, source_target_pairs={{0,1},{1,0},{2,3},{3,2},{4,5},{5,4},{6,7},{7,6},{8,9},{9,8},{10,11... | collective-permute-start | bytes 24584 | tf_op jit(solution)/shard_map/ppermute | solution.py:402
  15.8 1.3 %collective-permute-start.6 = (f32[17,1,128]{2,0,1:T(8,128)S(1)}, f32[17,1,128]{2,0,1:T(8,128)S(1)}, u32[]{:S(2)}, u32[]{:S(2)}) collective-permute-start(f32[17,1,128]{2,0,1:T(8,128)S(1)} %bitcast.30), channel_id=1, source_target_pairs={{0,16},{1,17},{2,18},{3,19},{4,20},{5,21},{6,22},{7,23},{8,24},{9,... | collective-permute-start | bytes 26120 | tf_op jit(solution)/shard_map/ppermute | solution.py:402

commit v11 on v7

--- a/solution.py
+++ b/solution.py
@@ -485,13 +485,13 @@
 
     stat = stat[:, None, :]
     stat = stat + exchange(stat, "gx", 0)
-    width = lax.axis_size("gy")
-    parts = lax.all_to_all(jnp.broadcast_to(stat[None], (width,) + stat.shape), "gy", 0, 0)
-    stat = jnp.sum(parts, axis=0)
     count = lax.axis_size("gx")
     groups = [list(range(i, count, 2)) for i in range(2)]
     parts = jnp.broadcast_to(stat[None], (count // 2,) + stat.shape)
     parts = lax.all_to_all(parts, "gx", 0, 0, axis_index_groups=groups)
+    stat = jnp.sum(parts, axis=0)
+    width = lax.axis_size("gy")
+    parts = lax.all_to_all(jnp.broadcast_to(stat[None], (width,) + stat.shape), "gy", 0, 0)
 
     weights, prior = pl.pallas_call(
         solve_kernel,

time: 50.1 us -> 50.1 us (level)
  no operation moved by 1% of the time
where the time goes in v11:
time: 50.1 us; the launch traced here: 49.9 us
  blocking collectives  31.6 us (63%)
  Pallas kernels  8.72 us (17%)
  starting transfers between devices  4.65 us (9%)
  waiting for transfers between devices  3.11 us (6%)
  other arithmetic  0.76 us (2%)
  between operations  0.73 us (1%)
    all_to_all x1, blocking collectives, per_device(): parts = lax.all_to_all(parts, 'gx', 0, 0, axis_index_groups=groups)  17.3 us
    all_to_all x1, blocking collectives, per_device(): lax.all_to_all(jnp.broadcast_to(stat[None], (width,) + stat.shape), 'gy',...  14.3 us
    ppermute x5, starting transfers between devices, exchange(): return lax.ppermute(block, ('gx', 'gy'), pairs(axis, first))  4.65 us
    ppermute x5, waiting for transfers between devices, exchange(): return lax.ppermute(block, ('gx', 'gy'), pairs(axis, first))  3.11 us
    pallas_call x1, Pallas kernels, per_device(): pl.pallas_call(inner_kernel, out_shape=(arr(CX * BLOCKS, 128),) + (arr(OB...  2.95 us
    pallas_call x1, Pallas kernels, per_device(): pl.pallas_call(solve_kernel, out_shape=(jax.ShapeDtypeStruct((256, 256),...  1.82 us
    pallas_call x1, Pallas kernels, per_device(): pl.pallas_call(rim_kernel, out_shape=(arr(CX * BLOCKS, 128), arr(STAT, 12...  1.58 us
    pallas_call x1, Pallas kernels, per_device(): pl.pallas_call(update_kernel, out_shape=arr(CX * BLOCKS, 128), in_specs=[...  1.28 us
  transfers between devices with their start and end apart: 5, of which 3 were waited for; matrix products, arithmetic and copies ran while one was open for 2% of the time, Pallas kernels for 6%

profile of v11, /device:TPU:2, one launch (start us, length us, event | category | flops | bytes accessed | tf_op | source)
XLA Modules:
  0.0 49.9 jit_solution(14240775839045859837)
XLA Ops:
  0.6 0.0 copy-start
  0.6 1.0 %rows.1 = (f32[4,4224]{1,0:T(4,128)S(1)}, f32[4,4224]{1,0:T(4,128)S(1)}, f32[64,64]{1,0:T(8,128)S(1)}) custom-call(f32[64,4096]{1,0:T(8,128)} %lat.1, f32[64,64]{1,0:T(8,128)} %kap_hbm.1), custom_call_target="tpu_custom_call" | custom-call | tf_op jit(solution)/shard_map/rows/pallas_call | solution.py:435
  1.6 0.0 copy-start.2
  1.7 0.0 copy-start.1
  1.7 2.4 %collective-permute-start = (f32[4,4224]{1,0:T(4,128)S(1)}, f32[4,4224]{1,0:T(4,128)S(1)}, u32[]{:S(2)}, u32[]{:S(2)}) collective-permute-start(f32[4,4224]{1,0:T(4,128)S(1)} %get-tuple-element.21), channel_id=1, source_target_pairs={{0,1},{1,0},{2,3},{3,2},{4,5},{5,4},{6,7},{7,6},{8,9},{9,8},{10,11... | collective-permute-start | bytes 202760 | tf_op jit(solution)/shard_map/ppermute | solution.py:392
  4.0 0.0 collective-permute-start.1
  4.0 0.7 %convert_bitcast_fusion = (f32[2,128]{1,0:T(2,128)S(1)}, s32[256]{0:T(256)S(1)}) fusion(s32[256]{0:T(256)} %param.7), kind=kLoop, calls=%fused_computation.2 | loop fusion | flops 2816 | bytes 3072 | tf_op jit(solution)/shard_map/reshape | solution.py:427
  4.7 0.1 stack.29
  4.8 1.5 %collective-permute-done.x_odd = f32[4,4224]{1,0:T(4,128)S(1)} collective-permute-done((f32[4,4224]{1,0:T(4,128)S(1)}, f32[4,4224]{1,0:T(4,128)S(1)}, u32[]{:S(2)}, u32[]{:S(2)}) %collective-permute-start) | collective-permute-done | bytes 67616 | tf_op jit(solution)/shard_map/ppermute | solution.py:392
  6.3 0.0 collective-permute-done.1.x_even
  6.3 0.1 broadcast_in_dim.10.flags
  6.4 0.0 copy-done
  6.4 0.1 cols.1
  6.5 1.3 %collective-permute-start.2 = (f32[72,256]{1,0:T(8,128)S(1)}, f32[72,256]{1,0:T(8,128)S(1)}, u32[]{:S(2)}, u32[]{:S(2)}) collective-permute-start(f32[72,256]{1,0:T(8,128)S(1)} %get-tuple-element.23), channel_id=1, source_target_pairs={{0,16},{1,2},{2,1},{3,4},{4,3},{5,6},{6,5},{7,8},{8,7},{9,10},{10,... | collective-permute-start | bytes 221192 | tf_op jit(solution)/shard_map/ppermute | solution.py:392
  7.8 0.9 %collective-permute-start.3 = (f32[72,256]{1,0:T(8,128)S(1)}, f32[72,256]{1,0:T(8,128)S(1)}, u32[]{:S(2)}, u32[]{:S(2)}) collective-permute-start(f32[72,256]{1,0:T(8,128)S(1)} %get-tuple-element.24), channel_id=1, source_target_pairs={{0,1},{1,0},{2,3},{3,2},{4,5},{5,4},{6,7},{7,6},{8,9},{9,8},{10,11... | collective-permute-start | bytes 221192 | tf_op jit(solution)/shard_map/ppermute | solution.py:392
  8.7 0.0 copy-done.2
  8.7 0.0 copy-done.1
  8.7 3.0 %inner.1 = (f32[2048,128]{1,0:T(8,128)S(1)}, f32[256,128]{1,0:T(8,128)S(1)}, f32[256,128]{1,0:T(8,128)S(1)}, f32[256,128]{1,0:T(8,128)S(1)}, f32[2576,128]{1,0:T...) custom-call(f32[8,128]{1,0:T(8,128)S(1)} %broadcast_in_dim.10.flags,, ...), custom_call_target="tpu_custom_call" | custom-call | flops 20000000 | bytes 12000000 | tf_op jit(solution)/shard_map/inner/pallas_call | solution.py:462
  11.6 0.0 collective-permute-done.2.y_odd
  11.6 0.5 collective-permute-done.3.y_even
  12.1 1.6 %rim.1 = (f32[2048,128]{1,0:T(8,128)S(1)}, f32[17,128]{1,0:T(8,128)S(1)}) custom-call(f32[8,128]{1,0:T(8,128)S(1)} %broadcast_in_dim.10.flags, s32[256]{0:T(256)S(1)} %get-tuple-element.39.cell_vmem, f32[72,256]{1,0:T(8,128)S(1)} %collective-permute-done.2.y_odd, f32[72,256]{1,0:T(8,128)S(1)} %collective-permute-done.3.y_even, ...), custom_call_target="tpu_custom_call", output_to_operand_aliasing={{0}: (12, {})} | custom-call | tf_op jit(solution)/shard_map/rim/pallas_call | solution.py:473
  13.7 0.1 collective-permute-start.4
  13.8 1.2 %collective-permute-done.4 = f32[17,1,128]{2,0,1:T(8,128)S(1)} collective-permute-done((f32[17,1,128]{2,0,1:T(8,128)S(1)}, f32[17,1,128]{2,0,1:T(8,128)S(1)}, u32[]{:S(2)}, u32[]{:S(2)}) %collective-permute-start.4) | collective-permute-done | bytes 8736 | tf_op jit(solution)/shard_map/ppermute | solution.py:392
  15.0 17.3 %all_to_all.10 = f32[8,17,1,128]{3,2,1,0:T(1,128)S(1)} all-to-all(f32[8,17,1,128]{3,2,1,0:T(1,128)S(1)} %broadcast_in_dim.26), channel_id=1, replica_groups={{0,32,64,96,128,160,192,224},{16,48,80,112,144,176,208,240},{1,33,65,97..., dimensions={0} | all-to-all | bytes 139264 | tf_op jit(solution)/shard_map/all_to_all | solution.py:491
  32.3 0.1 reduce_sum.9
  32.4 0.1 broadcast_in_dim.27
  32.5 14.3 %all_to_all.11.parts = f32[16,17,1,128]{3,2,1,0:T(1,128)S(1)} all-to-all(f32[16,17,1,128]{3,2,1,0:T(1,128)S(1)} %broadcast_in_dim.27), channel_id=1, replica_groups=mesh['gx'=16,'gy'=16] {'gy'}, dimensions={0} | all-to-all | bytes 278528 | tf_op jit(solution)/shard_map/all_to_all | solution.py:494
  46.8 1.8 %solve.1 = (bf16[256,256]{1,0:T(8,128)(2,1)S(1)}, f32[2048,128]{1,0:T(8,128)}) custom-call(f32[16,17,1,128]{3,2,1,0:T(1,128)S(1)} %all_to_all.11.parts, f32[2048,128]{1,0:T(8,128)S(1)} %get-tuple-element.35.tiles), custom_call_target="tpu_custom_call" | custom-call | tf_op jit(solution)/shard_map/solve/pallas_call | solution.py:496
  48.6 1.3 %update.1 = f32[2048,128]{1,0:T(8,128)} custom-call(f32[2048,128]{1,0:T(8,128)S(1)} %bitcast.29, bf16[256,256]{1,0:T(8,128)(2,1)S(1)} %get-tuple-element.36.weights), custom_call_target="tpu_custom_call" | custom-call | tf_op jit(solution)/shard_map/update/pallas_call | solution.py:505
  (4 shorter events, 0.1 us)
Async XLA Ops:
  0.6 5.7 %copy-start = (f32[64,4096]{1,0:T(8,128)S(1)}, f32[64,4096]{1,0:T(8,128)}, u32[]{:S(2)}) copy-start(f32[64,4096]{1,0:T(8,128)} %lat.1) | copy-start | bytes 3145732
  1.6 7.0 %copy-start.2 = (f32[256]{0:T(256)S(1)}, f32[256]{0:T(256)}, u32[]{:S(2)}) copy-start(f32[256]{0:T(256)} %param.8) | copy-start | bytes 3076
  1.7 7.0 %copy-start.1 = (f32[256]{0:T(256)S(1)}, f32[256]{0:T(256)}, u32[]{:S(2)}) copy-start(f32[256]{0:T(256)} %param.9) | copy-start | bytes 3076
  1.7 4.6 %collective-permute-start = (f32[4,4224]{1,0:T(4,128)S(1)}, f32[4,4224]{1,0:T(4,128)S(1)}, u32[]{:S(2)}, u32[]{:S(2)}) collective-permute-start(f32[4,4224]{1,0:T(4,128)S(1)} %get-tuple-element.21), channel_id=1, source_target_pairs={{0,1},{1,0},{2,3},{3,2},{4,5},{5,4},{6,7},{7,6},{8,9},{9,8},{10,11... | collective-permute-start | bytes 202760 | tf_op jit(solution)/shard_map/ppermute | solution.py:392
  4.0 2.3 %collective-permute-start.1 = (f32[4,4224]{1,0:T(4,128)S(1)}, f32[4,4224]{1,0:T(4,128)S(1)}, u32[]{:S(2)}, u32[]{:S(2)}) collective-permute-start(f32[4,4224]{1,0:T(4,128)S(1)} %get-tuple-element.22), channel_id=1, source_target_pairs={{0,16},{1,17},{2,18},{3,19},{4,20},{5,21},{6,22},{7,23},{8,24},{9,... | collective-permute-start | bytes 202760 | tf_op jit(solution)/shard_map/ppermute | solution.py:392
  6.5 5.2 %collective-permute-start.2 = (f32[72,256]{1,0:T(8,128)S(1)}, f32[72,256]{1,0:T(8,128)S(1)}, u32[]{:S(2)}, u32[]{:S(2)}) collective-permute-start(f32[72,256]{1,0:T(8,128)S(1)} %get-tuple-element.23), channel_id=1, source_target_pairs={{0,16},{1,2},{2,1},{3,4},{4,3},{5,6},{6,5},{7,8},{8,7},{9,10},{10,... | collective-permute-start | bytes 221192 | tf_op jit(solution)/shard_map/ppermute | solution.py:392
  7.8 4.4 %collective-permute-start.3 = (f32[72,256]{1,0:T(8,128)S(1)}, f32[72,256]{1,0:T(8,128)S(1)}, u32[]{:S(2)}, u32[]{:S(2)}) collective-permute-start(f32[72,256]{1,0:T(8,128)S(1)} %get-tuple-element.24), channel_id=1, source_target_pairs={{0,1},{1,0},{2,3},{3,2},{4,5},{5,4},{6,7},{7,6},{8,9},{9,8},{10,11... | collective-permute-start | bytes 221192 | tf_op jit(solution)/shard_map/ppermute | solution.py:392
  13.7 1.3 %collective-permute-start.4 = (f32[17,1,128]{2,0,1:T(8,128)S(1)}, f32[17,1,128]{2,0,1:T(8,128)S(1)}, u32[]{:S(2)}, u32[]{:S(2)}) collective-permute-start(f32[17,1,128]{2,0,1:T(8,128)S(1)} %bitcast.30), channel_id=1, source_target_pairs={{0,16},{1,17},{2,18},{3,19},{4,20},{5,21},{6,22},{7,23},{8,24},{9,... | collective-permute-start | bytes 26120 | tf_op jit(solution)/shard_map/ppermute | solution.py:392

commit v12 on v11

--- a/solution.py
+++ b/solution.py
@@ -211,20 +211,23 @@
     kext[...] = jnp.zeros((128, 128), F32)
     is_odd = jnp.broadcast_to(flags[4:5, :], (CX + 8, 128)) > 0.5
     is_odd = jnp.concatenate([is_odd, is_odd], axis=1)
-    for side in range(2):
-        lower, upper = (y_even, y_odd) if side == 0 else (y_odd, y_even)
+    sides = ((y_even, y_odd), (y_odd, y_even))
+    for side, (lower, upper) in enumerate(sides):
+        for i in range(HALO):
+            r = CX if i < 2 else CX + 7
+            at = slice(r, r + 1), lanes(i % 2)
+            row = side * HALO + i
+            kext[row : row + 1, :] = jnp.where(is_odd[0:1, 0:128], lower[at], upper[at])
+    shifted = jnp.transpose(kext[...])[0:TALL, :] - CENTRE
+    for side, (lower, upper) in enumerate(sides):
         msg = jnp.where(is_odd, lower[...], upper[...])
         flag = flags[2 + side : 3 + side, :]
-        for i in range(HALO):
-            r = CX if i < 2 else CX + 7
-            kext[i : i + 1, :] = msg[r : r + 1, lanes(i % 2)]
-        shifted = jnp.transpose(kext[...])[0:TALL, :] - CENTRE
-        upper = (lax.broadcasted_iota(jnp.int32, (TALL, 128), 1) >= MEMBERS).astype(jnp.int32)
+        half = (lax.broadcasted_iota(jnp.int32, (TALL, 128), 1) >= MEMBERS).astype(jnp.int32)
         for p in (-2, -1):
             i = p + 2 if side == 0 else -1 - p
             halo = msg[CX : CX + 4, lanes(i)], msg[CX + 4 : CX + 8, lanes(i)]
             fill(ext_out, p + 2, msg[0:CX, lanes(i)] * flag, *halo, low * flag, high * flag)
-            alpha_out[rows_of(p + 2), :] = jnp.take_along_axis(shifted, upper + 2 * i, axis=1)
+            alpha_out[rows_of(p + 2), :] = jnp.take_along_axis(shifted, half + (side * HALO + 2 * i), axis=1)
 
         def local(p):
             return p if side == 0 else BLOCKS - 1 - p

time: 50.1 us -> 50.1 us (level)
  no operation moved by 1% of the time
where the time goes in v12:
time: 50.1 us; the launch traced here: 49.9 us
  blocking collectives  31.6 us (63%)
  Pallas kernels  8.68 us (17%)
  starting transfers between devices  4.65 us (9%)
  waiting for transfers between devices  3.11 us (6%)
  other arithmetic  0.76 us (2%)
  between operations  0.73 us (1%)
    all_to_all x1, blocking collectives, per_device(): parts = lax.all_to_all(parts, 'gx', 0, 0, axis_index_groups=groups)  17.3 us
    all_to_all x1, blocking collectives, per_device(): lax.all_to_all(jnp.broadcast_to(stat[None], (width,) + stat.shape), 'gy',...  14.3 us
    ppermute x5, starting transfers between devices, exchange(): return lax.ppermute(block, ('gx', 'gy'), pairs(axis, first))  4.65 us
    ppermute x5, waiting for transfers between devices, exchange(): return lax.ppermute(block, ('gx', 'gy'), pairs(axis, first))  3.11 us
    pallas_call x1, Pallas kernels, per_device(): pl.pallas_call(inner_kernel, out_shape=(arr(CX * BLOCKS, 128),) + (arr(OB...  2.95 us
    pallas_call x1, Pallas kernels, per_device(): pl.pallas_call(solve_kernel, out_shape=(jax.ShapeDtypeStruct((256, 256),...  1.82 us
    pallas_call x1, Pallas kernels, per_device(): pl.pallas_call(rim_kernel, out_shape=(arr(CX * BLOCKS, 128), arr(STAT, 12...  1.55 us
    pallas_call x1, Pallas kernels, per_device(): pl.pallas_call(update_kernel, out_shape=arr(CX * BLOCKS, 128), in_specs=[...  1.28 us
  transfers between devices with their start and end apart: 5, of which 3 were waited for; matrix products, arithmetic and copies ran while one was open for 2% of the time, Pallas kernels for 6%

profile of v12, /device:TPU:2, one launch (start us, length us, event | category | flops | bytes accessed | tf_op | source)
XLA Modules:
  0.0 49.9 jit_solution(16457514101720990078)
XLA Ops:
  0.6 0.0 copy-start
  0.6 1.0 %rows.1 = (f32[4,4224]{1,0:T(4,128)S(1)}, f32[4,4224]{1,0:T(4,128)S(1)}, f32[64,64]{1,0:T(8,128)S(1)}) custom-call(f32[64,4096]{1,0:T(8,128)} %lat.1, f32[64,64]{1,0:T(8,128)} %kap_hbm.1), custom_call_target="tpu_custom_call" | custom-call | tf_op jit(solution)/shard_map/rows/pallas_call | solution.py:438
  1.6 0.0 copy-start.2
  1.7 0.0 copy-start.1
  1.7 2.4 %collective-permute-start = (f32[4,4224]{1,0:T(4,128)S(1)}, f32[4,4224]{1,0:T(4,128)S(1)}, u32[]{:S(2)}, u32[]{:S(2)}) collective-permute-start(f32[4,4224]{1,0:T(4,128)S(1)} %get-tuple-element.21), channel_id=1, source_target_pairs={{0,1},{1,0},{2,3},{3,2},{4,5},{5,4},{6,7},{7,6},{8,9},{9,8},{10,11... | collective-permute-start | bytes 202760 | tf_op jit(solution)/shard_map/ppermute | solution.py:395
  4.0 0.0 collective-permute-start.1
  4.0 0.7 %convert_bitcast_fusion = (f32[2,128]{1,0:T(2,128)S(1)}, s32[256]{0:T(256)S(1)}) fusion(s32[256]{0:T(256)} %param.7), kind=kLoop, calls=%fused_computation.2 | loop fusion | flops 2816 | bytes 3072 | tf_op jit(solution)/shard_map/reshape | solution.py:430
  4.7 0.1 stack.29
  4.8 1.5 %collective-permute-done.x_odd = f32[4,4224]{1,0:T(4,128)S(1)} collective-permute-done((f32[4,4224]{1,0:T(4,128)S(1)}, f32[4,4224]{1,0:T(4,128)S(1)}, u32[]{:S(2)}, u32[]{:S(2)}) %collective-permute-start) | collective-permute-done | bytes 67616 | tf_op jit(solution)/shard_map/ppermute | solution.py:395
  6.3 0.0 collective-permute-done.1.x_even
  6.3 0.1 broadcast_in_dim.10.flags
  6.4 0.0 copy-done
  6.4 0.1 cols.1
  6.5 1.3 %collective-permute-start.2 = (f32[72,256]{1,0:T(8,128)S(1)}, f32[72,256]{1,0:T(8,128)S(1)}, u32[]{:S(2)}, u32[]{:S(2)}) collective-permute-start(f32[72,256]{1,0:T(8,128)S(1)} %get-tuple-element.23), channel_id=1, source_target_pairs={{0,16},{1,2},{2,1},{3,4},{4,3},{5,6},{6,5},{7,8},{8,7},{9,10},{10,... | collective-permute-start | bytes 221192 | tf_op jit(solution)/shard_map/ppermute | solution.py:395
  7.8 0.9 %collective-permute-start.3 = (f32[72,256]{1,0:T(8,128)S(1)}, f32[72,256]{1,0:T(8,128)S(1)}, u32[]{:S(2)}, u32[]{:S(2)}) collective-permute-start(f32[72,256]{1,0:T(8,128)S(1)} %get-tuple-element.24), channel_id=1, source_target_pairs={{0,1},{1,0},{2,3},{3,2},{4,5},{5,4},{6,7},{7,6},{8,9},{9,8},{10,11... | collective-permute-start | bytes 221192 | tf_op jit(solution)/shard_map/ppermute | solution.py:395
  8.7 0.0 copy-done.2
  8.7 0.0 copy-done.1
  8.7 3.0 %inner.1 = (f32[2048,128]{1,0:T(8,128)S(1)}, f32[256,128]{1,0:T(8,128)S(1)}, f32[256,128]{1,0:T(8,128)S(1)}, f32[256,128]{1,0:T(8,128)S(1)}, f32[2576,128]{1,0:T...) custom-call(f32[8,128]{1,0:T(8,128)S(1)} %broadcast_in_dim.10.flags,, ...), custom_call_target="tpu_custom_call" | custom-call | flops 20000000 | bytes 12000000 | tf_op jit(solution)/shard_map/inner/pallas_call | solution.py:465
  11.6 0.0 collective-permute-done.2.y_odd
  11.6 0.5 collective-permute-done.3.y_even
  12.1 1.6 %rim.1 = (f32[2048,128]{1,0:T(8,128)S(1)}, f32[17,128]{1,0:T(8,128)S(1)}) custom-call(f32[8,128]{1,0:T(8,128)S(1)} %broadcast_in_dim.10.flags, s32[256]{0:T(256)S(1)} %get-tuple-element.39.cell_vmem, f32[72,256]{1,0:T(8,128)S(1)} %collective-permute-done.2.y_odd, f32[72,256]{1,0:T(8,128)S(1)} %collective-permute-done.3.y_even, ...), custom_call_target="tpu_custom_call", output_to_operand_aliasing={{0}: (12, {})} | custom-call | tf_op jit(solution)/shard_map/rim/pallas_call | solution.py:476
  13.7 0.1 collective-permute-start.4
  13.8 1.2 %collective-permute-done.4 = f32[17,1,128]{2,0,1:T(8,128)S(1)} collective-permute-done((f32[17,1,128]{2,0,1:T(8,128)S(1)}, f32[17,1,128]{2,0,1:T(8,128)S(1)}, u32[]{:S(2)}, u32[]{:S(2)}) %collective-permute-start.4) | collective-permute-done | bytes 8736 | tf_op jit(solution)/shard_map/ppermute | solution.py:395
  15.0 17.3 %all_to_all.10 = f32[8,17,1,128]{3,2,1,0:T(1,128)S(1)} all-to-all(f32[8,17,1,128]{3,2,1,0:T(1,128)S(1)} %broadcast_in_dim.26), channel_id=1, replica_groups={{0,32,64,96,128,160,192,224},{16,48,80,112,144,176,208,240},{1,33,65,97..., dimensions={0} | all-to-all | bytes 139264 | tf_op jit(solution)/shard_map/all_to_all | solution.py:494
  32.3 0.1 reduce_sum.9
  32.4 0.1 broadcast_in_dim.27
  32.5 14.3 %all_to_all.11.parts = f32[16,17,1,128]{3,2,1,0:T(1,128)S(1)} all-to-all(f32[16,17,1,128]{3,2,1,0:T(1,128)S(1)} %broadcast_in_dim.27), channel_id=1, replica_groups=mesh['gx'=16,'gy'=16] {'gy'}, dimensions={0} | all-to-all | bytes 278528 | tf_op jit(solution)/shard_map/all_to_all | solution.py:497
  46.8 1.8 %solve.1 = (bf16[256,256]{1,0:T(8,128)(2,1)S(1)}, f32[2048,128]{1,0:T(8,128)}) custom-call(f32[16,17,1,128]{3,2,1,0:T(1,128)S(1)} %all_to_all.11.parts, f32[2048,128]{1,0:T(8,128)S(1)} %get-tuple-element.35.tiles), custom_call_target="tpu_custom_call" | custom-call | tf_op jit(solution)/shard_map/solve/pallas_call | solution.py:499
  48.6 1.3 %update.1 = f32[2048,128]{1,0:T(8,128)} custom-call(f32[2048,128]{1,0:T(8,128)S(1)} %bitcast.29, bf16[256,256]{1,0:T(8,128)(2,1)S(1)} %get-tuple-element.36.weights), custom_call_target="tpu_custom_call" | custom-call | tf_op jit(solution)/shard_map/update/pallas_call | solution.py:508
  (4 shorter events, 0.1 us)
Async XLA Ops:
  0.6 5.7 %copy-start = (f32[64,4096]{1,0:T(8,128)S(1)}, f32[64,4096]{1,0:T(8,128)}, u32[]{:S(2)}) copy-start(f32[64,4096]{1,0:T(8,128)} %lat.1) | copy-start | bytes 3145732
  1.6 7.0 %copy-start.2 = (f32[256]{0:T(256)S(1)}, f32[256]{0:T(256)}, u32[]{:S(2)}) copy-start(f32[256]{0:T(256)} %param.8) | copy-start | bytes 3076
  1.7 7.0 %copy-start.1 = (f32[256]{0:T(256)S(1)}, f32[256]{0:T(256)}, u32[]{:S(2)}) copy-start(f32[256]{0:T(256)} %param.9) | copy-start | bytes 3076
  1.7 4.6 %collective-permute-start = (f32[4,4224]{1,0:T(4,128)S(1)}, f32[4,4224]{1,0:T(4,128)S(1)}, u32[]{:S(2)}, u32[]{:S(2)}) collective-permute-start(f32[4,4224]{1,0:T(4,128)S(1)} %get-tuple-element.21), channel_id=1, source_target_pairs={{0,1},{1,0},{2,3},{3,2},{4,5},{5,4},{6,7},{7,6},{8,9},{9,8},{10,11... | collective-permute-start | bytes 202760 | tf_op jit(solution)/shard_map/ppermute | solution.py:395
  4.0 2.3 %collective-permute-start.1 = (f32[4,4224]{1,0:T(4,128)S(1)}, f32[4,4224]{1,0:T(4,128)S(1)}, u32[]{:S(2)}, u32[]{:S(2)}) collective-permute-start(f32[4,4224]{1,0:T(4,128)S(1)} %get-tuple-element.22), channel_id=1, source_target_pairs={{0,16},{1,17},{2,18},{3,19},{4,20},{5,21},{6,22},{7,23},{8,24},{9,... | collective-permute-start | bytes 202760 | tf_op jit(solution)/shard_map/ppermute | solution.py:395
  6.5 5.2 %collective-permute-start.2 = (f32[72,256]{1,0:T(8,128)S(1)}, f32[72,256]{1,0:T(8,128)S(1)}, u32[]{:S(2)}, u32[]{:S(2)}) collective-permute-start(f32[72,256]{1,0:T(8,128)S(1)} %get-tuple-element.23), channel_id=1, source_target_pairs={{0,16},{1,2},{2,1},{3,4},{4,3},{5,6},{6,5},{7,8},{8,7},{9,10},{10,... | collective-permute-start | bytes 221192 | tf_op jit(solution)/shard_map/ppermute | solution.py:395
  7.8 4.4 %collective-permute-start.3 = (f32[72,256]{1,0:T(8,128)S(1)}, f32[72,256]{1,0:T(8,128)S(1)}, u32[]{:S(2)}, u32[]{:S(2)}) collective-permute-start(f32[72,256]{1,0:T(8,128)S(1)} %get-tuple-element.24), channel_id=1, source_target_pairs={{0,1},{1,0},{2,3},{3,2},{4,5},{5,4},{6,7},{7,6},{8,9},{9,8},{10,11... | collective-permute-start | bytes 221192 | tf_op jit(solution)/shard_map/ppermute | solution.py:395
  13.7 1.3 %collective-permute-start.4 = (f32[17,1,128]{2,0,1:T(8,128)S(1)}, f32[17,1,128]{2,0,1:T(8,128)S(1)}, u32[]{:S(2)}, u32[]{:S(2)}) collective-permute-start(f32[17,1,128]{2,0,1:T(8,128)S(1)} %bitcast.30), channel_id=1, source_target_pairs={{0,16},{1,17},{2,18},{3,19},{4,20},{5,21},{6,22},{7,23},{8,24},{9,... | collective-permute-start | bytes 26120 | tf_op jit(solution)/shard_map/ppermute | solution.py:395

commit v13 on v11

--- a/solution.py
+++ b/solution.py
@@ -285,15 +285,18 @@
         columns = [jnp.broadcast_to(aug[:, k : k + 1], (MEMBERS, 128)) for k in range(start, start + size)]
         block = [column[start : start + size] for column in columns]
         pivot_rows = aug[start : start + size]
-        for i in range(size):
-            here = row == i
-            inverse = 1.0 / block[i][i : i + 1]
-
-            def clear(a):
-                scaled = a[i : i + 1] * inverse
-                return jnp.where(here, scaled, a - block[i] * scaled)
-
-            block = block[: i + 1] + [clear(a) for a in block[i + 1 :]]
+        for i in range(0, size, 2):
+            c0, c1 = block[i], block[i + 1]
+            a, b, c, d = c0[i : i + 1], c1[i : i + 1], c0[i + 1 : i + 2], c1[i + 1 : i + 2]
+            inverse = 1.0 / (a * d - b * c)
+
+            def clear(m):
+                m0, m1 = m[i : i + 1], m[i + 1 : i + 2]
+                n0, n1 = (d * m0 - b * m1) * inverse, (a * m1 - c * m0) * inverse
+                rest = m - (c0 * n0 + c1 * n1)
+                return jnp.where(row == i, n0, jnp.where(row == i + 1, n1, rest))
+
+            block = block[: i + 2] + [clear(m) for m in block[i + 2 :]]
             pivot_rows = clear(pivot_rows)
         pieces = []
         for at in range(0, MEMBERS, size):

time: 50.1 us -> 50 us (level)
  no operation moved by 1% of the time
where the time goes in v13:
time: 50 us; the launch traced here: 49.8 us
  blocking collectives  31.6 us (63%)
  Pallas kernels  8.59 us (17%)
  starting transfers between devices  4.65 us (9%)
  waiting for transfers between devices  3.11 us (6%)
  other arithmetic  0.76 us (2%)
  between operations  0.73 us (1%)
    all_to_all x1, blocking collectives, per_device(): parts = lax.all_to_all(parts, 'gx', 0, 0, axis_index_groups=groups)  17.3 us
    all_to_all x1, blocking collectives, per_device(): lax.all_to_all(jnp.broadcast_to(stat[None], (width,) + stat.shape), 'gy',...  14.3 us
    ppermute x5, starting transfers between devices, exchange(): return lax.ppermute(block, ('gx', 'gy'), pairs(axis, first))  4.65 us
    ppermute x5, waiting for transfers between devices, exchange(): return lax.ppermute(block, ('gx', 'gy'), pairs(axis, first))  3.11 us
    pallas_call x1, Pallas kernels, per_device(): pl.pallas_call(inner_kernel, out_shape=(arr(CX * BLOCKS, 128),) + (arr(OB...  2.95 us
    pallas_call x1, Pallas kernels, per_device(): pl.pallas_call(solve_kernel, out_shape=(jax.ShapeDtypeStruct((256, 256),...  1.7 us
    pallas_call x1, Pallas kernels, per_device(): pl.pallas_call(rim_kernel, out_shape=(arr(CX * BLOCKS, 128), arr(STAT, 12...  1.58 us
    pallas_call x1, Pallas kernels, per_device(): pl.pallas_call(update_kernel, out_shape=arr(CX * BLOCKS, 128), in_specs=[...  1.28 us
  transfers between devices with their start and end apart: 5, of which 3 were waited for; matrix products, arithmetic and copies ran while one was open for 2% of the time, Pallas kernels for 6%

profile of v13, /device:TPU:2, one launch (start us, length us, event | category | flops | bytes accessed | tf_op | source)
XLA Modules:
  0.0 49.8 jit_solution(11965700007179012497)
XLA Ops:
  0.6 0.0 copy-start
  0.6 1.0 %rows.1 = (f32[4,4224]{1,0:T(4,128)S(1)}, f32[4,4224]{1,0:T(4,128)S(1)}, f32[64,64]{1,0:T(8,128)S(1)}) custom-call(f32[64,4096]{1,0:T(8,128)} %lat.1, f32[64,64]{1,0:T(8,128)} %kap_hbm.1), custom_call_target="tpu_custom_call" | custom-call | tf_op jit(solution)/shard_map/rows/pallas_call | solution.py:438
  1.6 0.0 copy-start.2
  1.7 0.0 copy-start.1
  1.7 2.4 %collective-permute-start = (f32[4,4224]{1,0:T(4,128)S(1)}, f32[4,4224]{1,0:T(4,128)S(1)}, u32[]{:S(2)}, u32[]{:S(2)}) collective-permute-start(f32[4,4224]{1,0:T(4,128)S(1)} %get-tuple-element.21), channel_id=1, source_target_pairs={{0,1},{1,0},{2,3},{3,2},{4,5},{5,4},{6,7},{7,6},{8,9},{9,8},{10,11... | collective-permute-start | bytes 202760 | tf_op jit(solution)/shard_map/ppermute | solution.py:395
  4.0 0.0 collective-permute-start.1
  4.0 0.7 %convert_bitcast_fusion = (f32[2,128]{1,0:T(2,128)S(1)}, s32[256]{0:T(256)S(1)}) fusion(s32[256]{0:T(256)} %param.7), kind=kLoop, calls=%fused_computation.2 | loop fusion | flops 2816 | bytes 3072 | tf_op jit(solution)/shard_map/reshape | solution.py:430
  4.7 0.1 stack.29
  4.8 1.5 %collective-permute-done.x_odd = f32[4,4224]{1,0:T(4,128)S(1)} collective-permute-done((f32[4,4224]{1,0:T(4,128)S(1)}, f32[4,4224]{1,0:T(4,128)S(1)}, u32[]{:S(2)}, u32[]{:S(2)}) %collective-permute-start) | collective-permute-done | bytes 67616 | tf_op jit(solution)/shard_map/ppermute | solution.py:395
  6.3 0.0 collective-permute-done.1.x_even
  6.3 0.1 broadcast_in_dim.10.flags
  6.4 0.0 copy-done
  6.4 0.1 cols.1
  6.5 1.3 %collective-permute-start.2 = (f32[72,256]{1,0:T(8,128)S(1)}, f32[72,256]{1,0:T(8,128)S(1)}, u32[]{:S(2)}, u32[]{:S(2)}) collective-permute-start(f32[72,256]{1,0:T(8,128)S(1)} %get-tuple-element.23), channel_id=1, source_target_pairs={{0,16},{1,2},{2,1},{3,4},{4,3},{5,6},{6,5},{7,8},{8,7},{9,10},{10,... | collective-permute-start | bytes 221192 | tf_op jit(solution)/shard_map/ppermute | solution.py:395
  7.8 0.9 %collective-permute-start.3 = (f32[72,256]{1,0:T(8,128)S(1)}, f32[72,256]{1,0:T(8,128)S(1)}, u32[]{:S(2)}, u32[]{:S(2)}) collective-permute-start(f32[72,256]{1,0:T(8,128)S(1)} %get-tuple-element.24), channel_id=1, source_target_pairs={{0,1},{1,0},{2,3},{3,2},{4,5},{5,4},{6,7},{7,6},{8,9},{9,8},{10,11... | collective-permute-start | bytes 221192 | tf_op jit(solution)/shard_map/ppermute | solution.py:395
  8.7 0.0 copy-done.2
  8.7 0.0 copy-done.1
  8.7 3.0 %inner.1 = (f32[2048,128]{1,0:T(8,128)S(1)}, f32[256,128]{1,0:T(8,128)S(1)}, f32[256,128]{1,0:T(8,128)S(1)}, f32[256,128]{1,0:T(8,128)S(1)}, f32[2576,128]{1,0:T...) custom-call(f32[8,128]{1,0:T(8,128)S(1)} %broadcast_in_dim.10.flags,, ...), custom_call_target="tpu_custom_call" | custom-call | flops 20000000 | bytes 12000000 | tf_op jit(solution)/shard_map/inner/pallas_call | solution.py:465
  11.6 0.0 collective-permute-done.2.y_odd
  11.6 0.5 collective-permute-done.3.y_even
  12.1 1.6 %rim.1 = (f32[2048,128]{1,0:T(8,128)S(1)}, f32[17,128]{1,0:T(8,128)S(1)}) custom-call(f32[8,128]{1,0:T(8,128)S(1)} %broadcast_in_dim.10.flags, s32[256]{0:T(256)S(1)} %get-tuple-element.39.cell_vmem, f32[72,256]{1,0:T(8,128)S(1)} %collective-permute-done.2.y_odd, f32[72,256]{1,0:T(8,128)S(1)} %collective-permute-done.3.y_even, ...), custom_call_target="tpu_custom_call", output_to_operand_aliasing={{0}: (12, {})} | custom-call | tf_op jit(solution)/shard_map/rim/pallas_call | solution.py:476
  13.7 0.1 collective-permute-start.4
  13.8 1.2 %collective-permute-done.4 = f32[17,1,128]{2,0,1:T(8,128)S(1)} collective-permute-done((f32[17,1,128]{2,0,1:T(8,128)S(1)}, f32[17,1,128]{2,0,1:T(8,128)S(1)}, u32[]{:S(2)}, u32[]{:S(2)}) %collective-permute-start.4) | collective-permute-done | bytes 8736 | tf_op jit(solution)/shard_map/ppermute | solution.py:395
  15.0 17.3 %all_to_all.10 = f32[8,17,1,128]{3,2,1,0:T(1,128)S(1)} all-to-all(f32[8,17,1,128]{3,2,1,0:T(1,128)S(1)} %broadcast_in_dim.26), channel_id=1, replica_groups={{0,32,64,96,128,160,192,224},{16,48,80,112,144,176,208,240},{1,33,65,97..., dimensions={0} | all-to-all | bytes 139264 | tf_op jit(solution)/shard_map/all_to_all | solution.py:494
  32.3 0.1 reduce_sum.9
  32.4 0.1 broadcast_in_dim.27
  32.5 14.3 %all_to_all.11.parts = f32[16,17,1,128]{3,2,1,0:T(1,128)S(1)} all-to-all(f32[16,17,1,128]{3,2,1,0:T(1,128)S(1)} %broadcast_in_dim.27), channel_id=1, replica_groups=mesh['gx'=16,'gy'=16] {'gy'}, dimensions={0} | all-to-all | bytes 278528 | tf_op jit(solution)/shard_map/all_to_all | solution.py:497
  46.8 1.7 %solve.1 = (bf16[256,256]{1,0:T(8,128)(2,1)S(1)}, f32[2048,128]{1,0:T(8,128)}) custom-call(f32[16,17,1,128]{3,2,1,0:T(1,128)S(1)} %all_to_all.11.parts, f32[2048,128]{1,0:T(8,128)S(1)} %get-tuple-element.35.tiles), custom_call_target="tpu_custom_call" | custom-call | tf_op jit(solution)/shard_map/solve/pallas_call | solution.py:499
  48.5 1.3 %update.1 = f32[2048,128]{1,0:T(8,128)} custom-call(f32[2048,128]{1,0:T(8,128)S(1)} %bitcast.29, bf16[256,256]{1,0:T(8,128)(2,1)S(1)} %get-tuple-element.36.weights), custom_call_target="tpu_custom_call" | custom-call | tf_op jit(solution)/shard_map/update/pallas_call | solution.py:508
  (4 shorter events, 0.1 us)
Async XLA Ops:
  0.6 5.7 %copy-start = (f32[64,4096]{1,0:T(8,128)S(1)}, f32[64,4096]{1,0:T(8,128)}, u32[]{:S(2)}) copy-start(f32[64,4096]{1,0:T(8,128)} %lat.1) | copy-start | bytes 3145732
  1.6 7.0 %copy-start.2 = (f32[256]{0:T(256)S(1)}, f32[256]{0:T(256)}, u32[]{:S(2)}) copy-start(f32[256]{0:T(256)} %param.8) | copy-start | bytes 3076
  1.7 7.0 %copy-start.1 = (f32[256]{0:T(256)S(1)}, f32[256]{0:T(256)}, u32[]{:S(2)}) copy-start(f32[256]{0:T(256)} %param.9) | copy-start | bytes 3076
  1.7 4.6 %collective-permute-start = (f32[4,4224]{1,0:T(4,128)S(1)}, f32[4,4224]{1,0:T(4,128)S(1)}, u32[]{:S(2)}, u32[]{:S(2)}) collective-permute-start(f32[4,4224]{1,0:T(4,128)S(1)} %get-tuple-element.21), channel_id=1, source_target_pairs={{0,1},{1,0},{2,3},{3,2},{4,5},{5,4},{6,7},{7,6},{8,9},{9,8},{10,11... | collective-permute-start | bytes 202760 | tf_op jit(solution)/shard_map/ppermute | solution.py:395
  4.0 2.3 %collective-permute-start.1 = (f32[4,4224]{1,0:T(4,128)S(1)}, f32[4,4224]{1,0:T(4,128)S(1)}, u32[]{:S(2)}, u32[]{:S(2)}) collective-permute-start(f32[4,4224]{1,0:T(4,128)S(1)} %get-tuple-element.22), channel_id=1, source_target_pairs={{0,16},{1,17},{2,18},{3,19},{4,20},{5,21},{6,22},{7,23},{8,24},{9,... | collective-permute-start | bytes 202760 | tf_op jit(solution)/shard_map/ppermute | solution.py:395
  6.5 5.2 %collective-permute-start.2 = (f32[72,256]{1,0:T(8,128)S(1)}, f32[72,256]{1,0:T(8,128)S(1)}, u32[]{:S(2)}, u32[]{:S(2)}) collective-permute-start(f32[72,256]{1,0:T(8,128)S(1)} %get-tuple-element.23), channel_id=1, source_target_pairs={{0,16},{1,2},{2,1},{3,4},{4,3},{5,6},{6,5},{7,8},{8,7},{9,10},{10,... | collective-permute-start | bytes 221192 | tf_op jit(solution)/shard_map/ppermute | solution.py:395
  7.8 4.4 %collective-permute-start.3 = (f32[72,256]{1,0:T(8,128)S(1)}, f32[72,256]{1,0:T(8,128)S(1)}, u32[]{:S(2)}, u32[]{:S(2)}) collective-permute-start(f32[72,256]{1,0:T(8,128)S(1)} %get-tuple-element.24), channel_id=1, source_target_pairs={{0,1},{1,0},{2,3},{3,2},{4,5},{5,4},{6,7},{7,6},{8,9},{9,8},{10,11... | collective-permute-start | bytes 221192 | tf_op jit(solution)/shard_map/ppermute | solution.py:395
  13.7 1.3 %collective-permute-start.4 = (f32[17,1,128]{2,0,1:T(8,128)S(1)}, f32[17,1,128]{2,0,1:T(8,128)S(1)}, u32[]{:S(2)}, u32[]{:S(2)}) collective-permute-start(f32[17,1,128]{2,0,1:T(8,128)S(1)} %bitcast.30), channel_id=1, source_target_pairs={{0,16},{1,17},{2,18},{3,19},{4,20},{5,21},{6,22},{7,23},{8,24},{9,... | collective-permute-start | bytes 26120 | tf_op jit(solution)/shard_map/ppermute | solution.py:395

commit v14 on v12

--- a/solution.py
+++ b/solution.py
@@ -288,15 +288,18 @@
         columns = [jnp.broadcast_to(aug[:, k : k + 1], (MEMBERS, 128)) for k in range(start, start + size)]
         block = [column[start : start + size] for column in columns]
         pivot_rows = aug[start : start + size]
-        for i in range(size):
-            here = row == i
-            inverse = 1.0 / block[i][i : i + 1]
-
-            def clear(a):
-                scaled = a[i : i + 1] * inverse
-                return jnp.where(here, scaled, a - block[i] * scaled)
-
-            block = block[: i + 1] + [clear(a) for a in block[i + 1 :]]
+        for i in range(0, size, 2):
+            c0, c1 = block[i], block[i + 1]
+            a, b, c, d = c0[i : i + 1], c1[i : i + 1], c0[i + 1 : i + 2], c1[i + 1 : i + 2]
+            inverse = 1.0 / (a * d - b * c)
+
+            def clear(m):
+                m0, m1 = m[i : i + 1], m[i + 1 : i + 2]
+                n0, n1 = (d * m0 - b * m1) * inverse, (a * m1 - c * m0) * inverse
+                rest = m - (c0 * n0 + c1 * n1)
+                return jnp.where(row == i, n0, jnp.where(row == i + 1, n1, rest))
+
+            block = block[: i + 2] + [clear(m) for m in block[i + 2 :]]
             pivot_rows = clear(pivot_rows)
         pieces = []
         for at in range(0, MEMBERS, size):

time: 50.1 us -> 49.9 us (level)
  no operation moved by 1% of the time
where the time goes in v14:
time: 49.9 us; the launch traced here: 49.8 us
  blocking collectives  31.6 us (63%)
  Pallas kernels  8.57 us (17%)
  starting transfers between devices  4.65 us (9%)
  waiting for transfers between devices  3.11 us (6%)
  other arithmetic  0.76 us (2%)
  between operations  0.73 us (1%)
    all_to_all x1, blocking collectives, per_device(): parts = lax.all_to_all(parts, 'gx', 0, 0, axis_index_groups=groups)  17.3 us
    all_to_all x1, blocking collectives, per_device(): lax.all_to_all(jnp.broadcast_to(stat[None], (width,) + stat.shape), 'gy',...  14.3 us
    ppermute x5, starting transfers between devices, exchange(): return lax.ppermute(block, ('gx', 'gy'), pairs(axis, first))  4.65 us
    ppermute x5, waiting for transfers between devices, exchange(): return lax.ppermute(block, ('gx', 'gy'), pairs(axis, first))  3.11 us
    pallas_call x1, Pallas kernels, per_device(): pl.pallas_call(inner_kernel, out_shape=(arr(CX * BLOCKS, 128),) + (arr(OB...  2.95 us
    pallas_call x1, Pallas kernels, per_device(): pl.pallas_call(solve_kernel, out_shape=(jax.ShapeDtypeStruct((256, 256),...  1.7 us
    pallas_call x1, Pallas kernels, per_device(): pl.pallas_call(rim_kernel, out_shape=(arr(CX * BLOCKS, 128), arr(STAT, 12...  1.55 us
    pallas_call x1, Pallas kernels, per_device(): pl.pallas_call(update_kernel, out_shape=arr(CX * BLOCKS, 128), in_specs=[...  1.28 us
  transfers between devices with their start and end apart: 5, of which 3 were waited for; matrix products, arithmetic and copies ran while one was open for 2% of the time, Pallas kernels for 6%

profile of v14, /device:TPU:2, one launch (start us, length us, event | category | flops | bytes accessed | tf_op | source)
XLA Modules:
  0.0 49.8 jit_solution(420208264934124278)
XLA Ops:
  0.6 0.0 copy-start
  0.6 1.0 %rows.1 = (f32[4,4224]{1,0:T(4,128)S(1)}, f32[4,4224]{1,0:T(4,128)S(1)}, f32[64,64]{1,0:T(8,128)S(1)}) custom-call(f32[64,4096]{1,0:T(8,128)} %lat.1, f32[64,64]{1,0:T(8,128)} %kap_hbm.1), custom_call_target="tpu_custom_call" | custom-call | tf_op jit(solution)/shard_map/rows/pallas_call | solution.py:441
  1.6 0.0 copy-start.2
  1.7 0.0 copy-start.1
  1.7 2.4 %collective-permute-start = (f32[4,4224]{1,0:T(4,128)S(1)}, f32[4,4224]{1,0:T(4,128)S(1)}, u32[]{:S(2)}, u32[]{:S(2)}) collective-permute-start(f32[4,4224]{1,0:T(4,128)S(1)} %get-tuple-element.21), channel_id=1, source_target_pairs={{0,1},{1,0},{2,3},{3,2},{4,5},{5,4},{6,7},{7,6},{8,9},{9,8},{10,11... | collective-permute-start | bytes 202760 | tf_op jit(solution)/shard_map/ppermute | solution.py:398
  4.0 0.0 collective-permute-start.1
  4.0 0.7 %convert_bitcast_fusion = (f32[2,128]{1,0:T(2,128)S(1)}, s32[256]{0:T(256)S(1)}) fusion(s32[256]{0:T(256)} %param.7), kind=kLoop, calls=%fused_computation.2 | loop fusion | flops 2816 | bytes 3072 | tf_op jit(solution)/shard_map/reshape | solution.py:433
  4.7 0.1 stack.29
  4.8 1.5 %collective-permute-done.x_odd = f32[4,4224]{1,0:T(4,128)S(1)} collective-permute-done((f32[4,4224]{1,0:T(4,128)S(1)}, f32[4,4224]{1,0:T(4,128)S(1)}, u32[]{:S(2)}, u32[]{:S(2)}) %collective-permute-start) | collective-permute-done | bytes 67616 | tf_op jit(solution)/shard_map/ppermute | solution.py:398
  6.3 0.0 collective-permute-done.1.x_even
  6.3 0.1 broadcast_in_dim.10.flags
  6.4 0.0 copy-done
  6.4 0.1 cols.1
  6.5 1.3 %collective-permute-start.2 = (f32[72,256]{1,0:T(8,128)S(1)}, f32[72,256]{1,0:T(8,128)S(1)}, u32[]{:S(2)}, u32[]{:S(2)}) collective-permute-start(f32[72,256]{1,0:T(8,128)S(1)} %get-tuple-element.23), channel_id=1, source_target_pairs={{0,16},{1,2},{2,1},{3,4},{4,3},{5,6},{6,5},{7,8},{8,7},{9,10},{10,... | collective-permute-start | bytes 221192 | tf_op jit(solution)/shard_map/ppermute | solution.py:398
  7.8 0.9 %collective-permute-start.3 = (f32[72,256]{1,0:T(8,128)S(1)}, f32[72,256]{1,0:T(8,128)S(1)}, u32[]{:S(2)}, u32[]{:S(2)}) collective-permute-start(f32[72,256]{1,0:T(8,128)S(1)} %get-tuple-element.24), channel_id=1, source_target_pairs={{0,1},{1,0},{2,3},{3,2},{4,5},{5,4},{6,7},{7,6},{8,9},{9,8},{10,11... | collective-permute-start | bytes 221192 | tf_op jit(solution)/shard_map/ppermute | solution.py:398
  8.7 0.0 copy-done.2
  8.7 0.0 copy-done.1
  8.7 3.0 %inner.1 = (f32[2048,128]{1,0:T(8,128)S(1)}, f32[256,128]{1,0:T(8,128)S(1)}, f32[256,128]{1,0:T(8,128)S(1)}, f32[256,128]{1,0:T(8,128)S(1)}, f32[2576,128]{1,0:T...) custom-call(f32[8,128]{1,0:T(8,128)S(1)} %broadcast_in_dim.10.flags,, ...), custom_call_target="tpu_custom_call" | custom-call | flops 20000000 | bytes 12000000 | tf_op jit(solution)/shard_map/inner/pallas_call | solution.py:468
  11.6 0.0 collective-permute-done.2.y_odd
  11.6 0.5 collective-permute-done.3.y_even
  12.1 1.6 %rim.1 = (f32[2048,128]{1,0:T(8,128)S(1)}, f32[17,128]{1,0:T(8,128)S(1)}) custom-call(f32[8,128]{1,0:T(8,128)S(1)} %broadcast_in_dim.10.flags, s32[256]{0:T(256)S(1)} %get-tuple-element.39.cell_vmem, f32[72,256]{1,0:T(8,128)S(1)} %collective-permute-done.2.y_odd, f32[72,256]{1,0:T(8,128)S(1)} %collective-permute-done.3.y_even, ...), custom_call_target="tpu_custom_call", output_to_operand_aliasing={{0}: (12, {})} | custom-call | tf_op jit(solution)/shard_map/rim/pallas_call | solution.py:479
  13.7 0.1 collective-permute-start.4
  13.8 1.2 %collective-permute-done.4 = f32[17,1,128]{2,0,1:T(8,128)S(1)} collective-permute-done((f32[17,1,128]{2,0,1:T(8,128)S(1)}, f32[17,1,128]{2,0,1:T(8,128)S(1)}, u32[]{:S(2)}, u32[]{:S(2)}) %collective-permute-start.4) | collective-permute-done | bytes 8736 | tf_op jit(solution)/shard_map/ppermute | solution.py:398
  15.0 17.3 %all_to_all.10 = f32[8,17,1,128]{3,2,1,0:T(1,128)S(1)} all-to-all(f32[8,17,1,128]{3,2,1,0:T(1,128)S(1)} %broadcast_in_dim.26), channel_id=1, replica_groups={{0,32,64,96,128,160,192,224},{16,48,80,112,144,176,208,240},{1,33,65,97..., dimensions={0} | all-to-all | bytes 139264 | tf_op jit(solution)/shard_map/all_to_all | solution.py:497
  32.3 0.1 reduce_sum.9
  32.4 0.1 broadcast_in_dim.27
  32.5 14.3 %all_to_all.11.parts = f32[16,17,1,128]{3,2,1,0:T(1,128)S(1)} all-to-all(f32[16,17,1,128]{3,2,1,0:T(1,128)S(1)} %broadcast_in_dim.27), channel_id=1, replica_groups=mesh['gx'=16,'gy'=16] {'gy'}, dimensions={0} | all-to-all | bytes 278528 | tf_op jit(solution)/shard_map/all_to_all | solution.py:500
  46.8 1.7 %solve.1 = (bf16[256,256]{1,0:T(8,128)(2,1)S(1)}, f32[2048,128]{1,0:T(8,128)}) custom-call(f32[16,17,1,128]{3,2,1,0:T(1,128)S(1)} %all_to_all.11.parts, f32[2048,128]{1,0:T(8,128)S(1)} %get-tuple-element.35.tiles), custom_call_target="tpu_custom_call" | custom-call | tf_op jit(solution)/shard_map/solve/pallas_call | solution.py:502
  48.5 1.3 %update.1 = f32[2048,128]{1,0:T(8,128)} custom-call(f32[2048,128]{1,0:T(8,128)S(1)} %bitcast.29, bf16[256,256]{1,0:T(8,128)(2,1)S(1)} %get-tuple-element.36.weights), custom_call_target="tpu_custom_call" | custom-call | tf_op jit(solution)/shard_map/update/pallas_call | solution.py:511
  (4 shorter events, 0.1 us)
Async XLA Ops:
  0.6 5.7 %copy-start = (f32[64,4096]{1,0:T(8,128)S(1)}, f32[64,4096]{1,0:T(8,128)}, u32[]{:S(2)}) copy-start(f32[64,4096]{1,0:T(8,128)} %lat.1) | copy-start | bytes 3145732
  1.6 7.0 %copy-start.2 = (f32[256]{0:T(256)S(1)}, f32[256]{0:T(256)}, u32[]{:S(2)}) copy-start(f32[256]{0:T(256)} %param.8) | copy-start | bytes 3076
  1.7 7.0 %copy-start.1 = (f32[256]{0:T(256)S(1)}, f32[256]{0:T(256)}, u32[]{:S(2)}) copy-start(f32[256]{0:T(256)} %param.9) | copy-start | bytes 3076
  1.7 4.6 %collective-permute-start = (f32[4,4224]{1,0:T(4,128)S(1)}, f32[4,4224]{1,0:T(4,128)S(1)}, u32[]{:S(2)}, u32[]{:S(2)}) collective-permute-start(f32[4,4224]{1,0:T(4,128)S(1)} %get-tuple-element.21), channel_id=1, source_target_pairs={{0,1},{1,0},{2,3},{3,2},{4,5},{5,4},{6,7},{7,6},{8,9},{9,8},{10,11... | collective-permute-start | bytes 202760 | tf_op jit(solution)/shard_map/ppermute | solution.py:398
  4.0 2.3 %collective-permute-start.1 = (f32[4,4224]{1,0:T(4,128)S(1)}, f32[4,4224]{1,0:T(4,128)S(1)}, u32[]{:S(2)}, u32[]{:S(2)}) collective-permute-start(f32[4,4224]{1,0:T(4,128)S(1)} %get-tuple-element.22), channel_id=1, source_target_pairs={{0,16},{1,17},{2,18},{3,19},{4,20},{5,21},{6,22},{7,23},{8,24},{9,... | collective-permute-start | bytes 202760 | tf_op jit(solution)/shard_map/ppermute | solution.py:398
  6.5 5.2 %collective-permute-start.2 = (f32[72,256]{1,0:T(8,128)S(1)}, f32[72,256]{1,0:T(8,128)S(1)}, u32[]{:S(2)}, u32[]{:S(2)}) collective-permute-start(f32[72,256]{1,0:T(8,128)S(1)} %get-tuple-element.23), channel_id=1, source_target_pairs={{0,16},{1,2},{2,1},{3,4},{4,3},{5,6},{6,5},{7,8},{8,7},{9,10},{10,... | collective-permute-start | bytes 221192 | tf_op jit(solution)/shard_map/ppermute | solution.py:398
  7.8 4.4 %collective-permute-start.3 = (f32[72,256]{1,0:T(8,128)S(1)}, f32[72,256]{1,0:T(8,128)S(1)}, u32[]{:S(2)}, u32[]{:S(2)}) collective-permute-start(f32[72,256]{1,0:T(8,128)S(1)} %get-tuple-element.24), channel_id=1, source_target_pairs={{0,1},{1,0},{2,3},{3,2},{4,5},{5,4},{6,7},{7,6},{8,9},{9,8},{10,11... | collective-permute-start | bytes 221192 | tf_op jit(solution)/shard_map/ppermute | solution.py:398
  13.7 1.3 %collective-permute-start.4 = (f32[17,1,128]{2,0,1:T(8,128)S(1)}, f32[17,1,128]{2,0,1:T(8,128)S(1)}, u32[]{:S(2)}, u32[]{:S(2)}) collective-permute-start(f32[17,1,128]{2,0,1:T(8,128)S(1)} %bitcast.30), channel_id=1, source_target_pairs={{0,16},{1,17},{2,18},{3,19},{4,20},{5,21},{6,22},{7,23},{8,24},{9,... | collective-permute-start | bytes 26120 | tf_op jit(solution)/shard_map/ppermute | solution.py:398
